TPU v7x, 32 devices: a whole 2x2x4 slice. The times are simulated.
32 devices in a mesh: group: 2 (over y), ctx: 4 (over z), head: 2 (over x), sub: 2 (over core).
Axes of the slice: x: 2, y: 2, z: 4, core: 2. Of those that a mesh axis runs over, the one named last changes fastest.
Arguments:
- q_lin: bfloat16 [2048, 32, 128], P(('group', 'ctx'), ('head', 'sub')), parts along dimension 0, may hold values from -1.796875 to 1.796875
- k_lin: bfloat16 [2048, 32, 128], P(('group', 'ctx'), ('head', 'sub')), parts along dimension 0, may hold values from -1.796875 to 1.796875
- v_lin: bfloat16 [2048, 32, 128], P(('group', 'ctx'), ('head', 'sub')), parts along dimension 0, may hold values from -6 to 6
- decay_log: float32 [2048, 32], P(('group', 'ctx'), ('head', 'sub')), parts along dimension 0, may hold values from -0.7 to 0, as said below
- q_soft: bfloat16 [2048, 32, 128], P(('group', 'ctx'), ('head', 'sub')), parts along dimension 0, may hold values from -8 to 8, as said below
- k_soft: bfloat16 [2048, 8, 128], P(('group', 'ctx'), ('head', 'sub')), parts along dimension 0, may hold values from -8 to 8, as said below
- v_soft: bfloat16 [2048, 8, 128], P(('group', 'ctx'), ('head', 'sub')), parts along dimension 0, may hold values from -6 to 6
- doc_starts: int32 [12], P('group'), parts along dimension 0, may hold values from 0 to 768, as said below
Outputs:
- lin_out: bfloat16 [2048, 32, 128], P(('group', 'ctx'), ('head', 'sub')), parts along dimension 0
- soft_out: bfloat16 [2048, 32, 128], P(('group', 'ctx'), ('head', 'sub')), parts along dimension 0
There are 2 independent parts, one for each index of `group`. A program takes and returns all parts, laid end to end along the dimension named above; each array names one. Nothing has to cross between parts.
Inputs may be any that keep to these rules, and one draw needn't show every extreme that they name: `decay_log`: entries are negative. `q_soft`: entries are at most 8 in magnitude. `k_soft`: entries are at most 8 in magnitude. `doc_starts`: starts never fall and are multiples of 256; equal starts (empty documents) may occur. The first is 0, the last is 768, and all others lie at or after position (3) * 256.
All inputs are finite; a program needn't handle non-finite values.
Results may differ from a plain program's by a relative error of at most 0.0075.
Values may be sent and summed in bfloat16 or wider, within the bound.
No kernel may reach another device: no remote copies, remote signals or barrier semaphores. Data moves between devices by JAX's collectives and lax.ppermute only.
A program may use at most 64 MiB of HBM per device.

v0:
```python
import math

import jax
import jax.numpy as jnp
from jax import lax
from jax.sharding import PartitionSpec as P


def carried_in(shard, axis, combine, identity):
    size, index = (lax.axis_size(axis), lax.axis_index(axis))
    everything = jax.tree.map(
        lambda part, kind: lax.all_gather(part.astype(kind), axis),
        shard,
        (jnp.bfloat16, jnp.bfloat16),
    )
    start = jax.tree.map(
        lambda part, zero: jnp.broadcast_to(jnp.asarray(zero, part.dtype), part.shape),
        shard,
        identity,
    )

    def step(k, before):
        reached = k < index
        new = combine(
            before, jax.tree.map(lambda part, own: part[k].astype(own.dtype), everything, shard)
        )
        return jax.tree.map(lambda a, b: jnp.where(reached, a, b), new, before)

    return lax.fori_loop(0, size, step, start)


def from_behind(value, axis, steps):
    count = lax.axis_size(axis)
    leading, last = (max(0, -steps), min(count, count - steps))
    return lax.ppermute(value, axis, [(source, source + steps) for source in range(leading, last)])


def doc_index(slice_locations, doc_starts):
    return jnp.sum((doc_starts[None, :] <= slice_locations[:, None]).astype(jnp.int32), axis=1) - 1


def chain_join(earlier, later):
    return (earlier[0] * later[0], earlier[1] * later[0][..., None, None] + later[1])


def lightning_part(q_lin, k_lin, v_lin, decay_log):
    rise = jnp.cumsum(decay_log, axis=0)
    scores = jnp.einsum("ihd,jhd->hij", q_lin, k_lin, preferred_element_type=jnp.float32)
    rows = jnp.arange(q_lin.shape[0])
    lower = (rows[:, None] >= rows[None, :])[None]
    gap = rise.T[:, :, None] - rise.T[:, None, :]
    fade = jnp.where(lower, jnp.exp(jnp.where(lower, gap, 0.0)), 0.0)
    inner = (scores * fade).astype(jnp.bfloat16)
    intra = jnp.einsum("hij,jhd->ihd", inner, v_lin, preferred_element_type=jnp.float32)
    block_decay = rise[-1]
    tail = (k_lin.astype(jnp.float32) * jnp.exp(block_decay[None, :] - rise)[:, :, None]).astype(
        jnp.bfloat16
    )
    local_state = jnp.einsum("jhd,jhe->hde", tail, v_lin, preferred_element_type=jnp.float32)
    return (rise, intra, block_decay, local_state)


def on_device(q_lin, k_lin, v_lin, decay_log, q_soft, k_soft, v_soft, doc_starts):
    rise, intra, block_decay, local_state = lightning_part(q_lin, k_lin, v_lin, decay_log)
    me = lax.axis_index("ctx")
    tok = q_soft.shape[0]
    ranks = lax.axis_size("ctx")
    bounds = doc_index(jnp.stack([me * tok, (me + 1) * tok]), doc_starts)
    keep_next = bounds[0] == bounds[1]
    factor = jnp.where(keep_next, jnp.exp(block_decay), jnp.zeros_like(block_decay))
    addend = jnp.where(keep_next, local_state, jnp.zeros_like(local_state))
    empty = (jnp.ones_like(block_decay), jnp.zeros_like(local_state))
    carried = carried_in((factor, addend), "ctx", chain_join, empty)
    state_in = carried[1]
    lead = q_lin.astype(jnp.float32) * jnp.exp(rise)[:, :, None]
    inter = jnp.einsum("ihd,hde->ihe", lead, state_in, precision=lax.Precision.HIGHEST)
    total = intra + inter
    lin_out = (total * lax.rsqrt(jnp.mean(total * total, axis=-1, keepdims=True) + 1e-06)).astype(
        jnp.bfloat16
    )
    kv_heads = k_soft.shape[1]
    group = q_soft.shape[1] // kv_heads
    head_dim = q_soft.shape[2]
    scale = 1.0 / math.sqrt(head_dim)
    q_pos = me * tok + jnp.arange(tok, dtype=jnp.int32)
    q_doc = doc_index(q_pos, doc_starts)
    q_four = q_soft.reshape(tok, kv_heads, group, head_dim)

    def tile(carry, k_tile, v_tile, k_start):
        k_pos = k_start + jnp.arange(k_tile.shape[0], dtype=jnp.int32)
        k_doc = doc_index(k_pos, doc_starts)
        allowed = (k_pos[None, :] <= q_pos[:, None]) & (k_doc[None, :] == q_doc[:, None])
        top, summed, acc = carry
        scores = (
            jnp.einsum("tkgd,skd->tkgs", q_four, k_tile, preferred_element_type=jnp.float32) * scale
        )
        scores = jnp.where(allowed[:, None, None, :], scores, -jnp.inf)
        new_top = jnp.maximum(top, jnp.max(scores, axis=-1))
        shrink = jnp.exp(top - new_top)
        weights = jnp.exp(scores - new_top[..., None])
        summed = summed * shrink + jnp.sum(weights, axis=-1)
        acc = acc * shrink[..., None] + jnp.einsum(
            "tkgs,skd->tkgd",
            weights.astype(jnp.bfloat16),
            v_tile,
            preferred_element_type=jnp.float32,
        )
        return (new_top, summed, acc)

    initial = (
        jnp.full((tok, kv_heads, group), -1e30, jnp.float32),
        jnp.zeros((tok, kv_heads, group), jnp.float32),
        jnp.zeros((tok, kv_heads, group, head_dim), jnp.float32),
    )
    first = tile(initial, k_soft, v_soft, me * tok)

    def passing(step, state):
        carry, k_held, v_held = state
        k_held, v_held = from_behind((k_held, v_held), "ctx", 1)
        carry = tile(carry, k_held, v_held, (me - step) * tok)
        return (carry, k_held, v_held)

    final = lax.fori_loop(1, ranks, passing, (first, k_soft, v_soft))
    top, summed, acc = final[0]
    soft_out = (
        (acc / summed[..., None]).reshape(tok, kv_heads * group, head_dim).astype(jnp.bfloat16)
    )
    return (lin_out, soft_out)


def solution(mesh):
    return jax.shard_map(
        on_device,
        mesh=mesh,
        in_specs=(
            P(("group", "ctx"), ("head", "sub"), None),
            P(("group", "ctx"), ("head", "sub"), None),
            P(("group", "ctx"), ("head", "sub"), None),
            P(("group", "ctx"), ("head", "sub")),
            P(("group", "ctx"), ("head", "sub"), None),
            P(("group", "ctx"), ("head", "sub"), None),
            P(("group", "ctx"), ("head", "sub"), None),
            P("group"),
        ),
        out_specs=(
            P(("group", "ctx"), ("head", "sub"), None),
            P(("group", "ctx"), ("head", "sub"), None),
        ),
        check_vma=False,
    )
```

profile of v0, /device:TPU:0, one launch (start us, length us, event | category | flops | bytes accessed | tf_op | source)
XLA Modules:
  0.0 88.6 jit_solution(816197125442971011)
XLA Ops:
  7.3 0.9 %fusion.34 = s32[2]{0:T(128)S(1)} fusion(s32[6]{0:T(128)} %param.19, s32[2]{0:T(128)S(1)} %pad_add_fusion), kind=kLoop, calls=%fused_computation.65 | loop fusion | flops 34 | bytes 40 | tf_op jit(solution)/shard_map/reduce_sum | solution.py:39
  8.3 0.6 fusion.39
  8.9 1.2 %reduce-window.6 = f32[8,2,128]{2,0,1:T(8,128)S(1)} reduce-window(f32[8,2,128]{2,0,1:T(8,128)} %bitcast.102, f32[]{:T(128)} %constant.111.clone.1), window={size=1x1x128 pad=0_0x0_0x127_0}, to_apply=%region_0.0 | reduce-window | flops 260096 | bytes 16388 | tf_op jit(solution)/shard_map/reduce-window
  10.1 0.2 slice_reduce_fusion
  10.4 0.2 slice_reduce_fusion.1
  10.6 0.1 copy.82
  12.1 1.4 %multiply_convert_fusion.2 = bf16[256,8,128]{2,1,0:T(8,128)(2,1)S(1)} fusion(bf16[256,8,128]{2,1,0:T(8,128)(2,1)} %param.13, f32[256,8]{1,0:T(8,128)S(1)} %copy.82), kind=kLoop, calls=%fused_computation.39 | loop fusion | flops 786432 | bytes 1056768 | tf_op jit(solution)/shard_map/convert_element_type | solution.py:56
  13.5 1.1 %fusion.16 = bf16[8,128,128]{2,1,0:T(8,128)(2,1)} fusion(bf16[256,8,128]{2,1,0:T(8,128)(2,1)S(1)} %multiply_convert_fusion.2, bf16[256,8,128]{2,1,0:T(8,128)(2,1)S(1)} %copy-done, pred[]{:T(512)} %bitcast.6), kind=kOutput, calls=%fused_computation.32 | convolution fusion | flops 67371008 | bytes 1310721 | tf_op jit(solution)/shard_map/jhd,jhe->hde/dot_general | solution.py:59
  14.6 0.2 fusion.33
  14.9 0.1 compare_and_fusion.1
  15.2 0.5 fusion.40
  15.7 0.3 fusion.11
  16.1 12.7 %all-gather.1 = bf16[4,1,8]{2,1,0:T(2,128)(2,1)S(1)} all-gather(bf16[1,1,8]{2,1,0:T(2,128)(2,1)S(1)} %bitcast.103), channel_id=1, replica_groups=mesh['group'=2,'ctx'=4,'head'=2,'sub'=2] {'ctx'}, dimensions={0}, use_global_device_ids=true | all-gather | bytes 80 | tf_op jit(solution)/shard_map/all_gather | solution.py:12
  28.9 0.9 fusion.14
  29.8 40.7 %while.38 = (s32[]{:T(128)}, f32[256,2,4]{0,2,1:T(4,128)S(1)}, f32[256,2,4]{0,2,1:T(4,128)S(1)}, f32[256,2,4,128]{3,0,2,1:T(8,128)S(1)}, bf16[256,2,128]{2,0,1:T...) while((s32[]{:T(128)}, f32[256,2,4]{0,2,1:T(4,128)S(1)}, ...), condition=%wide.region_13.14_spmd.clone, body=%wide.region_9.13_spmd.clone.sunk | while | flops 272835584 | bytes 11020549 | solution.py:123
  29.8 1.3 %collective-permute-start = (bf16[256,2,128]{2,0,1:T(8,128)(2,1)S(1)}, bf16[256,2,128]{2,0,1:T(8,128)(2,1)S(1)}, u32[]{:S(2)}, u32[]{:S(2)}) collective-permute-start(bf16[256,2,128]{2,0,1:T(8,128)(2,1)S(1)} %get-tuple-element.666), channel_id=1, source_target_pairs={{0,4},{4,8},{8,12},{1,5},{5,9},{9,13},{2,6},{6,10},{10,14},{3,7},{... | collective-permute-start | bytes 393224 | tf_op jit(solution)/shard_map/while/body/eval_jaxpr/ppermute | solution.py:35
  31.1 2.6 %collective-permute-start.1 = (bf16[256,2,128]{2,0,1:T(8,128)(2,1)S(1)}, bf16[256,2,128]{2,0,1:T(8,128)(2,1)S(1)}, u32[]{:S(2)}, u32[]{:S(2)}) collective-permute-start(bf16[256,2,128]{2,0,1:T(8,128)(2,1)S(1)} %get-tuple-element.667), channel_id=1, source_target_pairs={{0,4},{4,8},{8,12},{1,5},{5,9},{9,13},{2,6},{6,10},{10,14},{3,7},{... | collective-permute-start | bytes 393224 | tf_op jit(solution)/shard_map/while/body/eval_jaxpr/ppermute | solution.py:35
  33.8 0.1 compare_and_fusion.3
  34.0 3.8 %collective-permute-done = bf16[256,2,128]{2,0,1:T(8,128)(2,1)S(1)} collective-permute-done((bf16[256,2,128]{2,0,1:T(8,128)(2,1)S(1)}, bf16[256,2,128]{2,0,1:T(8,128)(2,1)S(1)}, u32[]{:S(2)}, u32[]{:S(2)}) %collective-permute-start) | collective-permute-done | bytes 131104 | tf_op jit(solution)/shard_map/while/body/eval_jaxpr/ppermute | solution.py:35
  37.7 0.5 fusion.54
  38.2 0.3 fusion.55
  38.6 3.8 %collective-permute-done.1 = bf16[256,2,128]{2,0,1:T(8,128)(2,1)S(1)} collective-permute-done((bf16[256,2,128]{2,0,1:T(8,128)(2,1)S(1)}, bf16[256,2,128]{2,0,1:T(8,128)(2,1)S(1)}, u32[]{:S(2)}, u32[]{:S(2)}) %collective-permute-start.1) | collective-permute-done | bytes 131104 | tf_op jit(solution)/shard_map/while/body/eval_jaxpr/ppermute | solution.py:35
  42.4 0.9 %fusion.56 = f32[256,2,4,128]{3,0,2,1:T(8,128)S(1)} fusion(f32[256,2,4,256]{0,3,2,1:T(8,128)S(1)} %get-tuple-element.620, f32[256,2,4,128]{3,0,2,1:T(8,128)S(1)} %get-tuple-element.665, f32[256,2,4]{0,2,1:T(4,128)S(1)} %max.12, f32[256,2,4]{0,2,1:T(4,128)S(1)} %bitcast.95, bf16[256,2,128]{2,0,1:T(8,128)(2,1)S(1)} %collective-permute-done.1), kind=kOutput, calls=%fused_computation.6.clone.1 | convolution fusion | flops 135790592 | bytes 4341760 | tf_op jit(solution)/shard_map/while/body/eval_jaxpr/tkgs,skd->tkgd/dot_general | solution.py:102
  43.4 7.7 %collective-permute-start = (bf16[256,2,128]{2,0,1:T(8,128)(2,1)S(1)}, bf16[256,2,128]{2,0,1:T(8,128)(2,1)S(1)}, u32[]{:S(2)}, u32[]{:S(2)}) collective-permute-start(bf16[256,2,128]{2,0,1:T(8,128)(2,1)S(1)} %get-tuple-element.666), channel_id=1, source_target_pairs={{0,4},{4,8},{8,12},{1,5},{5,9},{9,13},{2,6},{6,10},{10,14},{3,7},{... | collective-permute-start | bytes 393224 | tf_op jit(solution)/shard_map/while/body/eval_jaxpr/ppermute | solution.py:35
  51.1 5.4 %collective-permute-start.1 = (bf16[256,2,128]{2,0,1:T(8,128)(2,1)S(1)}, bf16[256,2,128]{2,0,1:T(8,128)(2,1)S(1)}, u32[]{:S(2)}, u32[]{:S(2)}) collective-permute-start(bf16[256,2,128]{2,0,1:T(8,128)(2,1)S(1)} %get-tuple-element.667), channel_id=1, source_target_pairs={{0,4},{4,8},{8,12},{1,5},{5,9},{9,13},{2,6},{6,10},{10,14},{3,7},{... | collective-permute-start | bytes 393224 | tf_op jit(solution)/shard_map/while/body/eval_jaxpr/ppermute | solution.py:35
  56.6 0.1 compare_and_fusion.3
  56.7 0.5 fusion.54
  57.2 0.3 fusion.55
  57.5 1.4 %collective-permute-done.1 = bf16[256,2,128]{2,0,1:T(8,128)(2,1)S(1)} collective-permute-done((bf16[256,2,128]{2,0,1:T(8,128)(2,1)S(1)}, bf16[256,2,128]{2,0,1:T(8,128)(2,1)S(1)}, u32[]{:S(2)}, u32[]{:S(2)}) %collective-permute-start.1) | collective-permute-done | bytes 131104 | tf_op jit(solution)/shard_map/while/body/eval_jaxpr/ppermute | solution.py:35
  59.0 0.9 %fusion.56 = f32[256,2,4,128]{3,0,2,1:T(8,128)S(1)} fusion(f32[256,2,4,256]{0,3,2,1:T(8,128)S(1)} %get-tuple-element.620, f32[256,2,4,128]{3,0,2,1:T(8,128)S(1)} %get-tuple-element.665, f32[256,2,4]{0,2,1:T(4,128)S(1)} %max.12, f32[256,2,4]{0,2,1:T(4,128)S(1)} %bitcast.95, bf16[256,2,128]{2,0,1:T(8,128)(2,1)S(1)} %collective-permute-done.1), kind=kOutput, calls=%fused_computation.6.clone.1 | convolution fusion | flops 135790592 | bytes 4341760 | tf_op jit(solution)/shard_map/while/body/eval_jaxpr/tkgs,skd->tkgd/dot_general | solution.py:102
  59.9 4.3 %collective-permute-start = (bf16[256,2,128]{2,0,1:T(8,128)(2,1)S(1)}, bf16[256,2,128]{2,0,1:T(8,128)(2,1)S(1)}, u32[]{:S(2)}, u32[]{:S(2)}) collective-permute-start(bf16[256,2,128]{2,0,1:T(8,128)(2,1)S(1)} %get-tuple-element.666), channel_id=1, source_target_pairs={{0,4},{4,8},{8,12},{1,5},{5,9},{9,13},{2,6},{6,10},{10,14},{3,7},{... | collective-permute-start | bytes 393224 | tf_op jit(solution)/shard_map/while/body/eval_jaxpr/ppermute | solution.py:35
  64.3 2.7 %collective-permute-start.1 = (bf16[256,2,128]{2,0,1:T(8,128)(2,1)S(1)}, bf16[256,2,128]{2,0,1:T(8,128)(2,1)S(1)}, u32[]{:S(2)}, u32[]{:S(2)}) collective-permute-start(bf16[256,2,128]{2,0,1:T(8,128)(2,1)S(1)} %get-tuple-element.667), channel_id=1, source_target_pairs={{0,4},{4,8},{8,12},{1,5},{5,9},{9,13},{2,6},{6,10},{10,14},{3,7},{... | collective-permute-start | bytes 393224 | tf_op jit(solution)/shard_map/while/body/eval_jaxpr/ppermute | solution.py:35
  67.3 0.8 collective-permute-done
  68.0 0.5 fusion.54
  68.5 0.3 fusion.55
  68.8 0.7 collective-permute-done.1
  69.5 0.9 %fusion.56 = f32[256,2,4,128]{3,0,2,1:T(8,128)S(1)} fusion(f32[256,2,4,256]{0,3,2,1:T(8,128)S(1)} %get-tuple-element.620, f32[256,2,4,128]{3,0,2,1:T(8,128)S(1)} %get-tuple-element.665, f32[256,2,4]{0,2,1:T(4,128)S(1)} %max.12, f32[256,2,4]{0,2,1:T(4,128)S(1)} %bitcast.95, bf16[256,2,128]{2,0,1:T(8,128)(2,1)S(1)} %collective-permute-done.1), kind=kOutput, calls=%fused_computation.6.clone.1 | convolution fusion | flops 135790592 | bytes 4341760 | tf_op jit(solution)/shard_map/while/body/eval_jaxpr/tkgs,skd->tkgd/dot_general | solution.py:102
  70.5 0.3 divide_convert_fusion
  70.8 1.2 %copy.94 = bf16[256,2,4,128]{3,2,1,0:T(4,128)(2,1)} copy(bf16[256,2,4,128]{3,0,2,1:T(8,128)(2,1)S(1)} %divide_convert_fusion) | data formatting | bytes 1048576 | tf_op jit(solution)/shard_map/convert_element_type | solution.py:126
  72.3 0.3 convert_multiply_fusion
  72.6 2.2 %fusion.13 = f32[256,8,128]{0,2,1:T(8,128)S(1)} fusion(f32[8,256]{1,0:T(8,128)S(1)} %add_bitcast_fusion.1, pred[256,256]{1,0:T(8,128)(4,1)S(1)} %iota_compare_fusion, bf16[256,8,128]{2,1,0:T(8,128)(2,1)} %param.13, bf16[256,8,128]{2,1,0:T(8,128)(2,1)} %param.12, bf16[256,8,128]{2,1,0:T(8,128)(2,1)S(1)} %copy-done), kind=kOutput, calls=%fused_computation.26 | convolution fusion | flops 271056896 | bytes 2695168 | tf_op jit(solution)/shard_map/hij,jhd->ihd/dot_general | solution.py:54
  74.8 4.5 %while.39 = (s32[]{:T(128)}, f32[8,128,128]{2,1,0:T(8,128)S(1)}, s32[]{:T(128)}, bf16[4,8]{1,0:T(4,128)(2,1)S(1)}, bf16[4,8,128,128]{3,2,1,0:T(8,128)(2,1)}, /*index=5*/s32[]{:T(128)}, s32[]{:T(128)}) while((s32[]{:T(128)}, f32[8,128,128]{2,1,0:T(8,128)S(1)}, s32[]{:T(128)}, bf16[4,8]{1,0:T(4,128)(2,1)S(1)}, ...), condition=%wide.region_4.5_spmd.clone, body=%wide.region_3.4_spmd.clone.sunk | while | flops 655372 | bytes 1310905 | solution.py:29
  74.9 1.1 %fusion.57 = f32[8,128,128]{2,1,0:T(8,128)S(1)} fusion(f32[8,128,128]{2,1,0:T(8,128)S(1)} %get-tuple-element.636, bf16[4,8,128,128]{3,2,1,0:T(8,128)(2,1)} %get-tuple-element.646, s32[]{:T(128)} %get-tuple-element.635, f32[8]{0:T(128)S(1)} %bitcast_convert_fusion.2, pred[]{:T(512)S(6)} %compare.3, pred[]{:T(512)S(6)} %lt.31), kind=kLoop, calls=%fused_computation.18.clone.1 | loop fusion | flops 655360 | bytes 1310758 | tf_op jit(solution)/shard_map/while/body/eval_jaxpr/jit(_where)/select_n | solution.py:27
  76.0 1.1 %fusion.57 = f32[8,128,128]{2,1,0:T(8,128)S(1)} fusion(f32[8,128,128]{2,1,0:T(8,128)S(1)} %get-tuple-element.636, bf16[4,8,128,128]{3,2,1,0:T(8,128)(2,1)} %get-tuple-element.646, s32[]{:T(128)} %get-tuple-element.635, f32[8]{0:T(128)S(1)} %bitcast_convert_fusion.2, pred[]{:T(512)S(6)} %compare.3, pred[]{:T(512)S(6)} %lt.31), kind=kLoop, calls=%fused_computation.18.clone.1 | loop fusion | flops 655360 | bytes 1310758 | tf_op jit(solution)/shard_map/while/body/eval_jaxpr/jit(_where)/select_n | solution.py:27
  77.1 1.1 %fusion.57 = f32[8,128,128]{2,1,0:T(8,128)S(1)} fusion(f32[8,128,128]{2,1,0:T(8,128)S(1)} %get-tuple-element.636, bf16[4,8,128,128]{3,2,1,0:T(8,128)(2,1)} %get-tuple-element.646, s32[]{:T(128)} %get-tuple-element.635, f32[8]{0:T(128)S(1)} %bitcast_convert_fusion.2, pred[]{:T(512)S(6)} %compare.3, pred[]{:T(512)S(6)} %lt.31), kind=kLoop, calls=%fused_computation.18.clone.1 | loop fusion | flops 655360 | bytes 1310758 | tf_op jit(solution)/shard_map/while/body/eval_jaxpr/jit(_where)/select_n | solution.py:27
  78.3 1.1 %fusion.57 = f32[8,128,128]{2,1,0:T(8,128)S(1)} fusion(f32[8,128,128]{2,1,0:T(8,128)S(1)} %get-tuple-element.636, bf16[4,8,128,128]{3,2,1,0:T(8,128)(2,1)} %get-tuple-element.646, s32[]{:T(128)} %get-tuple-element.635, f32[8]{0:T(128)S(1)} %bitcast_convert_fusion.2, pred[]{:T(512)S(6)} %compare.3, pred[]{:T(512)S(6)} %lt.31), kind=kLoop, calls=%fused_computation.18.clone.1 | loop fusion | flops 655360 | bytes 1310758 | tf_op jit(solution)/shard_map/while/body/eval_jaxpr/jit(_where)/select_n | solution.py:27
  79.4 1.2 %multiply_reduce_fusion = (f32[256,8]{0,1:T(8,128)S(1)}, f32[256,8,128]{0,2,1:T(8,128)S(1)}) fusion(f32[256,8,128]{0,2,1:T(8,128)S(1)} %fusion.13, f32[8,128,128]{2,1,0:T(8,128)S(1)} %get-tuple-element.361, f32[256,8,128]{2,1,0:T(8,128)S(1)} %convert_multiply_fusion), kind=kOutput, calls=%fused_computation.37 | convolution fusion | flops 403437568 | bytes 3678208 | tf_op jit(solution)/shard_map/ihd,hde->ihe/dot_general | solution.py:76
  80.7 1.1 %copy.95 = bf16[256,8,128]{2,1,0:T(8,128)(2,1)} copy(bf16[256,8,128]{0,2,1:T(8,128)(2,1)S(1)} %multiply_convert_fusion.1) | data formatting | bytes 1048576
  (69 shorter events, 1.6 us)
Async XLA Ops:
  7.2 6.4 %copy-start = (bf16[256,8,128]{2,1,0:T(8,128)(2,1)S(1)}, bf16[256,8,128]{2,1,0:T(8,128)(2,1)}, u32[]{:S(2)}) copy-start(bf16[256,8,128]{2,1,0:T(8,128)(2,1)} %param.14) | copy-start | bytes 1572868
  7.2 7.6 %copy-start.5 = (s32[6]{0:T(128)S(1)}, s32[6]{0:T(128)}, u32[]{:S(2)}) copy-start(s32[6]{0:T(128)} %param.19) | copy-start | bytes 76
  7.2 7.9 %copy-start.3 = (bf16[256,8,128]{2,1,0:T(8,128)(2,1)S(1)}, bf16[256,8,128]{2,1,0:T(8,128)(2,1)}, u32[]{:S(2)}) copy-start(bf16[256,8,128]{2,1,0:T(8,128)(2,1)} %param.16) | copy-start | bytes 1572868
  7.2 67.6 %all-gather.4.cloned.1.call-start = ((), (), s32[]{:S(2)}) async-start(), calls=%async_computation | async-start | bytes 1310720 | tf_op jit(solution)/shard_map/all_gather | solution.py:12
  12.1 3.1 %copy-start.1 = (bf16[256,2,128]{2,1,0:T(2,128)(2,1)S(1)}, bf16[256,2,128]{2,1,0:T(2,128)(2,1)}, u32[]{:S(2)}) copy-start(bf16[256,2,128]{2,1,0:T(2,128)(2,1)} %param.17) | copy-start | bytes 393220
  15.2 0.9 %copy-start.2 = (bf16[256,2,128]{2,1,0:T(2,128)(2,1)S(1)}, bf16[256,2,128]{2,1,0:T(2,128)(2,1)}, u32[]{:S(2)}) copy-start(bf16[256,2,128]{2,1,0:T(2,128)(2,1)} %param.18) | copy-start | bytes 393220
  29.8 8.0 %collective-permute-start = (bf16[256,2,128]{2,0,1:T(8,128)(2,1)S(1)}, bf16[256,2,128]{2,0,1:T(8,128)(2,1)S(1)}, u32[]{:S(2)}, u32[]{:S(2)}) collective-permute-start(bf16[256,2,128]{2,0,1:T(8,128)(2,1)S(1)} %get-tuple-element.666), channel_id=1, source_target_pairs={{0,4},{4,8},{8,12},{1,5},{5,9},{9,13},{2,6},{6,10},{10,14},{3,7},{... | collective-permute-start | bytes 393224 | tf_op jit(solution)/shard_map/while/body/eval_jaxpr/ppermute | solution.py:35
  31.1 11.3 %collective-permute-start.1 = (bf16[256,2,128]{2,0,1:T(8,128)(2,1)S(1)}, bf16[256,2,128]{2,0,1:T(8,128)(2,1)S(1)}, u32[]{:S(2)}, u32[]{:S(2)}) collective-permute-start(bf16[256,2,128]{2,0,1:T(8,128)(2,1)S(1)} %get-tuple-element.667), channel_id=1, source_target_pairs={{0,4},{4,8},{8,12},{1,5},{5,9},{9,13},{2,6},{6,10},{10,14},{3,7},{... | collective-permute-start | bytes 393224 | tf_op jit(solution)/shard_map/while/body/eval_jaxpr/ppermute | solution.py:35
  43.4 13.3 %collective-permute-start = (bf16[256,2,128]{2,0,1:T(8,128)(2,1)S(1)}, bf16[256,2,128]{2,0,1:T(8,128)(2,1)S(1)}, u32[]{:S(2)}, u32[]{:S(2)}) collective-permute-start(bf16[256,2,128]{2,0,1:T(8,128)(2,1)S(1)} %get-tuple-element.666), channel_id=1, source_target_pairs={{0,4},{4,8},{8,12},{1,5},{5,9},{9,13},{2,6},{6,10},{10,14},{3,7},{... | collective-permute-start | bytes 393224 | tf_op jit(solution)/shard_map/while/body/eval_jaxpr/ppermute | solution.py:35
  51.1 7.9 %collective-permute-start.1 = (bf16[256,2,128]{2,0,1:T(8,128)(2,1)S(1)}, bf16[256,2,128]{2,0,1:T(8,128)(2,1)S(1)}, u32[]{:S(2)}, u32[]{:S(2)}) collective-permute-start(bf16[256,2,128]{2,0,1:T(8,128)(2,1)S(1)} %get-tuple-element.667), channel_id=1, source_target_pairs={{0,4},{4,8},{8,12},{1,5},{5,9},{9,13},{2,6},{6,10},{10,14},{3,7},{... | collective-permute-start | bytes 393224 | tf_op jit(solution)/shard_map/while/body/eval_jaxpr/ppermute | solution.py:35
  59.9 8.1 %collective-permute-start = (bf16[256,2,128]{2,0,1:T(8,128)(2,1)S(1)}, bf16[256,2,128]{2,0,1:T(8,128)(2,1)S(1)}, u32[]{:S(2)}, u32[]{:S(2)}) collective-permute-start(bf16[256,2,128]{2,0,1:T(8,128)(2,1)S(1)} %get-tuple-element.666), channel_id=1, source_target_pairs={{0,4},{4,8},{8,12},{1,5},{5,9},{9,13},{2,6},{6,10},{10,14},{3,7},{... | collective-permute-start | bytes 393224 | tf_op jit(solution)/shard_map/while/body/eval_jaxpr/ppermute | solution.py:35
  64.3 5.2 %collective-permute-start.1 = (bf16[256,2,128]{2,0,1:T(8,128)(2,1)S(1)}, bf16[256,2,128]{2,0,1:T(8,128)(2,1)S(1)}, u32[]{:S(2)}, u32[]{:S(2)}) collective-permute-start(bf16[256,2,128]{2,0,1:T(8,128)(2,1)S(1)} %get-tuple-element.667), channel_id=1, source_target_pairs={{0,4},{4,8},{8,12},{1,5},{5,9},{9,13},{2,6},{6,10},{10,14},{3,7},{... | collective-permute-start | bytes 393224 | tf_op jit(solution)/shard_map/while/body/eval_jaxpr/ppermute | solution.py:35
  70.5 1.8 %copy-start.4 = (bf16[256,8,128]{2,1,0:T(8,128)(2,1)S(1)}, bf16[256,8,128]{2,1,0:T(8,128)(2,1)}, u32[]{:S(2)}) copy-start(bf16[256,8,128]{2,1,0:T(8,128)(2,1)} %param.12) | copy-start | bytes 1572868
Sparse Core Ops, SparseCore 0:
  14.7 33.3 all-gather.3
where the time goes:
time: 89.1 us; the launch traced here: 88.6 us
  starting transfers between devices  24.1 us (27%)
  between operations  15.6 us (18%)
  blocking collectives  12.7 us (14%)
  other arithmetic  11.6 us (13%)
  waiting for transfers between devices  10.5 us (12%)
  matrix products  10 us (11%)
  local copies, waits for them, and re-layouts  3.77 us (4%)
    ppermute x6, starting transfers between devices, from_behind(): lax.ppermute(value, axis, [(source, source + steps) for source in range(l...  24 us
    all_gather x1, blocking collectives, carried_in(): lax.all_gather(part.astype(kind), axis)  12.7 us
    ppermute x6, waiting for transfers between devices, from_behind(): lax.ppermute(value, axis, [(source, source + steps) for source in range(l...  10.4 us
    select_n x4, other arithmetic, step(): return jax.tree.map(lambda a, b: jnp.where(reached, a, b), new, before)  4.37 us
    dot_general x4, matrix products, tile(): jnp.einsum('tkgs,skd->tkgd', weights.astype(jnp.bfloat16), v_tile, prefer...  3.72 us
    dot_general x1, matrix products, lightning_part(): jnp.einsum('hij,jhd->ihd', inner, v_lin, preferred_element_type=jnp.float32)  2.18 us
    dot_general x4, matrix products, tile(): jnp.einsum('tkgd,skd->tkgs', q_four, k_tile, preferred_element_type=jnp.f...  1.85 us
  transfers between devices with their start and end apart: 7, of which 5 were waited for; matrix products, arithmetic and copies ran while one was open for 14% of the time, Pallas kernels for 0%

commit v1 on v0

v1 whole, which is shorter than its diff:
```python
import functools
import math

import jax
import jax.numpy as jnp
from jax import lax
from jax.experimental import pallas as pl
from jax.experimental.pallas import tpu as pltpu
from jax.sharding import PartitionSpec as P

F32 = jnp.float32
BF16 = jnp.bfloat16
MASKED = -1e30
VMEM = pl.BlockSpec(memory_space=pltpu.VMEM)
SMEM = pl.BlockSpec(memory_space=pltpu.SMEM)


def call(body, outs, ins, scratch=(), flops=0, name=None):
    moved = sum(math.prod(x.shape) * x.dtype.itemsize for x in list(outs) + [i for i, _ in ins])
    return pl.pallas_call(
        body,
        out_shape=tuple(outs),
        in_specs=[spec for _, spec in ins],
        out_specs=tuple(VMEM for _ in outs),
        scratch_shapes=list(scratch),
        cost_estimate=pl.CostEstimate(flops=flops, bytes_accessed=moved, transcendentals=0),
        name=name,
    )(*[value for value, _ in ins])


def shaped(shape, dtype):
    return jax.ShapeDtypeStruct(shape, dtype)


def rise_of(decay):
    tok = decay.shape[0]
    rows = lax.broadcasted_iota(jnp.int32, (tok, tok), 0)
    columns = lax.broadcasted_iota(jnp.int32, (tok, tok), 1)
    lower = (rows >= columns).astype(F32)
    return jnp.dot(lower, decay, precision=lax.Precision.HIGHEST, preferred_element_type=F32)


def state_body(keep_ref, k_ref, v_ref, a_ref, state_ref, send_ref, decay_ref, wide):
    tok, heads, _ = k_ref.shape
    rise = rise_of(a_ref[...])
    last = rise[tok - 1 : tok, :]
    decay_ref[...] = jnp.exp(last)
    fade = jnp.exp(last - rise)
    wide[0] = k_ref[...].astype(F32)
    wide[1] = v_ref[...].astype(F32)
    keep = keep_ref[0] > 0
    for h in range(heads):
        tail = (wide[0, :, h, :] * fade[:, h : h + 1]).astype(BF16)
        value = wide[1, :, h, :].astype(BF16)
        state = lax.dot_general(
            tail, value, (((0,), (0,)), ((), ())), preferred_element_type=F32
        )
        state_ref[h] = state
        send_ref[h] = jnp.where(keep, state, 0.0).astype(BF16)


def intra_body(q_ref, k_ref, v_ref, a_ref, intra_ref, query_ref, lift_ref, wide):
    tok, heads, _ = k_ref.shape
    rise = rise_of(a_ref[...])
    rise_t = jnp.transpose(rise)
    lift_ref[...] = jnp.exp(rise)
    wide[0] = q_ref[...].astype(F32)
    wide[1] = k_ref[...].astype(F32)
    wide[2] = v_ref[...].astype(F32)
    rows = lax.broadcasted_iota(jnp.int32, (tok, tok), 0)
    columns = lax.broadcasted_iota(jnp.int32, (tok, tok), 1)
    lower = rows >= columns
    for h in range(heads):
        query = wide[0, :, h, :].astype(BF16)
        key = wide[1, :, h, :].astype(BF16)
        value = wide[2, :, h, :].astype(BF16)
        query_ref[h] = query
        scores = lax.dot_general(
            query, key, (((1,), (1,)), ((), ())), preferred_element_type=F32
        )
        gap = jnp.where(lower, rise[:, h : h + 1] - rise_t[h : h + 1, :], MASKED)
        inner = (scores * jnp.exp(gap)).astype(BF16)
        intra_ref[h] = jnp.dot(inner, value, preferred_element_type=F32)


def finish_lin_body(intra_ref, query_ref, lift_ref, state_ref, out_ref, wide):
    heads = query_ref.shape[0]
    for h in range(heads):
        inter = jnp.dot(query_ref[h], state_ref[h], preferred_element_type=F32)
        total = intra_ref[h] + lift_ref[:, h : h + 1] * inter
        mean = jnp.mean(total * total, axis=-1, keepdims=True)
        wide[:, h, :] = total * lax.rsqrt(mean + 1e-06)
    out_ref[...] = wide[...].astype(BF16)


def tile_of(kv_heads, heads, q, k_ref, v_ref, split, bias, causal):
    keys = k_ref.shape[0] // kv_heads
    rows = q.shape[0]
    group = heads // kv_heads
    split[0] = k_ref[...].astype(F32)
    split[1] = v_ref[...].astype(F32)
    head_of_row = (lax.broadcasted_iota(jnp.int32, (rows, 128), 0) % heads) // group
    scores = None
    values = []
    for g in range(kv_heads):
        key = split[0, pl.ds(g, keys, stride=kv_heads), :].astype(BF16)
        values.append(split[1, pl.ds(g, keys, stride=kv_heads), :].astype(BF16))
        part = lax.dot_general(q, key, (((1,), (1,)), ((), ())), preferred_element_type=F32)
        mine = jnp.tile(head_of_row, (1, keys // 128)) == g
        scores = part if g == 0 else jnp.where(mine, part, scores)
    scores = scores * (1.0 / math.sqrt(q.shape[1]))
    if causal:
        position = lax.broadcasted_iota(jnp.int32, (rows, keys), 0) // heads
        column = lax.broadcasted_iota(jnp.int32, (rows, keys), 1)
        scores = jnp.where(column <= position, scores, MASKED)
    else:
        scores = scores + bias
    top = jnp.max(scores, axis=-1, keepdims=True)

    def mix(weights):
        weights = weights.astype(BF16)
        acc = None
        for g in range(kv_heads):
            part = jnp.dot(weights, values[g], preferred_element_type=F32)
            acc = part if g == 0 else jnp.where(head_of_row == g, part, acc)
        ones = jnp.ones((keys, 128), BF16)
        return acc, jnp.dot(weights, ones, preferred_element_type=F32)

    return scores, top, mix


def first_tile_body(kv_heads, heads, q_ref, k_ref, v_ref, top_ref, sum_ref, acc_ref, split):
    scores, top, mix = tile_of(kv_heads, heads, q_ref[...], k_ref, v_ref, split, None, True)
    acc, summed = mix(jnp.exp(scores - top))
    top_ref[...] = jnp.broadcast_to(top, top_ref.shape)
    sum_ref[...] = summed
    acc_ref[...] = acc


def next_tile_body(
    kv_heads, heads, last, bias_ref, q_ref, k_ref, v_ref, top_ref, sum_ref, acc_ref, *rest
):
    scores, top, mix = tile_of(
        kv_heads, heads, q_ref[...], k_ref, v_ref, rest[-1], bias_ref[0], False
    )
    old = top_ref[:, :1]
    new = jnp.maximum(old, top)
    acc, summed = mix(jnp.exp(scores - new))
    shrink = jnp.exp(old - new)
    acc = acc_ref[...] * shrink + acc
    summed = sum_ref[...] * shrink + summed
    if last:
        rest[0][...] = (acc / summed).astype(BF16)
    else:
        rest[0][...] = jnp.broadcast_to(new, top_ref.shape)
        rest[1][...] = summed
        rest[2][...] = acc


def doc_index(position, doc_starts):
    return jnp.sum((doc_starts <= position).astype(jnp.int32)) - 1


def on_device(q_lin, k_lin, v_lin, decay_log, q_soft, k_soft, v_soft, doc_starts):
    tok, heads, dim = q_lin.shape
    soft_heads, kv_heads = (q_soft.shape[1], k_soft.shape[1])
    ranks = lax.axis_size("ctx")
    me = lax.axis_index("ctx")
    here = doc_index(me * tok, doc_starts)
    keep = (here == doc_index((me + 1) * tok, doc_starts)).astype(jnp.int32)[None]

    rows, cols = (tok * soft_heads, tok * kv_heads)
    q = q_soft.reshape(rows, dim)
    held = (k_soft.reshape(cols, dim), v_soft.reshape(cols, dim))
    wide_row = shaped((rows, 128), F32)
    split = pltpu.VMEM((2, cols, dim), F32)
    tile_flops = 6 * rows * tok * dim

    state, send, factor = call(
        state_body,
        (shaped((heads, dim, dim), F32), shaped((heads, dim, dim), BF16), shaped((1, heads), F32)),
        ((keep, SMEM), (k_lin, VMEM), (v_lin, VMEM), (decay_log, VMEM)),
        (pltpu.VMEM((2, tok, heads, dim), F32),),
        flops=2 * heads * tok * dim * dim,
        name="state",
    )
    factor = factor[0][:, None, None]

    stats = call(
        functools.partial(first_tile_body, kv_heads, soft_heads),
        (wide_row, wide_row, wide_row),
        ((q, VMEM), (held[0], VMEM), (held[1], VMEM)),
        (split,),
        flops=tile_flops,
        name="first_tile",
    )
    for step in range(1, ranks - 1):
        pairs = [(i, i + 1) for i in range(step - 1, ranks - 2)]
        held = lax.ppermute(held, "ctx", pairs)
        seen = (me >= step) & (doc_index((me - step) * tok, doc_starts) == here)
        bias = jnp.where(seen, 0.0, MASKED).astype(F32)[None]
        last = step == ranks - 2
        stats = call(
            functools.partial(next_tile_body, kv_heads, soft_heads, last),
            (shaped((rows, dim), BF16),) if last else (wide_row, wide_row, wide_row),
            ((bias, SMEM), (q, VMEM), (held[0], VMEM), (held[1], VMEM))
            + tuple((x, VMEM) for x in stats),
            (split,),
            flops=tile_flops,
            name="last_tile" if last else "next_tile",
        )
    soft_out = stats[0].reshape(q_soft.shape)

    entering = jnp.zeros((heads, dim, dim), BF16)
    for step in range(ranks - 2):
        arrived = lax.ppermute(send, "ctx", [(step, step + 1)])
        entering = jnp.where(me == step + 1, arrived, entering)
        if step < ranks - 3:
            send = jnp.where(keep[0] > 0, factor * arrived.astype(F32) + state, 0.0).astype(BF16)

    intra, query, lift = call(
        intra_body,
        (shaped((heads, tok, dim), F32), shaped((heads, tok, dim), BF16), shaped((tok, heads), F32)),
        ((q_lin, VMEM), (k_lin, VMEM), (v_lin, VMEM), (decay_log, VMEM)),
        (pltpu.VMEM((3, tok, heads, dim), F32),),
        flops=4 * heads * tok * tok * dim,
        name="intra",
    )
    (lin_out,) = call(
        finish_lin_body,
        (shaped((tok, heads, dim), BF16),),
        ((intra, VMEM), (query, VMEM), (lift, VMEM), (entering, VMEM)),
        (pltpu.VMEM((tok, heads, dim), F32),),
        flops=2 * heads * tok * dim * dim,
        name="finish_lin",
    )
    return (lin_out, soft_out)


def solution(mesh):
    wide = P(("group", "ctx"), ("head", "sub"), None)
    return jax.shard_map(
        on_device,
        mesh=mesh,
        in_specs=(wide, wide, wide, P(("group", "ctx"), ("head", "sub")), wide, wide, wide, P("group")),
        out_specs=(wide, wide),
        check_vma=False,
    )
```

time: 89.1 us -> 57.5 us (0.65)
  Pallas kernels: 0 us -> 32.9 us
  starting transfers between devices: 24.1 us -> 11.3 us
  blocking collectives: 12.7 us -> 0 us
  between operations: 15.6 us -> 3.39 us
  matrix products: 10 us -> 0 us
  other arithmetic: 11.6 us -> 2.66 us
  waiting for transfers between devices: 10.5 us -> 3.96 us
  local copies, waits for them, and re-layouts: 3.77 us -> 2.8 us
    pallas_call x0 -> x6, Pallas kernels: none -> 32.9 us  [call(): pl.pallas_call(body, out_shape=tuple(outs), in_specs=[spec for _, spec in...]
    ppermute x6, starting transfers between devices: 24 us -> 11.3 us  [the longest x4 5.65 us: on_device(): held = lax.ppermute(held, 'ctx', pairs)]
    all_gather x1 -> x0, blocking collectives: 12.7 us -> none  [carried_in(): lax.all_gather(part.astype(kind), axis)]
    dot_general x11 -> x0, matrix products: 10 us -> none  [the longest x4 3.72 us: tile(): jnp.einsum('tkgs,skd->tkgd', weights.astype(jnp.bfloat16), v_tile, prefer...]
    ppermute x6, waiting for transfers between devices: 10.4 us -> 3.96 us  [the longest x2 2.78 us: on_device(): arrived = lax.ppermute(send, 'ctx', [(step, step + 1)])]
    select_n x4 -> x1, other arithmetic: 4.37 us -> 0.74 us  [on_device(): entering = jnp.where(me == step + 1, arrived, entering)]
    reduce_sum x9 -> x1, other arithmetic: 2.48 us -> 0.72 us  [doc_index(): return jnp.sum((doc_starts <= position).astype(jnp.int32)) - 1]
    unnamed x17 -> x19, local copies, waits for them, and re-layouts: 1.31 us -> 2.8 us
  transfers between devices with their start and end apart: 7 -> 6, of which waited for: 5 -> 3; matrix products, arithmetic and copies ran while one was open for 14% -> 2% of each run, Pallas kernels for 0% -> 43%
where the time goes in v1:
time: 57.5 us; the launch traced here: 57 us
  Pallas kernels  32.9 us (57%)
  starting transfers between devices  11.3 us (20%)
  waiting for transfers between devices  3.96 us (7%)
  between operations  3.39 us (6%)
  local copies, waits for them, and re-layouts  2.8 us (5%)
  other arithmetic  2.66 us (5%)
    pallas_call x6, Pallas kernels, call(): pl.pallas_call(body, out_shape=tuple(outs), in_specs=[spec for _, spec in...  32.9 us
    ppermute x4, starting transfers between devices, on_device(): held = lax.ppermute(held, 'ctx', pairs)  5.65 us
    ppermute x2, starting transfers between devices, on_device(): arrived = lax.ppermute(send, 'ctx', [(step, step + 1)])  5.64 us
    unnamed x19, local copies, waits for them, and re-layouts  2.8 us
    ppermute x2, waiting for transfers between devices, on_device(): arrived = lax.ppermute(send, 'ctx', [(step, step + 1)])  2.78 us
    convert_element_type x1, other arithmetic, on_device(): jnp.where(keep[0] > 0, factor * arrived.astype(F32) + state, 0.0)  1.2 us
    ppermute x4, waiting for transfers between devices, on_device(): held = lax.ppermute(held, 'ctx', pairs)  1.17 us
  transfers between devices with their start and end apart: 6, of which 3 were waited for; matrix products, arithmetic and copies ran while one was open for 2% of the time, Pallas kernels for 43%

profile of v1, /device:TPU:0, one launch (start us, length us, event | category | flops | bytes accessed | tf_op | source)
XLA Modules:
  0.0 57.0 jit_solution(14632654264955505590)
XLA Ops:
  0.6 0.0 copy-start.6
  0.6 0.6 %copy-done.6 = s32[6]{0:T(128)S(1)} copy-done((s32[6]{0:T(128)S(1)}, s32[6]{0:T(128)}, u32[]{:S(2)}) %copy-start.6) | copy-done | bytes 48
  1.3 0.0 copy-start.4
  1.3 0.7 %fusion.3 = (s32[]{:T(128)}, s32[]{:T(128)}, s32[]{:T(128)}, s32[]{:T(128)}) fusion(s32[6]{0:T(128)S(1)} %copy-done.6, s32[]{:T(128)S(6)} %mul.28, s32[]{:T(128)S(6)} %mul.23, s32[]{:T(128)S(6)} %mul.22, s32[]{:T(128)S(6)} %mul.27), kind=kLoop, calls=%fused_computation.9 | loop fusion | flops 68 | bytes 56 | tf_op jit(solution)/shard_map/reduce_sum | solution.py:161
  3.3 0.0 copy-done.4
  3.3 0.8 %copy.10.a_ref = f32[256,8]{1,0:T(8,128)} copy(f32[256,8]{0,1:T(8,128)S(1)} %copy-done.4) | data formatting | bytes 16384 | tf_op args[3]
  4.1 0.0 copy-start.7
  4.1 0.0 copy-start.8
  4.1 4.6 %state.1 = (f32[8,128,128]{2,1,0:T(8,128)}, bf16[8,128,128]{2,1,0:T(8,128)(2,1)}, f32[1,8]{1,0:T(1,128)}) custom-call(s32[1]{0:T(128)} %bitcast.keep_ref, bf16[256,8,128]{2,1,0:T(8,128)(2,1)} %k_ref.3, bf16[256,8,128]{2,1,0:T(8,128)(2,1)} %v_ref.3, f32[256,8]{1,0:T(8,128)} %copy.10.a_ref), custom_call_target="tpu_custom_call" | custom-call | flops 67108864 | bytes 1843236 | tf_op jit(solution)/shard_map/state/pallas_call | solution.py:20
  8.7 5.0 %collective-permute-start = (bf16[8,128,128]{2,1,0:T(8,128)(2,1)}, bf16[8,128,128]{2,1,0:T(8,128)(2,1)S(1)}, u32[]{:S(2)}, u32[]{:S(2)}) collective-permute-start(bf16[8,128,128]{2,1,0:T(8,128)(2,1)} %get-tuple-element.18), channel_id=1, source_target_pairs={{0,4},{1,5},{2,6},{3,7},{16,20},{17,21},{18,22},{19,23}} | collective-permute-start | bytes 786440 | tf_op jit(solution)/shard_map/ppermute | solution.py:216
  13.7 0.0 copy-done.7
  13.7 1.3 %collective-permute-start.2 = (bf16[512,128]{1,0:T(8,128)(2,1)S(1)}, bf16[512,128]{1,0:T(8,128)(2,1)S(1)}, u32[]{:S(2)}, u32[]{:S(2)}) collective-permute-start(bf16[512,128]{1,0:T(8,128)(2,1)S(1)} %bitcast.14), channel_id=1, source_target_pairs={{0,4},{4,8},{1,5},{5,9},{2,6},{6,10},{3,7},{7,11},{16,20},{20,24},... | collective-permute-start | bytes 393224 | tf_op jit(solution)/shard_map/ppermute | solution.py:199
  15.0 0.0 copy-done.8
  15.0 2.9 %collective-permute-start.4 = (bf16[512,128]{1,0:T(8,128)(2,1)S(1)}, bf16[512,128]{1,0:T(8,128)(2,1)S(1)}, u32[]{:S(2)}, u32[]{:S(2)}) collective-permute-start(bf16[512,128]{1,0:T(8,128)(2,1)S(1)} %bitcast.16), channel_id=1, source_target_pairs={{0,4},{4,8},{1,5},{5,9},{2,6},{6,10},{3,7},{7,11},{16,20},{20,24},... | collective-permute-start | bytes 393224 | tf_op jit(solution)/shard_map/ppermute | solution.py:199
  17.9 2.8 %collective-permute-done = bf16[8,128,128]{2,1,0:T(8,128)(2,1)S(1)} collective-permute-done((bf16[8,128,128]{2,1,0:T(8,128)(2,1)}, bf16[8,128,128]{2,1,0:T(8,128)(2,1)S(1)}, u32[]{:S(2)}, u32[]{:S(2)}) %collective-permute-start) | collective-permute-done | bytes 262176 | tf_op jit(solution)/shard_map/ppermute | solution.py:216
  20.6 0.0 copy-start.5
  20.6 0.7 %copy-done.5 = f32[1,8]{1,0:T(1,128)S(1)} copy-done((f32[1,8]{1,0:T(1,128)S(1)}, f32[1,8]{1,0:T(1,128)}, u32[]{:S(2)}) %copy-start.5) | copy-done | bytes 56
  21.3 1.2 %select_convert_fusion = bf16[8,128,128]{2,1,0:T(8,128)(2,1)S(1)} fusion(f32[8,128,128]{2,1,0:T(8,128)} %get-tuple-element.19, bf16[8,128,128]{2,1,0:T(8,128)(2,1)S(1)} %collective-permute-done, f32[8]{0:T(128)S(1)} %bitcast.12, pred[]{:T(512)S(6)} %gt.3), kind=kLoop, calls=%fused_computation | loop fusion | flops 655360 | bytes 1048609 | tf_op jit(solution)/shard_map/convert_element_type | solution.py:219
  22.5 0.7 %collective-permute-start.1 = (bf16[8,128,128]{2,1,0:T(8,128)(2,1)S(1)}, bf16[8,128,128]{2,1,0:T(8,128)(2,1)S(1)}, u32[]{:S(2)}, u32[]{:S(2)}) collective-permute-start(bf16[8,128,128]{2,1,0:T(8,128)(2,1)S(1)} %select_convert_fusion), channel_id=1, source_target_pairs={{4,8},{5,9},{6,10},{7,11},{20,24},{21,25},{22,26},{23,27}} | collective-permute-start | bytes 786440 | tf_op jit(solution)/shard_map/ppermute | solution.py:216
  23.2 0.2 collective-permute-done.2.k_ref
  23.3 0.0 copy-start
  23.4 0.7 %collective-permute-start.3 = (bf16[512,128]{1,0:T(8,128)(2,1)S(1)}, bf16[512,128]{1,0:T(8,128)(2,1)S(1)}, u32[]{:S(2)}, u32[]{:S(2)}) collective-permute-start(bf16[512,128]{1,0:T(8,128)(2,1)S(1)} %collective-permute-done.2.k_ref), channel_id=1, source_target_pairs={{4,8},{5,9},{6,10},{7,11},{20,24},{21,25},{22,26},{23,27}} | collective-permute-start | bytes 393224 | tf_op jit(solution)/shard_map/ppermute | solution.py:199
  24.0 1.0 %collective-permute-done.4.v_ref = bf16[512,128]{1,0:T(8,128)(2,1)S(1)} collective-permute-done((bf16[512,128]{1,0:T(8,128)(2,1)S(1)}, bf16[512,128]{1,0:T(8,128)(2,1)S(1)}, u32[]{:S(2)}, u32[]{:S(2)}) %collective-permute-start.4) | collective-permute-done | bytes 131104 | tf_op jit(solution)/shard_map/ppermute | solution.py:199
  25.0 0.0 copy-start.1
  25.0 0.8 %collective-permute-start.5 = (bf16[512,128]{1,0:T(8,128)(2,1)S(1)}, bf16[512,128]{1,0:T(8,128)(2,1)S(1)}, u32[]{:S(2)}, u32[]{:S(2)}) collective-permute-start(bf16[512,128]{1,0:T(8,128)(2,1)S(1)} %collective-permute-done.4.v_ref), channel_id=1, source_target_pairs={{4,8},{5,9},{6,10},{7,11},{20,24},{21,25},{22,26},{23,27}} | collective-permute-start | bytes 393224 | tf_op jit(solution)/shard_map/ppermute | solution.py:199
  27.2 6.9 %intra.1 = (f32[8,256,128]{2,1,0:T(8,128)}, bf16[8,256,128]{2,1,0:T(8,128)(2,1)}, f32[256,8]{1,0:T(8,128)}) custom-call(bf16[256,8,128]{2,1,0:T(8,128)(2,1)} %q_ref.1, bf16[256,8,128]{2,1,0:T(8,128)(2,1)} %k_ref.3, bf16[256,8,128]{2,1,0:T(8,128)(2,1)} %v_ref.3, f32[256,8]{1,0:T(8,128)} %copy.10.a_ref), custom_call_target="tpu_custom_call" | custom-call | flops 268435456 | bytes 3162112 | tf_op jit(solution)/shard_map/intra/pallas_call | solution.py:20
  34.1 0.0 copy-done
  34.1 0.0 copy-done.1
  34.1 4.6 %first_tile.1 = (f32[2048,128]{1,0:T(8,128)}, f32[2048,128]{1,0:T(8,128)}, f32[2048,128]{1,0:T(8,128)}) custom-call(bf16[2048,128]{1,0:T(8,128)(2,1)} %bitcast.8, bf16[512,128]{1,0:T(8,128)(2,1)} %bitcast.13, bf16[512,128]{1,0:T(8,128)(2,1)} %bitcast.15), custom_call_target="tpu_custom_call" | custom-call | flops 402653184 | bytes 3932160 | tf_op jit(solution)/shard_map/first_tile/pallas_call | solution.py:20
  38.7 6.8 %next_tile.1 = (f32[2048,128]{1,0:T(8,128)}, f32[2048,128]{1,0:T(8,128)}, f32[2048,128]{1,0:T(8,128)}) custom-call(f32[1]{0:T(128)} %bitcast.6.bias_ref, bf16[2048,128]{1,0:T(8,128)(2,1)} %bitcast.9, bf16[512,128]{1,0:T(8,128)(2,1)} %copy-done, bf16[512,128]{1,0:T(8,128)(2,1)} %copy-done.1, f32[2048,128]{1,0:T(8,128)} %get-tuple-element.20.top_ref, ...), custom_call_target="tpu_custom_call" | custom-call | flops 402653184 | bytes 7077892 | tf_op jit(solution)/shard_map/next_tile/pallas_call | solution.py:20
  45.4 0.0 collective-permute-done.3.k_ref
  45.5 0.0 copy-start.2
  45.5 0.0 collective-permute-done.5.v_ref
  45.5 0.0 copy-start.3
  45.5 0.6 %copy-done.2 = bf16[512,128]{1,0:T(8,128)(2,1)} copy-done((bf16[512,128]{1,0:T(8,128)(2,1)}, bf16[512,128]{1,0:T(8,128)(2,1)S(1)}, u32[]{:S(2)}) %copy-start.2) | copy-done | bytes 131096
  46.1 0.0 copy-done.3
  46.1 6.2 %last_tile.1 = bf16[2048,128]{1,0:T(8,128)(2,1)} custom-call(f32[1]{0:T(128)} %bitcast.2.bias_ref, bf16[2048,128]{1,0:T(8,128)(2,1)} %bitcast.10, bf16[512,128]{1,0:T(8,128)(2,1)} %copy-done.2, bf16[512,128]{1,0:T(8,128)(2,1)} %copy-done.3, f32[2048,128]{1,0:T(8,128)} %get-tuple-element.23.top_ref, f32[2048,128]{1,0:T(8,128)} %get-tuple-element.24.sum_ref, ...), custom_call_target="tpu_custom_call" | custom-call | flops 402653184 | bytes 4456452 | tf_op jit(solution)/shard_map/last_tile/pallas_call | solution.py:20
  52.4 0.0 collective-permute-done.1
  52.4 0.7 %select_select_fusion.state_ref = bf16[8,128,128]{2,1,0:T(8,128)(2,1)} fusion(bf16[8,128,128]{2,1,0:T(8,128)(2,1)S(1)} %collective-permute-done.1, bf16[8,128,128]{2,1,0:T(8,128)(2,1)S(1)} %collective-permute-done, pred[]{:T(512)S(6)} %eq.17, pred[]{:T(512)S(6)} %eq.15), kind=kLoop, calls=%fused_computation.1 | loop fusion | flops 262144 | bytes 786434 | tf_op jit(solution)/shard_map/jit(_where)/select_n | solution.py:217
  53.1 3.8 %finish_lin.1 = bf16[256,8,128]{2,1,0:T(8,128)(2,1)} custom-call(f32[8,256,128]{2,1,0:T(8,128)} %get-tuple-element.14.intra_ref, bf16[8,256,128]{2,1,0:T(8,128)(2,1)} %get-tuple-element.15.query_ref, f32[256,8]{1,0:T(8,128)} %get-tuple-element.16.lift_ref, bf16[8,128,128]{2,1,0:T(8,128)(2,1)} %select_select_fusion.state_ref), custom_call_target="tpu_custom_call" | custom-call | flops 67108864 | bytes 2367488 | tf_op jit(solution)/shard_map/finish_lin/pallas_call | solution.py:20
Async XLA Ops:
  0.6 0.7 %copy-start.6 = (s32[6]{0:T(128)S(1)}, s32[6]{0:T(128)}, u32[]{:S(2)}) copy-start(s32[6]{0:T(128)} %param.15) | copy-start | bytes 76
  1.3 2.0 %copy-start.4 = (f32[256,8]{0,1:T(8,128)S(1)}, f32[256,8]{0,1:T(8,128)}, u32[]{:S(2)}) copy-start(f32[256,8]{0,1:T(8,128)} %param.11) | copy-start | bytes 24580
  4.1 9.5 %copy-start.7 = (bf16[256,2,128]{2,1,0:T(2,128)(2,1)S(1)}, bf16[256,2,128]{2,1,0:T(2,128)(2,1)}, u32[]{:S(2)}) copy-start(bf16[256,2,128]{2,1,0:T(2,128)(2,1)} %param.13) | copy-start | bytes 393220
  4.1 10.9 %copy-start.8 = (bf16[256,2,128]{2,1,0:T(2,128)(2,1)S(1)}, bf16[256,2,128]{2,1,0:T(2,128)(2,1)}, u32[]{:S(2)}) copy-start(bf16[256,2,128]{2,1,0:T(2,128)(2,1)} %param.14) | copy-start | bytes 393220
  8.7 11.9 %collective-permute-start = (bf16[8,128,128]{2,1,0:T(8,128)(2,1)}, bf16[8,128,128]{2,1,0:T(8,128)(2,1)S(1)}, u32[]{:S(2)}, u32[]{:S(2)}) collective-permute-start(bf16[8,128,128]{2,1,0:T(8,128)(2,1)} %get-tuple-element.18), channel_id=1, source_target_pairs={{0,4},{1,5},{2,6},{3,7},{16,20},{17,21},{18,22},{19,23}} | collective-permute-start | bytes 786440 | tf_op jit(solution)/shard_map/ppermute | solution.py:216
  13.7 9.7 %collective-permute-start.2 = (bf16[512,128]{1,0:T(8,128)(2,1)S(1)}, bf16[512,128]{1,0:T(8,128)(2,1)S(1)}, u32[]{:S(2)}, u32[]{:S(2)}) collective-permute-start(bf16[512,128]{1,0:T(8,128)(2,1)S(1)} %bitcast.14), channel_id=1, source_target_pairs={{0,4},{4,8},{1,5},{5,9},{2,6},{6,10},{3,7},{7,11},{16,20},{20,24},... | collective-permute-start | bytes 393224 | tf_op jit(solution)/shard_map/ppermute | solution.py:199
  15.0 10.0 %collective-permute-start.4 = (bf16[512,128]{1,0:T(8,128)(2,1)S(1)}, bf16[512,128]{1,0:T(8,128)(2,1)S(1)}, u32[]{:S(2)}, u32[]{:S(2)}) collective-permute-start(bf16[512,128]{1,0:T(8,128)(2,1)S(1)} %bitcast.16), channel_id=1, source_target_pairs={{0,4},{4,8},{1,5},{5,9},{2,6},{6,10},{3,7},{7,11},{16,20},{20,24},... | collective-permute-start | bytes 393224 | tf_op jit(solution)/shard_map/ppermute | solution.py:199
  20.6 0.7 %copy-start.5 = (f32[1,8]{1,0:T(1,128)S(1)}, f32[1,8]{1,0:T(1,128)}, u32[]{:S(2)}) copy-start(f32[1,8]{1,0:T(1,128)} %get-tuple-element.17) | copy-start | bytes 100
  22.5 29.9 %collective-permute-start.1 = (bf16[8,128,128]{2,1,0:T(8,128)(2,1)S(1)}, bf16[8,128,128]{2,1,0:T(8,128)(2,1)S(1)}, u32[]{:S(2)}, u32[]{:S(2)}) collective-permute-start(bf16[8,128,128]{2,1,0:T(8,128)(2,1)S(1)} %select_convert_fusion), channel_id=1, source_target_pairs={{4,8},{5,9},{6,10},{7,11},{20,24},{21,25},{22,26},{23,27}} | collective-permute-start | bytes 786440 | tf_op jit(solution)/shard_map/ppermute | solution.py:216
  23.3 10.8 %copy-start = (bf16[512,128]{1,0:T(8,128)(2,1)}, bf16[512,128]{1,0:T(8,128)(2,1)S(1)}, u32[]{:S(2)}) copy-start(bf16[512,128]{1,0:T(8,128)(2,1)S(1)} %collective-permute-done.2.k_ref) | copy-start | bytes 393220
  23.4 22.1 %collective-permute-start.3 = (bf16[512,128]{1,0:T(8,128)(2,1)S(1)}, bf16[512,128]{1,0:T(8,128)(2,1)S(1)}, u32[]{:S(2)}, u32[]{:S(2)}) collective-permute-start(bf16[512,128]{1,0:T(8,128)(2,1)S(1)} %collective-permute-done.2.k_ref), channel_id=1, source_target_pairs={{4,8},{5,9},{6,10},{7,11},{20,24},{21,25},{22,26},{23,27}} | collective-permute-start | bytes 393224 | tf_op jit(solution)/shard_map/ppermute | solution.py:199
  25.0 9.1 %copy-start.1 = (bf16[512,128]{1,0:T(8,128)(2,1)}, bf16[512,128]{1,0:T(8,128)(2,1)S(1)}, u32[]{:S(2)}) copy-start(bf16[512,128]{1,0:T(8,128)(2,1)S(1)} %collective-permute-done.4.v_ref) | copy-start | bytes 393220
  25.0 20.4 %collective-permute-start.5 = (bf16[512,128]{1,0:T(8,128)(2,1)S(1)}, bf16[512,128]{1,0:T(8,128)(2,1)S(1)}, u32[]{:S(2)}, u32[]{:S(2)}) collective-permute-start(bf16[512,128]{1,0:T(8,128)(2,1)S(1)} %collective-permute-done.4.v_ref), channel_id=1, source_target_pairs={{4,8},{5,9},{6,10},{7,11},{20,24},{21,25},{22,26},{23,27}} | collective-permute-start | bytes 393224 | tf_op jit(solution)/shard_map/ppermute | solution.py:199
  45.5 0.7 %copy-start.2 = (bf16[512,128]{1,0:T(8,128)(2,1)}, bf16[512,128]{1,0:T(8,128)(2,1)S(1)}, u32[]{:S(2)}) copy-start(bf16[512,128]{1,0:T(8,128)(2,1)S(1)} %collective-permute-done.3.k_ref) | copy-start | bytes 393220
  45.5 0.7 %copy-start.3 = (bf16[512,128]{1,0:T(8,128)(2,1)}, bf16[512,128]{1,0:T(8,128)(2,1)S(1)}, u32[]{:S(2)}) copy-start(bf16[512,128]{1,0:T(8,128)(2,1)S(1)} %collective-permute-done.5.v_ref) | copy-start | bytes 393220

commit v2 on v1

v2 whole, which is shorter than its diff:
```python
import functools
import math

import jax
import jax.numpy as jnp
from jax import lax
from jax.experimental import pallas as pl
from jax.experimental.pallas import tpu as pltpu
from jax.sharding import PartitionSpec as P

F32 = jnp.float32
BF16 = jnp.bfloat16
MASKED = -1e30
LOG2E = 1.0 / math.log(2.0)
VMEM = pl.BlockSpec(memory_space=pltpu.VMEM)
SMEM = pl.BlockSpec(memory_space=pltpu.SMEM)


def shaped(shape, dtype):
    return jax.ShapeDtypeStruct(shape, dtype)


def call(body, outs, ins, scratch=(), flops=0, name=None):
    moved = sum(math.prod(x.shape) * x.dtype.itemsize for x in list(outs) + [i for i, _ in ins])
    return pl.pallas_call(
        body,
        out_shape=tuple(outs),
        in_specs=[spec for _, spec in ins],
        out_specs=tuple(VMEM for _ in outs),
        scratch_shapes=list(scratch),
        cost_estimate=pl.CostEstimate(flops=flops, bytes_accessed=moved, transcendentals=0),
        compiler_params=pltpu.CompilerParams(vmem_limit_bytes=16 << 20),
        name=name,
    )(*[value for value, _ in ins])


def doc_at(docs_ref, position):
    count = jnp.int32(0)
    for i in range(docs_ref.shape[0]):
        count += (docs_ref[i] <= position).astype(jnp.int32)
    return count


def rise_of(decay_t):
    tok = decay_t.shape[1]
    rows = lax.broadcasted_iota(jnp.int32, (tok, tok), 0)
    columns = lax.broadcasted_iota(jnp.int32, (tok, tok), 1)
    upper = (rows <= columns).astype(F32)
    return jnp.dot(decay_t, upper, precision=lax.Precision.HIGHEST, preferred_element_type=F32)


def dot_t(a, b):
    return lax.dot_general(a, b, (((1,), (1,)), ((), ())), preferred_element_type=F32)


def dot(a, b):
    return jnp.dot(a, b, preferred_element_type=F32)


def state_body(me_ref, docs_ref, k_ref, v_ref, a_ref, state_ref, send_ref, factor_ref, kh_ref, vh_ref, kw, vw):
    heads, tok = a_ref.shape
    start = me_ref[0] * tok
    keep = doc_at(docs_ref, start) == doc_at(docs_ref, start + tok)
    rise = rise_of(a_ref[...])
    last = rise[:, tok - 1 : tok]
    factor_ref[...] = jnp.where(keep, jnp.broadcast_to(jnp.exp(last), factor_ref.shape), 0.0)
    fade = jnp.exp(last - rise)
    kw[...] = k_ref[...].astype(F32)
    vw[...] = v_ref[...].astype(F32)
    for h in range(heads):
        key = kw[pl.ds(h, tok, stride=heads), :]
        value = vw[pl.ds(h, tok, stride=heads), :].astype(BF16)
        kh_ref[h] = key.astype(BF16)
        vh_ref[h] = value
        tail_t = (jnp.transpose(key) * fade[h : h + 1, :]).astype(BF16)
        state = jnp.where(keep, dot(tail_t, value), 0.0)
        state_ref[h] = state
        send_ref[h] = state.astype(BF16)


def intra_body(q_ref, kh_ref, vh_ref, a_ref, intra_ref, qh_ref, lift_ref, qw):
    heads, tok = a_ref.shape
    rise_t = rise_of(a_ref[...]) * LOG2E
    rise = jnp.transpose(rise_t)
    lift_ref[...] = jnp.exp2(rise)
    qw[...] = q_ref[...].astype(F32)
    half = tok // 2
    lower = lax.broadcasted_iota(jnp.int32, (half, half), 0) >= lax.broadcasted_iota(
        jnp.int32, (half, half), 1
    )
    for h in range(heads):
        query = qw[pl.ds(h, tok, stride=heads), :].astype(BF16)
        qh_ref[h] = query
        key, value = (kh_ref[h], vh_ref[h])
        column = rise[:, h : h + 1]
        row = rise_t[h : h + 1, :]
        for part in range(2):
            low, high = (part * half, (part + 1) * half)
            scores = dot_t(query[low:high], key[:high])
            gap = column[low:high] - row[:, :high]
            end = jnp.where(lower, gap[:, low:], MASKED)
            gap = jnp.concatenate([gap[:, :low], end], axis=1) if part else end
            inner = (scores * jnp.exp2(gap)).astype(BF16)
            intra_ref[h, low:high] = dot(inner, value[:high])


def finish_lin_body(intra_ref, qh_ref, lift_ref, before_ref, arrived_ref, out_ref, wide):
    heads, tok, dim = qh_ref.shape
    for h in range(heads):
        inter = dot(qh_ref[h], before_ref[h] + arrived_ref[h])
        total = intra_ref[h] + lift_ref[:, h : h + 1] * inter
        mean = jnp.sum(total * total, axis=-1, keepdims=True) * (1.0 / dim)
        wide[pl.ds(h, tok, stride=heads), :] = total * lax.rsqrt(mean + 1e-06)
    out_ref[...] = wide[...].astype(BF16)


def keys_of(ref, wide, count, g):
    keys = ref.shape[0] // count
    if count == 1:
        return ref[...]
    if g == 0:
        wide[...] = ref[...].astype(F32)
    return wide[pl.ds(g, keys, stride=count), :].astype(BF16)


def first_tile_body(kv_heads, heads, q_ref, k_ref, v_ref, qh_ref, top_ref, acc_ref, qw, kw, vw):
    tok = q_ref.shape[0] // heads
    power = LOG2E / math.sqrt(q_ref.shape[1])
    half = tok // 2
    lower = lax.broadcasted_iota(jnp.int32, (half, half), 0) >= lax.broadcasted_iota(
        jnp.int32, (half, half), 1
    )
    qw[...] = q_ref[...].astype(F32)
    ones = jnp.ones((tok, 128), BF16)
    for g in range(kv_heads):
        key = keys_of(k_ref, kw, kv_heads, g)
        value = jnp.concatenate([keys_of(v_ref, vw, kv_heads, g), ones], axis=1)
        for h in range(g * heads // kv_heads, (g + 1) * heads // kv_heads):
            query = qw[pl.ds(h, tok, stride=heads), :].astype(BF16)
            qh_ref[h] = query
            for part in range(2):
                low, high = (part * half, (part + 1) * half)
                scores = dot_t(query[low:high], key[:high])
                end = jnp.where(lower, scores[:, low:], MASKED)
                scores = jnp.concatenate([scores[:, :low], end], axis=1) if part else end
                top = jnp.max(scores, axis=-1, keepdims=True)
                weights = jnp.exp2((scores - top) * power).astype(BF16)
                top_ref[h, low:high] = jnp.broadcast_to(top, (half, 128))
                acc_ref[h, low:high] = dot(weights, value[:high])


def next_tile_body(
    kv_heads, step, last, me_ref, docs_ref, qh_ref, k_ref, v_ref, top_ref, acc_ref, *rest
):
    heads, tok, dim = qh_ref.shape
    kw, vw = rest[-2:]
    power = LOG2E / math.sqrt(dim)
    start = me_ref[0] * tok
    seen = (me_ref[0] >= step) & (doc_at(docs_ref, start - step * tok) == doc_at(docs_ref, start))
    bias = jnp.where(seen, 0.0, MASKED).astype(F32)
    half = tok // 2
    ones = jnp.ones((tok, 128), BF16)
    for g in range(kv_heads):
        key = keys_of(k_ref, kw, kv_heads, g)
        value = jnp.concatenate([keys_of(v_ref, vw, kv_heads, g), ones], axis=1)
        for h in range(g * heads // kv_heads, (g + 1) * heads // kv_heads):
            for part in range(2):
                low, high = (part * half, (part + 1) * half)
                scores = dot_t(qh_ref[h, low:high], key)
                old = top_ref[h, low:high]
                top = jnp.max(scores, axis=-1, keepdims=True) + bias
                new = jnp.maximum(old, jnp.broadcast_to(top, old.shape))
                shift = jnp.tile(new - bias, (1, tok // 128))
                weights = jnp.exp2((scores - shift) * power).astype(BF16)
                shrink = jnp.exp2((old - new) * power)
                both = dot(weights, value)
                acc = acc_ref[h, low:high, :dim] * shrink + both[:, :dim]
                summed = acc_ref[h, low:high, dim:] * shrink + both[:, dim:]
                if last:
                    rest[1][pl.ds(low * heads + h, half, stride=heads), :] = acc / summed
                else:
                    rest[0][h, low:high] = new
                    rest[1][h, low:high, :dim] = acc
                    rest[1][h, low:high, dim:] = summed
    if last:
        rest[0][...] = rest[1][...].astype(BF16)


def on_device(q_lin, k_lin, v_lin, decay_log, q_soft, k_soft, v_soft, doc_starts):
    tok, heads, dim = q_lin.shape
    soft_heads, kv_heads = (q_soft.shape[1], k_soft.shape[1])
    ranks = lax.axis_size("ctx")
    me = lax.axis_index("ctx")[None]
    flat = lambda x: x.reshape(-1, dim)
    q_lin, k_lin, v_lin, q_soft, k_soft, v_soft = map(
        flat, (q_lin, k_lin, v_lin, q_soft, k_soft, v_soft)
    )
    decay_t = decay_log.T
    place = ((me, SMEM), (doc_starts, SMEM))
    wide_lin = pltpu.VMEM(q_lin.shape, F32)
    wide_q = pltpu.VMEM(q_soft.shape, F32)
    wide_k = pltpu.VMEM(k_soft.shape, F32)
    per_head = shaped((heads, tok, dim), BF16)

    state, send, factor, k_heads, v_heads = call(
        state_body,
        (
            shaped((heads, dim, dim), F32),
            shaped((heads, dim, dim), BF16),
            shaped((heads, 128), F32),
            per_head,
            per_head,
        ),
        place + ((k_lin, VMEM), (v_lin, VMEM), (decay_t, VMEM)),
        (wide_lin, wide_lin),
        flops=2 * heads * tok * dim * dim,
        name="state",
    )

    tile_flops = 6 * soft_heads * tok * tok * dim
    stat_shapes = (shaped((soft_heads, tok, 128), F32), shaped((soft_heads, tok, 2 * dim), F32))
    query, *stats = call(
        functools.partial(first_tile_body, kv_heads, soft_heads),
        (shaped((soft_heads, tok, dim), BF16),) + stat_shapes,
        ((q_soft, VMEM), (k_soft, VMEM), (v_soft, VMEM)),
        (wide_q, wide_k, wide_k),
        flops=tile_flops,
        name="first_tile",
    )
    held = (k_soft, v_soft)
    for step in range(1, ranks - 1):
        pairs = [(i, i + 1) for i in range(step - 1, ranks - 2)]
        held = lax.ppermute(held, "ctx", pairs)
        last = step == ranks - 2
        stats = call(
            functools.partial(next_tile_body, kv_heads, step, last),
            (shaped(q_soft.shape, BF16),) if last else stat_shapes,
            place
            + ((query, VMEM), (held[0], VMEM), (held[1], VMEM))
            + tuple((x, VMEM) for x in stats),
            ((wide_q,) if last else ()) + (wide_k, wide_k),
            flops=tile_flops,
            name="last_tile" if last else "next_tile",
        )
    soft_out = stats[0].reshape(tok, soft_heads, dim)

    before = jnp.zeros((heads, dim, dim), BF16)
    arrived = None
    for step in range(ranks - 2):
        if arrived is not None:
            before = before + arrived
            send = (factor[:, None, :] * arrived.astype(F32) + state).astype(BF16)
        arrived = lax.ppermute(send, "ctx", [(step, step + 1)])

    intra, query, lift = call(
        intra_body,
        (shaped((heads, tok, dim), F32), per_head, shaped((tok, heads), F32)),
        ((q_lin, VMEM), (k_heads, VMEM), (v_heads, VMEM), (decay_t, VMEM)),
        (wide_lin,),
        flops=4 * heads * tok * tok * dim,
        name="intra",
    )
    (lin_out,) = call(
        finish_lin_body,
        (shaped(q_lin.shape, BF16),),
        ((intra, VMEM), (query, VMEM), (lift, VMEM), (before, VMEM), (arrived, VMEM)),
        (wide_lin,),
        flops=2 * heads * tok * dim * dim,
        name="finish_lin",
    )
    return (lin_out.reshape(tok, heads, dim), soft_out)


def solution(mesh):
    wide = P(("group", "ctx"), ("head", "sub"), None)
    return jax.shard_map(
        on_device,
        mesh=mesh,
        in_specs=(wide, wide, wide, P(("group", "ctx"), ("head", "sub")), wide, wide, wide, P("group")),
        out_specs=(wide, wide),
        check_vma=False,
    )
```

time: 57.5 us -> 33.2 us (0.58)
  the two profiles are of different devices: /device:TPU:0 before, /device:TPU:22 now
where the time goes in v2:
time: 33.2 us; the launch traced here: 32.9 us
  Pallas kernels  10.9 us (33%)
  waiting for transfers between devices  10.6 us (32%)
  starting transfers between devices  7.11 us (21%)
  local copies, waits for them, and re-layouts  3.5 us (11%)
  between operations  0.79 us (2%)
    pallas_call x6, Pallas kernels, call(): pl.pallas_call(body, out_shape=tuple(outs), in_specs=[spec for _, spec in...  10.9 us
    ppermute x4, waiting for transfers between devices, on_device(): held = lax.ppermute(held, 'ctx', pairs)  10.5 us
    ppermute x4, starting transfers between devices, on_device(): held = lax.ppermute(held, 'ctx', pairs)  5.15 us
    unnamed x18, local copies, waits for them, and re-layouts  3.5 us
    ppermute x2, starting transfers between devices, on_device(): arrived = lax.ppermute(send, 'ctx', [(step, step + 1)])  1.97 us
  transfers between devices with their start and end apart: 6, of which 4 were waited for; matrix products, arithmetic and copies ran while one was open for 0% of the time, Pallas kernels for 23%

profile of v2, /device:TPU:22, one launch (start us, length us, event | category | flops | bytes accessed | tf_op | source)
XLA Modules:
  0.0 32.9 jit_solution(5405109283941240235)
XLA Ops:
  0.6 0.0 copy-start
  0.6 0.0 copy-start.1
  0.7 1.1 %copy-done.1 = bf16[256,8,128]{2,1,0:T(8,128)(2,1)S(1)} copy-done((bf16[256,8,128]{2,1,0:T(8,128)(2,1)S(1)}, bf16[256,8,128]{2,1,0:T(8,128)(2,1)}, u32[]{:S(2)}) %copy-start.1) | copy-done | bytes 524312
  1.7 0.0 copy-start.2
  1.7 1.0 %copy-done.2 = bf16[256,8,128]{2,1,0:T(8,128)(2,1)S(1)} copy-done((bf16[256,8,128]{2,1,0:T(8,128)(2,1)S(1)}, bf16[256,8,128]{2,1,0:T(8,128)(2,1)}, u32[]{:S(2)}) %copy-start.2) | copy-done | bytes 524312
  2.8 0.0 copy-start.3
  2.8 0.7 %copy-done.3 = f32[256,8]{0,1:T(8,128)S(1)} copy-done((f32[256,8]{0,1:T(8,128)S(1)}, f32[256,8]{0,1:T(8,128)}, u32[]{:S(2)}) %copy-start.3) | copy-done | bytes 8216
  3.5 0.0 copy-start.4
  3.5 0.7 %copy-done.4 = s32[6]{0:T(128)S(1)} copy-done((s32[6]{0:T(128)S(1)}, s32[6]{0:T(128)}, u32[]{:S(2)}) %copy-start.4) | copy-done | bytes 48
  4.1 0.0 copy-start.6
  4.1 0.0 copy-start.7
  4.1 0.0 copy-start.8
  4.1 1.5 %state.1 = (f32[8,128,128]{2,1,0:T(8,128)S(1)}, bf16[8,128,128]{2,1,0:T(8,128)(2,1)S(1)}, f32[8,128]{1,0:T(8,128)S(1)}, bf16[8,256,128]{2,1,0:T(8,128)(2,1)S(1)}, bf16[8,256,128]{2,1,0:T(8,128)(2,1)S(1)}) custom-call(s32[1]{0:T(128)} %bitcast.1.me_ref, s32[6]{0:T(128)S(1)} %copy-done.4, bf16[2048,128]{1,0:T(8,128)(2,1)S(1)} %bitcast.11, ...), custom_call_target="tpu_custom_call" | custom-call | flops 67108864 | bytes 2895900 | tf_op jit(solution)/shard_map/state/pallas_call | solution.py:25
  5.6 0.0 copy-start.5
  5.6 0.7 %collective-permute-start = (bf16[8,128,128]{2,1,0:T(8,128)(2,1)S(1)}, bf16[8,128,128]{2,1,0:T(8,128)(2,1)S(1)}, u32[]{:S(2)}, u32[]{:S(2)}) collective-permute-start(bf16[8,128,128]{2,1,0:T(8,128)(2,1)S(1)} %get-tuple-element.20), channel_id=1, source_target_pairs={{0,4},{1,5},{2,6},{3,7},{16,20},{17,21},{18,22},{19,23}} | collective-permute-start | bytes 786440 | tf_op jit(solution)/shard_map/ppermute | solution.py:253
  6.3 1.3 %collective-permute-start.2 = (bf16[512,128]{1,0:T(8,128)(2,1)}, bf16[512,128]{1,0:T(8,128)(2,1)S(1)}, u32[]{:S(2)}, u32[]{:S(2)}) collective-permute-start(bf16[512,128]{1,0:T(8,128)(2,1)} %bitcast.16), channel_id=1, source_target_pairs={{0,4},{4,8},{1,5},{5,9},{2,6},{6,10},{3,7},{7,11},{16,20},{20,24},... | collective-permute-start | bytes 393224 | tf_op jit(solution)/shard_map/ppermute | solution.py:233
  7.6 1.3 %collective-permute-start.4 = (bf16[512,128]{1,0:T(8,128)(2,1)}, bf16[512,128]{1,0:T(8,128)(2,1)S(1)}, u32[]{:S(2)}, u32[]{:S(2)}) collective-permute-start(bf16[512,128]{1,0:T(8,128)(2,1)} %bitcast.18), channel_id=1, source_target_pairs={{0,4},{4,8},{1,5},{5,9},{2,6},{6,10},{3,7},{7,11},{16,20},{20,24},... | collective-permute-start | bytes 393224 | tf_op jit(solution)/shard_map/ppermute | solution.py:233
  8.9 0.0 collective-permute-done.before_ref
  8.9 0.1 add_convert_fusion
  9.0 1.3 %collective-permute-start.1 = (bf16[8,128,128]{2,1,0:T(8,128)(2,1)S(1)}, bf16[8,128,128]{2,1,0:T(8,128)(2,1)S(1)}, u32[]{:S(2)}, u32[]{:S(2)}) collective-permute-start(bf16[8,128,128]{2,1,0:T(8,128)(2,1)S(1)} %add_convert_fusion), channel_id=1, source_target_pairs={{4,8},{5,9},{6,10},{7,11},{20,24},{21,25},{22,26},{23,27}} | collective-permute-start | bytes 786440 | tf_op jit(solution)/shard_map/ppermute | solution.py:253
  10.3 4.2 %collective-permute-done.2.k_ref = bf16[512,128]{1,0:T(8,128)(2,1)S(1)} collective-permute-done((bf16[512,128]{1,0:T(8,128)(2,1)}, bf16[512,128]{1,0:T(8,128)(2,1)S(1)}, u32[]{:S(2)}, u32[]{:S(2)}) %collective-permute-start.2) | collective-permute-done | bytes 131104 | tf_op jit(solution)/shard_map/ppermute | solution.py:233
  14.5 1.3 %collective-permute-start.3 = (bf16[512,128]{1,0:T(8,128)(2,1)S(1)}, bf16[512,128]{1,0:T(8,128)(2,1)S(1)}, u32[]{:S(2)}, u32[]{:S(2)}) collective-permute-start(bf16[512,128]{1,0:T(8,128)(2,1)S(1)} %collective-permute-done.2.k_ref), channel_id=1, source_target_pairs={{4,8},{5,9},{6,10},{7,11},{20,24},{21,25},{22,26},{23,27}} | collective-permute-start | bytes 393224 | tf_op jit(solution)/shard_map/ppermute | solution.py:233
  15.8 0.6 %collective-permute-done.4.v_ref = bf16[512,128]{1,0:T(8,128)(2,1)S(1)} collective-permute-done((bf16[512,128]{1,0:T(8,128)(2,1)}, bf16[512,128]{1,0:T(8,128)(2,1)S(1)}, u32[]{:S(2)}, u32[]{:S(2)}) %collective-permute-start.4) | collective-permute-done | bytes 131104 | tf_op jit(solution)/shard_map/ppermute | solution.py:233
  16.5 1.3 %collective-permute-start.5 = (bf16[512,128]{1,0:T(8,128)(2,1)S(1)}, bf16[512,128]{1,0:T(8,128)(2,1)S(1)}, u32[]{:S(2)}, u32[]{:S(2)}) collective-permute-start(bf16[512,128]{1,0:T(8,128)(2,1)S(1)} %collective-permute-done.4.v_ref), channel_id=1, source_target_pairs={{4,8},{5,9},{6,10},{7,11},{20,24},{21,25},{22,26},{23,27}} | collective-permute-start | bytes 393224 | tf_op jit(solution)/shard_map/ppermute | solution.py:233
  17.8 0.0 copy-done
  17.8 2.1 %intra.1 = (f32[8,256,128]{2,1,0:T(8,128)S(1)}, bf16[8,256,128]{2,1,0:T(8,128)(2,1)S(1)}, f32[256,8]{1,0:T(8,128)S(1)}) custom-call(bf16[2048,128]{1,0:T(8,128)(2,1)S(1)} %bitcast.10, bf16[8,256,128]{2,1,0:T(8,128)(2,1)S(1)} %get-tuple-element.15.kh_ref, bf16[8,256,128]{2,1,0:T(8,128)(2,1)S(1)} %get-tuple-element.16.vh_ref, f32[8,256]{1,0:T(8,128)S(1)} %bitcast.14), custom_call_target="tpu_custom_call" | custom-call | flops 268435456 | bytes 3162112 | tf_op jit(solution)/shard_map/intra/pallas_call | solution.py:25
  19.9 0.0 copy-done.6
  19.9 0.0 copy-done.7
  19.9 0.0 copy-done.8
  19.9 1.2 %first_tile.1 = (bf16[8,256,128]{2,1,0:T(8,128)(2,1)S(1)}, f32[8,256,128]{2,1,0:T(8,128)S(1)}, f32[8,256,256]{2,1,0:T(8,128)S(1)}) custom-call(bf16[2048,128]{1,0:T(8,128)(2,1)S(1)} %bitcast.15, bf16[512,128]{1,0:T(8,128)(2,1)S(1)} %bitcast.17, bf16[512,128]{1,0:T(8,128)(2,1)S(1)} %bitcast.19), custom_call_target="tpu_custom_call" | custom-call | flops 402653184 | bytes 4456448 | tf_op jit(solution)/shard_map/first_tile/pallas_call | solution.py:25
  21.1 0.0 copy-done.5
  21.1 1.6 %next_tile.1 = (f32[8,256,128]{2,1,0:T(8,128)S(1)}, f32[8,256,256]{2,1,0:T(8,128)S(1)}) custom-call(s32[1]{0:T(128)} %bitcast.1.me_ref, s32[6]{0:T(128)S(1)} %copy-done.5, bf16[8,256,128]{2,1,0:T(8,128)(2,1)S(1)} %get-tuple-element.23.qh_ref, bf16[512,128]{1,0:T(8,128)(2,1)S(1)} %collective-permute-done.2.k_ref, ...), custom_call_target="tpu_custom_call" | custom-call | flops 402653184 | bytes 7077916 | tf_op jit(solution)/shard_map/next_tile/pallas_call | solution.py:25
  22.8 4.3 %collective-permute-done.3.k_ref = bf16[512,128]{1,0:T(8,128)(2,1)S(1)} collective-permute-done((bf16[512,128]{1,0:T(8,128)(2,1)S(1)}, bf16[512,128]{1,0:T(8,128)(2,1)S(1)}, u32[]{:S(2)}, u32[]{:S(2)}) %collective-permute-start.3) | collective-permute-done | bytes 131104 | tf_op jit(solution)/shard_map/ppermute | solution.py:233
  27.0 1.4 %collective-permute-done.5.v_ref = bf16[512,128]{1,0:T(8,128)(2,1)S(1)} collective-permute-done((bf16[512,128]{1,0:T(8,128)(2,1)S(1)}, bf16[512,128]{1,0:T(8,128)(2,1)S(1)}, u32[]{:S(2)}, u32[]{:S(2)}) %collective-permute-start.5) | collective-permute-done | bytes 131104 | tf_op jit(solution)/shard_map/ppermute | solution.py:233
  28.4 2.6 %last_tile.1 = bf16[2048,128]{1,0:T(8,128)(2,1)} custom-call(s32[1]{0:T(128)} %bitcast.1.me_ref, s32[6]{0:T(128)S(1)} %copy-done.5, bf16[8,256,128]{2,1,0:T(8,128)(2,1)S(1)} %get-tuple-element.23.qh_ref, bf16[512,128]{1,0:T(8,128)(2,1)S(1)} %collective-permute-done.3.k_ref, bf16[512,128]{1,0:T(8,128)(2,1)S(1)} %collective-permute-done.5.v_ref, ...), custom_call_target="tpu_custom_call" | custom-call | flops 402653184 | bytes 4456476 | tf_op jit(solution)/shard_map/last_tile/pallas_call | solution.py:25
  31.0 0.0 collective-permute-done.1.arrived_ref
  31.0 1.9 %finish_lin.1 = bf16[2048,128]{1,0:T(8,128)(2,1)} custom-call(f32[8,256,128]{2,1,0:T(8,128)S(1)} %get-tuple-element.17.intra_ref, bf16[8,256,128]{2,1,0:T(8,128)(2,1)S(1)} %get-tuple-element.18.qh_ref, f32[256,8]{1,0:T(8,128)S(1)} %get-tuple-element.19.lift_ref, bf16[8,128,128]{2,1,0:T(8,128)(2,1)S(1)} %collective-permute-done.before_ref, ...), custom_call_target="tpu_custom_call" | custom-call | flops 67108864 | bytes 2629632 | tf_op jit(solution)/shard_map/finish_lin/pallas_call | solution.py:25
Async XLA Ops:
  0.6 17.1 %copy-start = (bf16[256,8,128]{2,1,0:T(8,128)(2,1)S(1)}, bf16[256,8,128]{2,1,0:T(8,128)(2,1)}, u32[]{:S(2)}) copy-start(bf16[256,8,128]{2,1,0:T(8,128)(2,1)} %param.8) | copy-start | bytes 1572868
  0.6 1.1 %copy-start.1 = (bf16[256,8,128]{2,1,0:T(8,128)(2,1)S(1)}, bf16[256,8,128]{2,1,0:T(8,128)(2,1)}, u32[]{:S(2)}) copy-start(bf16[256,8,128]{2,1,0:T(8,128)(2,1)} %param.9) | copy-start | bytes 1572868
  1.7 1.0 %copy-start.2 = (bf16[256,8,128]{2,1,0:T(8,128)(2,1)S(1)}, bf16[256,8,128]{2,1,0:T(8,128)(2,1)}, u32[]{:S(2)}) copy-start(bf16[256,8,128]{2,1,0:T(8,128)(2,1)} %param.10) | copy-start | bytes 1572868
  2.8 0.7 %copy-start.3 = (f32[256,8]{0,1:T(8,128)S(1)}, f32[256,8]{0,1:T(8,128)}, u32[]{:S(2)}) copy-start(f32[256,8]{0,1:T(8,128)} %param.11) | copy-start | bytes 24580
  3.5 0.7 %copy-start.4 = (s32[6]{0:T(128)S(1)}, s32[6]{0:T(128)}, u32[]{:S(2)}) copy-start(s32[6]{0:T(128)} %docs_ref.5) | copy-start | bytes 76
  4.1 15.8 %copy-start.6 = (bf16[256,8,128]{2,1,0:T(8,128)(2,1)S(1)}, bf16[256,8,128]{2,1,0:T(8,128)(2,1)}, u32[]{:S(2)}) copy-start(bf16[256,8,128]{2,1,0:T(8,128)(2,1)} %param.12) | copy-start | bytes 1572868
  4.1 15.8 %copy-start.7 = (bf16[256,2,128]{2,1,0:T(2,128)(2,1)S(1)}, bf16[256,2,128]{2,1,0:T(2,128)(2,1)}, u32[]{:S(2)}) copy-start(bf16[256,2,128]{2,1,0:T(2,128)(2,1)} %param.13) | copy-start | bytes 393220
  4.1 15.8 %copy-start.8 = (bf16[256,2,128]{2,1,0:T(2,128)(2,1)S(1)}, bf16[256,2,128]{2,1,0:T(2,128)(2,1)}, u32[]{:S(2)}) copy-start(bf16[256,2,128]{2,1,0:T(2,128)(2,1)} %param.14) | copy-start | bytes 393220
  5.6 15.5 %copy-start.5 = (s32[6]{0:T(128)S(1)}, s32[6]{0:T(128)}, u32[]{:S(2)}) copy-start(s32[6]{0:T(128)} %docs_ref.5) | copy-start | bytes 76
  5.6 3.3 %collective-permute-start = (bf16[8,128,128]{2,1,0:T(8,128)(2,1)S(1)}, bf16[8,128,128]{2,1,0:T(8,128)(2,1)S(1)}, u32[]{:S(2)}, u32[]{:S(2)}) collective-permute-start(bf16[8,128,128]{2,1,0:T(8,128)(2,1)S(1)} %get-tuple-element.20), channel_id=1, source_target_pairs={{0,4},{1,5},{2,6},{3,7},{16,20},{17,21},{18,22},{19,23}} | collective-permute-start | bytes 786440 | tf_op jit(solution)/shard_map/ppermute | solution.py:253
  6.3 8.2 %collective-permute-start.2 = (bf16[512,128]{1,0:T(8,128)(2,1)}, bf16[512,128]{1,0:T(8,128)(2,1)S(1)}, u32[]{:S(2)}, u32[]{:S(2)}) collective-permute-start(bf16[512,128]{1,0:T(8,128)(2,1)} %bitcast.16), channel_id=1, source_target_pairs={{0,4},{4,8},{1,5},{5,9},{2,6},{6,10},{3,7},{7,11},{16,20},{20,24},... | collective-permute-start | bytes 393224 | tf_op jit(solution)/shard_map/ppermute | solution.py:233
  7.6 8.9 %collective-permute-start.4 = (bf16[512,128]{1,0:T(8,128)(2,1)}, bf16[512,128]{1,0:T(8,128)(2,1)S(1)}, u32[]{:S(2)}, u32[]{:S(2)}) collective-permute-start(bf16[512,128]{1,0:T(8,128)(2,1)} %bitcast.18), channel_id=1, source_target_pairs={{0,4},{4,8},{1,5},{5,9},{2,6},{6,10},{3,7},{7,11},{16,20},{20,24},... | collective-permute-start | bytes 393224 | tf_op jit(solution)/shard_map/ppermute | solution.py:233
  9.0 22.0 %collective-permute-start.1 = (bf16[8,128,128]{2,1,0:T(8,128)(2,1)S(1)}, bf16[8,128,128]{2,1,0:T(8,128)(2,1)S(1)}, u32[]{:S(2)}, u32[]{:S(2)}) collective-permute-start(bf16[8,128,128]{2,1,0:T(8,128)(2,1)S(1)} %add_convert_fusion), channel_id=1, source_target_pairs={{4,8},{5,9},{6,10},{7,11},{20,24},{21,25},{22,26},{23,27}} | collective-permute-start | bytes 786440 | tf_op jit(solution)/shard_map/ppermute | solution.py:253
  14.5 12.5 %collective-permute-start.3 = (bf16[512,128]{1,0:T(8,128)(2,1)S(1)}, bf16[512,128]{1,0:T(8,128)(2,1)S(1)}, u32[]{:S(2)}, u32[]{:S(2)}) collective-permute-start(bf16[512,128]{1,0:T(8,128)(2,1)S(1)} %collective-permute-done.2.k_ref), channel_id=1, source_target_pairs={{4,8},{5,9},{6,10},{7,11},{20,24},{21,25},{22,26},{23,27}} | collective-permute-start | bytes 393224 | tf_op jit(solution)/shard_map/ppermute | solution.py:233
  16.5 12.0 %collective-permute-start.5 = (bf16[512,128]{1,0:T(8,128)(2,1)S(1)}, bf16[512,128]{1,0:T(8,128)(2,1)S(1)}, u32[]{:S(2)}, u32[]{:S(2)}) collective-permute-start(bf16[512,128]{1,0:T(8,128)(2,1)S(1)} %collective-permute-done.4.v_ref), channel_id=1, source_target_pairs={{4,8},{5,9},{6,10},{7,11},{20,24},{21,25},{22,26},{23,27}} | collective-permute-start | bytes 393224 | tf_op jit(solution)/shard_map/ppermute | solution.py:233

commit v3 on v2

v3 whole, which is shorter than its diff:
```python
import functools
import math

import jax
import jax.numpy as jnp
from jax import lax
from jax.experimental import pallas as pl
from jax.experimental.pallas import tpu as pltpu
from jax.sharding import PartitionSpec as P


F32 = jnp.float32
BF16 = jnp.bfloat16
MASKED = -1e30
LOG2E = 1.0 / math.log(2.0)
VMEM = pl.BlockSpec(memory_space=pltpu.VMEM)
SMEM = pl.BlockSpec(memory_space=pltpu.SMEM)
HBM = pl.BlockSpec(memory_space=pltpu.HBM)
DMA = pltpu.SemaphoreType.DMA


def shaped(shape, dtype):
    return jax.ShapeDtypeStruct(shape, dtype)


def call(body, outs, ins, scratch=(), flops=0, out_spec=VMEM):
    moved = sum(math.prod(x.shape) * x.dtype.itemsize for x in list(outs) + [i for i, _ in ins])
    return pl.pallas_call(
        body,
        out_shape=tuple(outs),
        in_specs=[spec for _, spec in ins],
        out_specs=tuple(out_spec for _ in outs),
        scratch_shapes=list(scratch),
        cost_estimate=pl.CostEstimate(flops=flops, bytes_accessed=moved, transcendentals=0),
        compiler_params=pltpu.CompilerParams(vmem_limit_bytes=16 << 20),
    )(*[pltpu.with_memory_space_constraint(x, pltpu.HBM) if spec is HBM else x for x, spec in ins])


def doc_at(docs_ref, position):
    count = jnp.int32(0)
    for i in range(docs_ref.shape[0]):
        count += (docs_ref[i] <= position).astype(jnp.int32)
    return count


def rise_of(decay_t):
    tok = decay_t.shape[1]
    rows = lax.broadcasted_iota(jnp.int32, (tok, tok), 0)
    columns = lax.broadcasted_iota(jnp.int32, (tok, tok), 1)
    upper = (rows <= columns).astype(F32)
    return jnp.dot(decay_t, upper, precision=lax.Precision.HIGHEST, preferred_element_type=F32)


def dot_t(a, b):
    return lax.dot_general(a, b, (((1,), (1,)), ((), ())), preferred_element_type=F32)


def dot(a, b):
    return jnp.dot(a, b, preferred_element_type=F32)


def load_body(me_ref, docs_hbm, k_hbm, v_hbm, a_hbm, kh_ref, vh_ref, rise_ref, flags_ref, docs, kb, vb, ab, kw, vw, sems):
    heads, tok, _ = kh_ref.shape
    copies = [
        pltpu.make_async_copy(src, dst, sems.at[i])
        for i, (src, dst) in enumerate(((docs_hbm, docs), (a_hbm, ab), (k_hbm, kb), (v_hbm, vb)))
    ]
    for copy in copies:
        copy.start()
    copies[0].wait()
    here = me_ref[0]
    doc = doc_at(docs, here * tok)
    keep = doc == doc_at(docs, (here + 1) * tok)
    flags_ref[0:1] = jnp.full((1, 128), jnp.where(keep, 1.0, 0.0), F32)
    for step in range(1, flags_ref.shape[0]):
        seen = (here >= step) & (doc_at(docs, (here - step) * tok) == doc)
        flags_ref[step : step + 1] = jnp.full((1, 128), jnp.where(seen, 0.0, MASKED), F32)
    copies[1].wait()
    rise_ref[...] = rise_of(ab[...])
    for copy, narrow, wide, out in ((copies[2], kb, kw, kh_ref), (copies[3], vb, vw, vh_ref)):
        copy.wait()
        wide[...] = narrow[...].astype(F32)
        for h in range(heads):
            out[h] = wide[pl.ds(h, tok, stride=heads), :].astype(BF16)


def state_body(flags_ref, rise_ref, kh_ref, vh_ref, *rest):
    later = (len(rest) - 4) // 2
    fetched, (state_ref, send_ref, factor_ref), placed = (rest[:later], rest[later : later + 3], rest[later + 3 : -1])
    copies = [
        pltpu.make_async_copy(src, dst, rest[-1].at[i])
        for i, (src, dst) in enumerate(zip(fetched, placed))
    ]
    for copy in copies:
        copy.start()
    heads, tok, _ = kh_ref.shape
    keep = flags_ref[0:1, :]
    rise = rise_ref[...]
    last = rise[:, tok - 1 : tok]
    factor_ref[...] = jnp.broadcast_to(jnp.exp(last), factor_ref.shape) * keep
    fade = jnp.exp(last - rise)
    for h in range(heads):
        tail_t = (jnp.transpose(kh_ref[h].astype(F32)) * fade[h : h + 1, :]).astype(BF16)
        state = dot(tail_t, vh_ref[h]) * keep
        state_ref[h] = state
        send_ref[h] = state.astype(BF16)
    for copy in copies:
        copy.wait()


def intra_body(q_ref, kh_ref, vh_ref, rise_ref, intra_ref, qh_ref, lift_ref, qw):
    heads, tok, dim = kh_ref.shape
    rise_t = rise_ref[...] * LOG2E
    rise = jnp.transpose(rise_t)
    qw[...] = q_ref[...].astype(F32)
    half = tok // 2
    lower = lax.broadcasted_iota(jnp.int32, (half, half), 0) >= lax.broadcasted_iota(
        jnp.int32, (half, half), 1
    )
    for h in range(heads):
        query = qw[pl.ds(h, tok, stride=heads), :].astype(BF16)
        qh_ref[h] = query
        key, value = (kh_ref[h], vh_ref[h])
        column = jnp.broadcast_to(rise[:, h : h + 1], (tok, dim))
        lift_ref[h] = jnp.exp2(column)
        row = rise_t[h : h + 1, :]
        for part in range(2):
            low, high = (part * half, (part + 1) * half)
            scores = dot_t(query[low:high], key[:high])
            side = column[low:high, :half]
            end = jnp.exp2(jnp.where(lower, side - row[:, low:high], MASKED))
            fade = jnp.concatenate([jnp.exp2(side - row[:, :low]), end], axis=1) if part else end
            intra_ref[h, low:high] = dot((scores * fade).astype(BF16), value[:high])


def put_out(wide, narrow, out_hbm, sem, part, parts):
    rows = wide.shape[0] // parts
    here = pl.ds(part * rows, rows)
    narrow[here] = wide[here].astype(BF16)
    copy = pltpu.make_async_copy(narrow.at[here], out_hbm.at[here], sem.at[part])
    copy.start()
    return copy


PARTS = 4


def finish_lin_body(intra_ref, qh_ref, lift_ref, before_ref, arrived_ref, out_ref, wide, narrow, sem):
    heads, tok, dim = qh_ref.shape
    ones = jnp.full((dim, dim), 1.0, BF16)
    size = tok // PARTS
    copies = []
    for part in range(PARTS):
        rows = pl.ds(part * size, size)
        for h in range(heads):
            inter = dot(qh_ref[h, rows], before_ref[h] + arrived_ref[h])
            total = intra_ref[h, rows] + lift_ref[h, rows] * inter
            mean = dot((total * total).astype(BF16), ones) * (1.0 / dim)
            wide[pl.ds(part * size * heads + h, size, stride=heads), :] = total * lax.rsqrt(
                mean + 1e-06
            )
        copies.append(put_out(wide, narrow, out_ref, sem, part, PARTS))
    for copy in copies:
        copy.wait()


def keys_of(ref, wide, count, g):
    keys = ref.shape[0] // count
    if count == 1:
        return ref[...]
    if g == 0:
        wide[...] = ref[...].astype(F32)
    return wide[pl.ds(g, keys, stride=count), :].astype(BF16)


def first_tile_body(kv_heads, heads, q_ref, k_ref, v_ref, qh_ref, top_ref, acc_ref, qw, kw, vw):
    tok = q_ref.shape[0] // heads
    power = LOG2E / math.sqrt(q_ref.shape[1])
    half = tok // 2
    lower = lax.broadcasted_iota(jnp.int32, (half, half), 0) >= lax.broadcasted_iota(
        jnp.int32, (half, half), 1
    )
    qw[...] = q_ref[...].astype(F32)
    ones = jnp.ones((tok, 128), BF16)
    for g in range(kv_heads):
        key = keys_of(k_ref, kw, kv_heads, g)
        value = jnp.concatenate([keys_of(v_ref, vw, kv_heads, g), ones], axis=1)
        for h in range(g * heads // kv_heads, (g + 1) * heads // kv_heads):
            query = qw[pl.ds(h, tok, stride=heads), :].astype(BF16)
            qh_ref[h] = query
            for part in range(2):
                low, high = (part * half, (part + 1) * half)
                scores = dot_t(query[low:high], key[:high])
                end = jnp.where(lower, scores[:, low:], MASKED)
                scores = jnp.concatenate([scores[:, :low], end], axis=1) if part else end
                top = jnp.max(scores, axis=-1, keepdims=True)
                weights = jnp.exp2((scores - top) * power).astype(BF16)
                top_ref[h, low:high] = jnp.broadcast_to(top, (half, 128))
                acc_ref[h, low:high] = dot(weights, value[:high])


def next_tile_body(
    kv_heads, step, last, flags_ref, qh_ref, k_ref, v_ref, top_ref, acc_ref, *rest
):
    heads, tok, dim = qh_ref.shape
    kw, vw = rest[-2:]
    power = LOG2E / math.sqrt(dim)
    bias = flags_ref[step : step + 1, :]
    parts = PARTS if last else 2
    size = tok // parts
    ones = jnp.ones((tok, 128), BF16)
    sides = []
    for g in range(kv_heads):
        value = jnp.concatenate([keys_of(v_ref, vw, kv_heads, g), ones], axis=1)
        sides.append((keys_of(k_ref, kw, kv_heads, g), value))
    copies = []
    for part in range(parts):
        rows = pl.ds(part * size, size)
        for h in range(heads):
            key, value = sides[h * kv_heads // heads]
            scores = dot_t(qh_ref[h, rows], key)
            old = top_ref[h, rows]
            top = jnp.max(scores, axis=-1, keepdims=True) + bias
            new = jnp.maximum(old, top)
            shift = jnp.tile(new - bias, (1, tok // 128))
            weights = jnp.exp2((scores - shift) * power).astype(BF16)
            shrink = jnp.exp2((old - new) * power)
            both = dot(weights, value)
            acc = acc_ref[h, rows, :dim] * shrink + both[:, :dim]
            summed = acc_ref[h, rows, dim:] * shrink + both[:, dim:]
            if last:
                rest[1][pl.ds(part * size * heads + h, size, stride=heads), :] = acc / summed
            else:
                rest[0][h, rows] = new
                rest[1][h, rows, :dim] = acc
                rest[1][h, rows, dim:] = summed
        if last:
            copies.append(put_out(rest[1], rest[2], rest[0], rest[3], part, parts))
    for copy in copies:
        copy.wait()


def on_device(q_lin, k_lin, v_lin, decay_log, q_soft, k_soft, v_soft, doc_starts):
    tok, heads, dim = q_lin.shape
    soft_heads, kv_heads = (q_soft.shape[1], k_soft.shape[1])
    ranks = lax.axis_size("ctx")
    me = lax.axis_index("ctx")[None]
    flat = lambda x: x.reshape(-1, dim)
    q_lin, k_lin, v_lin, q_soft, k_soft, v_soft = map(
        flat, (q_lin, k_lin, v_lin, q_soft, k_soft, v_soft)
    )
    decay_t = decay_log.T
    wide_lin = pltpu.VMEM(q_lin.shape, F32)
    wide_q = pltpu.VMEM(q_soft.shape, F32)
    wide_k = pltpu.VMEM(k_soft.shape, F32)
    flat_lin = pltpu.VMEM(q_lin.shape, BF16)
    per_head = shaped((heads, tok, dim), BF16)

    k_heads, v_heads, rise, flags = call(
        load_body,
        (
            per_head,
            per_head,
            shaped((heads, tok), F32),
            shaped((ranks, 128), F32),
        ),
        ((me, SMEM), (doc_starts, HBM), (k_lin, HBM), (v_lin, HBM), (decay_t, HBM)),
        (
            pltpu.SMEM(doc_starts.shape, jnp.int32),
            flat_lin,
            flat_lin,
            pltpu.VMEM((heads, tok), F32),
            wide_lin,
            wide_lin,
            DMA((4,)),
        ),
    )
    fetched = (q_lin, q_soft, k_soft, v_soft)
    state, send, factor, q_lin_here, q_here, k_here, v_here = call(
        state_body,
        (shaped((heads, dim, dim), F32), shaped((heads, dim, dim), BF16), shaped((heads, 128), F32))
        + tuple(shaped(x.shape, x.dtype) for x in fetched),
        ((flags, VMEM), (rise, VMEM), (k_heads, VMEM), (v_heads, VMEM))
        + tuple((x, HBM) for x in fetched),
        (DMA((4,)),),
        flops=2 * heads * tok * dim * dim,
    )

    tile_flops = 6 * soft_heads * tok * tok * dim
    stat_shapes = (shaped((soft_heads, tok, 128), F32), shaped((soft_heads, tok, 2 * dim), F32))
    soft_query, *stats = call(
        functools.partial(first_tile_body, kv_heads, soft_heads),
        (shaped((soft_heads, tok, dim), BF16),) + stat_shapes,
        ((q_here, VMEM), (k_here, VMEM), (v_here, VMEM)),
        (wide_q, wide_k, wide_k),
        flops=tile_flops,
    )
    keys, values = k_soft, v_soft
    for step in range(1, ranks - 1):
        pairs = [(i, i + 1) for i in range(step - 1, ranks - 2)]
        keys = lax.ppermute(keys, "ctx", pairs)
        values = lax.ppermute(values, "ctx", pairs)
        last = step == ranks - 2
        stats = call(
            functools.partial(next_tile_body, kv_heads, step, last),
            (shaped(q_soft.shape, BF16),) if last else stat_shapes,
            ((flags, VMEM), (soft_query, VMEM), (keys, VMEM), (values, VMEM))
            + tuple((x, VMEM) for x in stats),
            ((wide_q, pltpu.VMEM(q_soft.shape, BF16), DMA((PARTS,))) if last else ())
            + (wide_k, wide_k),
            flops=tile_flops,
            out_spec=HBM if last else VMEM,
        )
    soft_out = stats[0].reshape(tok, soft_heads, dim)

    before = jnp.zeros((heads, dim, dim), BF16)
    arrived = None
    for step in range(1, ranks - 1):
        if arrived is not None:
            before = before + arrived
            send = (factor[:, None, :] * arrived.astype(F32) + state).astype(BF16)
        arrived = lax.ppermute(send, "ctx", [(step - 1, step)])

    intra, lin_query, lift = call(
        intra_body,
        (shaped((heads, tok, dim), F32), per_head, shaped((heads, tok, dim), F32)),
        ((q_lin_here, VMEM), (k_heads, VMEM), (v_heads, VMEM), (rise, VMEM)),
        (wide_lin,),
        flops=4 * heads * tok * tok * dim,
    )
    (lin_out,) = call(
        finish_lin_body,
        (shaped(q_lin.shape, BF16),),
        ((intra, VMEM), (lin_query, VMEM), (lift, VMEM), (before, VMEM), (arrived, VMEM)),
        (wide_lin, flat_lin, DMA((PARTS,))),
        flops=2 * heads * tok * dim * dim,
        out_spec=HBM,
    )
    return (lin_out.reshape(tok, heads, dim), soft_out)


def solution(mesh):
    wide = P(("group", "ctx"), ("head", "sub"), None)

    return jax.shard_map(
        on_device,
        mesh=mesh,
        in_specs=(wide, wide, wide, P(("group", "ctx"), ("head", "sub")), wide, wide, wide, P("group")),
        out_specs=(wide, wide),
        check_vma=False,
    )
```

time: 33.2 us -> 31 us (0.934)
  the two profiles are of different devices: /device:TPU:22 before, /device:TPU:16 now
where the time goes in v3:
time: 31 us; the launch traced here: 30.7 us
  waiting for transfers between devices  11.4 us (37%)
  Pallas kernels  11.3 us (36%)
  starting transfers between devices  7.11 us (23%)
  between operations  0.77 us (2%)
    pallas_call x7, Pallas kernels, call(): pl.pallas_call(body, out_shape=tuple(outs), in_specs=[spec for _, spec in...  11.3 us
    ppermute x2, waiting for transfers between devices, on_device(): keys = lax.ppermute(keys, 'ctx', pairs)  9.33 us
    ppermute x2, starting transfers between devices, on_device(): keys = lax.ppermute(keys, 'ctx', pairs)  2.57 us
    ppermute x2, starting transfers between devices, on_device(): values = lax.ppermute(values, 'ctx', pairs)  2.57 us
    ppermute x2, waiting for transfers between devices, on_device(): values = lax.ppermute(values, 'ctx', pairs)  2.06 us
    ppermute x2, starting transfers between devices, on_device(): arrived = lax.ppermute(send, 'ctx', [(step - 1, step)])  1.97 us
  transfers between devices with their start and end apart: 6, of which 4 were waited for; matrix products, arithmetic and copies ran while one was open for 0% of the time, Pallas kernels for 22%

profile of v3, /device:TPU:16, one launch (start us, length us, event | category | flops | bytes accessed | tf_op | source)
XLA Modules:
  0.0 30.7 jit_solution(3509410470848787187)
XLA Ops:
  0.6 0.0 copy-start.1
  0.6 0.0 copy-start
  0.7 1.6 %shard_map.95 = (bf16[8,256,128]{2,1,0:T(8,128)(2,1)S(1)}, bf16[8,256,128]{2,1,0:T(8,128)(2,1)S(1)}, f32[8,256]{1,0:T(8,128)S(1)}, f32[4,128]{1,0:T(4,128)S(1)}) custom-call(s32[1]{0:T(128)} %bitcast.me_ref, s32[6]{0:T(128)} %docs_hbm.1, bf16[2048,128]{1,0:T(8,128)(2,1)} %bitcast.11, bf16[2048,128]{1,0:T(8,128)(2,1)} %bitcast.12, f32[8,256]{1,0:T(8,128)} %bitcast.20), custom_call_target="tpu_custom_call" | custom-call | bytes 2115612 | tf_op jit(solution)/shard_map/pallas_call | solution.py:28
  2.3 1.4 %shard_map.96 = (f32[8,128,128]{2,1,0:T(8,128)S(1)}, bf16[8,128,128]{2,1,0:T(8,128)(2,1)S(1)}, f32[8,128]{1,0:T(8,128)S(1)}, bf16[2048,128]{1,0:T(8,128)(2,1)S(1...) custom-call(f32[4,128]{1,0:T(4,128)S(1)} %get-tuple-element.21.flags_ref, ...), custom_call_target="tpu_custom_call" | custom-call | flops 67108864 | bytes 4470784 | tf_op jit(solution)/shard_map/pallas_call | solution.py:28
  3.7 0.7 %collective-permute-start = (bf16[8,128,128]{2,1,0:T(8,128)(2,1)S(1)}, bf16[8,128,128]{2,1,0:T(8,128)(2,1)S(1)}, u32[]{:S(2)}, u32[]{:S(2)}) collective-permute-start(bf16[8,128,128]{2,1,0:T(8,128)(2,1)S(1)} %get-tuple-element.29), channel_id=1, source_target_pairs={{0,4},{1,5},{2,6},{3,7},{16,20},{17,21},{18,22},{19,23}} | collective-permute-start | bytes 786440 | tf_op jit(solution)/shard_map/ppermute | solution.py:322
  4.4 0.0 copy-done
  4.4 1.3 %collective-permute-start.2 = (bf16[512,128]{1,0:T(8,128)(2,1)S(1)}, bf16[512,128]{1,0:T(8,128)(2,1)S(1)}, u32[]{:S(2)}, u32[]{:S(2)}) collective-permute-start(bf16[512,128]{1,0:T(8,128)(2,1)S(1)} %bitcast.17), channel_id=1, source_target_pairs={{0,4},{4,8},{1,5},{5,9},{2,6},{6,10},{3,7},{7,11},{16,20},{20,24},... | collective-permute-start | bytes 393224 | tf_op jit(solution)/shard_map/ppermute | solution.py:301
  5.7 0.0 copy-done.1
  5.7 1.3 %collective-permute-start.4 = (bf16[512,128]{1,0:T(8,128)(2,1)S(1)}, bf16[512,128]{1,0:T(8,128)(2,1)S(1)}, u32[]{:S(2)}, u32[]{:S(2)}) collective-permute-start(bf16[512,128]{1,0:T(8,128)(2,1)S(1)} %bitcast.19), channel_id=1, source_target_pairs={{0,4},{4,8},{1,5},{5,9},{2,6},{6,10},{3,7},{7,11},{16,20},{20,24},... | collective-permute-start | bytes 393224 | tf_op jit(solution)/shard_map/ppermute | solution.py:302
  7.0 0.0 collective-permute-done.before_ref
  7.0 0.1 add_convert_fusion
  7.1 1.3 %collective-permute-start.1 = (bf16[8,128,128]{2,1,0:T(8,128)(2,1)S(1)}, bf16[8,128,128]{2,1,0:T(8,128)(2,1)S(1)}, u32[]{:S(2)}, u32[]{:S(2)}) collective-permute-start(bf16[8,128,128]{2,1,0:T(8,128)(2,1)S(1)} %add_convert_fusion), channel_id=1, source_target_pairs={{4,8},{5,9},{6,10},{7,11},{20,24},{21,25},{22,26},{23,27}} | collective-permute-start | bytes 786440 | tf_op jit(solution)/shard_map/ppermute | solution.py:322
  8.4 4.0 %collective-permute-done.2.k_ref = bf16[512,128]{1,0:T(8,128)(2,1)S(1)} collective-permute-done((bf16[512,128]{1,0:T(8,128)(2,1)S(1)}, bf16[512,128]{1,0:T(8,128)(2,1)S(1)}, u32[]{:S(2)}, u32[]{:S(2)}) %collective-permute-start.2) | collective-permute-done | bytes 131104 | tf_op jit(solution)/shard_map/ppermute | solution.py:301
  12.4 1.3 %collective-permute-start.3 = (bf16[512,128]{1,0:T(8,128)(2,1)S(1)}, bf16[512,128]{1,0:T(8,128)(2,1)S(1)}, u32[]{:S(2)}, u32[]{:S(2)}) collective-permute-start(bf16[512,128]{1,0:T(8,128)(2,1)S(1)} %collective-permute-done.2.k_ref), channel_id=1, source_target_pairs={{4,8},{5,9},{6,10},{7,11},{20,24},{21,25},{22,26},{23,27}} | collective-permute-start | bytes 393224 | tf_op jit(solution)/shard_map/ppermute | solution.py:301
  13.7 0.7 %collective-permute-done.4.v_ref = bf16[512,128]{1,0:T(8,128)(2,1)S(1)} collective-permute-done((bf16[512,128]{1,0:T(8,128)(2,1)S(1)}, bf16[512,128]{1,0:T(8,128)(2,1)S(1)}, u32[]{:S(2)}, u32[]{:S(2)}) %collective-permute-start.4) | collective-permute-done | bytes 131104 | tf_op jit(solution)/shard_map/ppermute | solution.py:302
  14.3 1.3 %collective-permute-start.5 = (bf16[512,128]{1,0:T(8,128)(2,1)S(1)}, bf16[512,128]{1,0:T(8,128)(2,1)S(1)}, u32[]{:S(2)}, u32[]{:S(2)}) collective-permute-start(bf16[512,128]{1,0:T(8,128)(2,1)S(1)} %collective-permute-done.4.v_ref), channel_id=1, source_target_pairs={{4,8},{5,9},{6,10},{7,11},{20,24},{21,25},{22,26},{23,27}} | collective-permute-start | bytes 393224 | tf_op jit(solution)/shard_map/ppermute | solution.py:302
  15.6 1.9 %shard_map.97 = (f32[8,256,128]{2,1,0:T(8,128)S(1)}, bf16[8,256,128]{2,1,0:T(8,128)(2,1)S(1)}, f32[8,256,128]{2,1,0:T(8,128)S(1)}) custom-call(bf16[2048,128]{1,0:T(8,128)(2,1)S(1)} %get-tuple-element.25.q_ref, bf16[8,256,128]{2,1,0:T(8,128)(2,1)S(1)} %get-tuple-element.23.kh_ref, bf16[8,256,128]{2,1,0:T(8,128)(2,1)S(1)} %get-tuple-element.24.vh_ref, ...), custom_call_target="tpu_custom_call" | custom-call | flops 268435456 | bytes 4202496 | tf_op jit(solution)/shard_map/pallas_call | solution.py:28
  17.5 1.2 %shard_map.99 = (bf16[8,256,128]{2,1,0:T(8,128)(2,1)S(1)}, f32[8,256,128]{2,1,0:T(8,128)S(1)}, f32[8,256,256]{2,1,0:T(8,128)S(1)}) custom-call(bf16[2048,128]{1,0:T(8,128)(2,1)S(1)} %get-tuple-element.32.q_ref, bf16[512,128]{1,0:T(8,128)(2,1)S(1)} %get-tuple-element.33.k_ref, bf16[512,128]{1,0:T(8,128)(2,1)S(1)} %get-tuple-element.34.v_ref), custom_call_target="tpu_custom_call" | custom-call | flops 402653184 | bytes 4456448 | tf_op jit(solution)/shard_map/pallas_call | solution.py:28
  18.6 1.1 %shard_map.100 = (f32[8,256,128]{2,1,0:T(8,128)S(1)}, f32[8,256,256]{2,1,0:T(8,128)S(1)}) custom-call(f32[4,128]{1,0:T(4,128)S(1)} %get-tuple-element.21.flags_ref, bf16[8,256,128]{2,1,0:T(8,128)(2,1)S(1)} %get-tuple-element.35.qh_ref, bf16[512,128]{1,0:T(8,128)(2,1)S(1)} %collective-permute-done.2.k_ref, bf16[512,128]{1,0:T(8,128)(2,1)S(1)} %collective-permute-done.4.v_ref, ...), custom_call_target="tpu_custom_call" | custom-call | flops 402653184 | bytes 7079936 | tf_op jit(solution)/shard_map/pallas_call | solution.py:28
  19.7 5.3 %collective-permute-done.3.k_ref = bf16[512,128]{1,0:T(8,128)(2,1)S(1)} collective-permute-done((bf16[512,128]{1,0:T(8,128)(2,1)S(1)}, bf16[512,128]{1,0:T(8,128)(2,1)S(1)}, u32[]{:S(2)}, u32[]{:S(2)}) %collective-permute-start.3) | collective-permute-done | bytes 131104 | tf_op jit(solution)/shard_map/ppermute | solution.py:301
  25.1 1.4 %collective-permute-done.5.v_ref = bf16[512,128]{1,0:T(8,128)(2,1)S(1)} collective-permute-done((bf16[512,128]{1,0:T(8,128)(2,1)S(1)}, bf16[512,128]{1,0:T(8,128)(2,1)S(1)}, u32[]{:S(2)}, u32[]{:S(2)}) %collective-permute-start.5) | collective-permute-done | bytes 131104 | tf_op jit(solution)/shard_map/ppermute | solution.py:302
  26.5 2.6 %shard_map.101 = bf16[2048,128]{1,0:T(8,128)(2,1)} custom-call(f32[4,128]{1,0:T(4,128)S(1)} %get-tuple-element.21.flags_ref, bf16[8,256,128]{2,1,0:T(8,128)(2,1)S(1)} %get-tuple-element.35.qh_ref, bf16[512,128]{1,0:T(8,128)(2,1)S(1)} %collective-permute-done.3.k_ref, bf16[512,128]{1,0:T(8,128)(2,1)S(1)} %collective-permute-done.5.v_ref, ...), custom_call_target="tpu_custom_call" | custom-call | flops 402653184 | bytes 4458496 | tf_op jit(solution)/shard_map/pallas_call | solution.py:28
  29.1 0.0 collective-permute-done.1.arrived_ref
  29.1 1.6 %shard_map.98 = bf16[2048,128]{1,0:T(8,128)(2,1)} custom-call(f32[8,256,128]{2,1,0:T(8,128)S(1)} %get-tuple-element.26.intra_ref, bf16[8,256,128]{2,1,0:T(8,128)(2,1)S(1)} %get-tuple-element.27.qh_ref, f32[8,256,128]{2,1,0:T(8,128)S(1)} %get-tuple-element.28.lift_ref, bf16[8,128,128]{2,1,0:T(8,128)(2,1)S(1)} %collective-permute-done.before_ref, ...), custom_call_target="tpu_custom_call" | custom-call | flops 67108864 | bytes 3670016 | tf_op jit(solution)/shard_map/pallas_call | solution.py:28
Async XLA Ops:
  0.6 5.0 %copy-start.1 = (bf16[256,2,128]{2,1,0:T(2,128)(2,1)S(1)}, bf16[256,2,128]{2,1,0:T(2,128)(2,1)}, u32[]{:S(2)}) copy-start(bf16[256,2,128]{2,1,0:T(2,128)(2,1)} %param.14) | copy-start | bytes 393220
  0.6 3.7 %copy-start = (bf16[256,2,128]{2,1,0:T(2,128)(2,1)S(1)}, bf16[256,2,128]{2,1,0:T(2,128)(2,1)}, u32[]{:S(2)}) copy-start(bf16[256,2,128]{2,1,0:T(2,128)(2,1)} %param.13) | copy-start | bytes 393220
  3.7 3.3 %collective-permute-start = (bf16[8,128,128]{2,1,0:T(8,128)(2,1)S(1)}, bf16[8,128,128]{2,1,0:T(8,128)(2,1)S(1)}, u32[]{:S(2)}, u32[]{:S(2)}) collective-permute-start(bf16[8,128,128]{2,1,0:T(8,128)(2,1)S(1)} %get-tuple-element.29), channel_id=1, source_target_pairs={{0,4},{1,5},{2,6},{3,7},{16,20},{17,21},{18,22},{19,23}} | collective-permute-start | bytes 786440 | tf_op jit(solution)/shard_map/ppermute | solution.py:322
  4.4 8.0 %collective-permute-start.2 = (bf16[512,128]{1,0:T(8,128)(2,1)S(1)}, bf16[512,128]{1,0:T(8,128)(2,1)S(1)}, u32[]{:S(2)}, u32[]{:S(2)}) collective-permute-start(bf16[512,128]{1,0:T(8,128)(2,1)S(1)} %bitcast.17), channel_id=1, source_target_pairs={{0,4},{4,8},{1,5},{5,9},{2,6},{6,10},{3,7},{7,11},{16,20},{20,24},... | collective-permute-start | bytes 393224 | tf_op jit(solution)/shard_map/ppermute | solution.py:301
  5.7 8.6 %collective-permute-start.4 = (bf16[512,128]{1,0:T(8,128)(2,1)S(1)}, bf16[512,128]{1,0:T(8,128)(2,1)S(1)}, u32[]{:S(2)}, u32[]{:S(2)}) collective-permute-start(bf16[512,128]{1,0:T(8,128)(2,1)S(1)} %bitcast.19), channel_id=1, source_target_pairs={{0,4},{4,8},{1,5},{5,9},{2,6},{6,10},{3,7},{7,11},{16,20},{20,24},... | collective-permute-start | bytes 393224 | tf_op jit(solution)/shard_map/ppermute | solution.py:302
  7.1 22.0 %collective-permute-start.1 = (bf16[8,128,128]{2,1,0:T(8,128)(2,1)S(1)}, bf16[8,128,128]{2,1,0:T(8,128)(2,1)S(1)}, u32[]{:S(2)}, u32[]{:S(2)}) collective-permute-start(bf16[8,128,128]{2,1,0:T(8,128)(2,1)S(1)} %add_convert_fusion), channel_id=1, source_target_pairs={{4,8},{5,9},{6,10},{7,11},{20,24},{21,25},{22,26},{23,27}} | collective-permute-start | bytes 786440 | tf_op jit(solution)/shard_map/ppermute | solution.py:322
  12.4 12.7 %collective-permute-start.3 = (bf16[512,128]{1,0:T(8,128)(2,1)S(1)}, bf16[512,128]{1,0:T(8,128)(2,1)S(1)}, u32[]{:S(2)}, u32[]{:S(2)}) collective-permute-start(bf16[512,128]{1,0:T(8,128)(2,1)S(1)} %collective-permute-done.2.k_ref), channel_id=1, source_target_pairs={{4,8},{5,9},{6,10},{7,11},{20,24},{21,25},{22,26},{23,27}} | collective-permute-start | bytes 393224 | tf_op jit(solution)/shard_map/ppermute | solution.py:301
  14.3 12.2 %collective-permute-start.5 = (bf16[512,128]{1,0:T(8,128)(2,1)S(1)}, bf16[512,128]{1,0:T(8,128)(2,1)S(1)}, u32[]{:S(2)}, u32[]{:S(2)}) collective-permute-start(bf16[512,128]{1,0:T(8,128)(2,1)S(1)} %collective-permute-done.4.v_ref), channel_id=1, source_target_pairs={{4,8},{5,9},{6,10},{7,11},{20,24},{21,25},{22,26},{23,27}} | collective-permute-start | bytes 393224 | tf_op jit(solution)/shard_map/ppermute | solution.py:302

commit v4 on v3

--- a/solution.py
+++ b/solution.py
@@ -17,6 +17,7 @@
 SMEM = pl.BlockSpec(memory_space=pltpu.SMEM)
 HBM = pl.BlockSpec(memory_space=pltpu.HBM)
 DMA = pltpu.SemaphoreType.DMA
+HALVES = 2
 
 
 def shaped(shape, dtype):
@@ -84,26 +85,33 @@
             out[h] = wide[pl.ds(h, tok, stride=heads), :].astype(BF16)
 
 
-def state_body(flags_ref, rise_ref, kh_ref, vh_ref, *rest):
-    later = (len(rest) - 4) // 2
-    fetched, (state_ref, send_ref, factor_ref), placed = (rest[:later], rest[later : later + 3], rest[later + 3 : -1])
+def state_body(flags_ref, rise_ref, kh_ref, vh_ref, *outs):
+    heads, tok, _ = kh_ref.shape
+    states, sends, factors = (outs[:HALVES], outs[HALVES : 2 * HALVES], outs[2 * HALVES :])
+    keep = flags_ref[0:1, :]
+    rise = rise_ref[...]
+    last = rise[:, tok - 1 : tok]
+    factor = jnp.broadcast_to(jnp.exp(last), (heads, 128)) * keep
+    fade = jnp.exp(last - rise)
+    size = heads // HALVES
+    for half in range(HALVES):
+        factors[half][...] = factor[half * size : (half + 1) * size]
+        for i in range(size):
+            h = half * size + i
+            tail_t = (jnp.transpose(kh_ref[h].astype(F32)) * fade[h : h + 1, :]).astype(BF16)
+            state = dot(tail_t, vh_ref[h]) * keep
+            states[half][i] = state
+            sends[half][i] = state.astype(BF16)
+
+
+def fetch_body(*refs):
+    count = len(refs) // 2
     copies = [
-        pltpu.make_async_copy(src, dst, rest[-1].at[i])
-        for i, (src, dst) in enumerate(zip(fetched, placed))
+        pltpu.make_async_copy(src, dst, refs[-1].at[i])
+        for i, (src, dst) in enumerate(zip(refs[:count], refs[count:-1]))
     ]
     for copy in copies:
         copy.start()
-    heads, tok, _ = kh_ref.shape
-    keep = flags_ref[0:1, :]
-    rise = rise_ref[...]
-    last = rise[:, tok - 1 : tok]
-    factor_ref[...] = jnp.broadcast_to(jnp.exp(last), factor_ref.shape) * keep
-    fade = jnp.exp(last - rise)
-    for h in range(heads):
-        tail_t = (jnp.transpose(kh_ref[h].astype(F32)) * fade[h : h + 1, :]).astype(BF16)
-        state = dot(tail_t, vh_ref[h]) * keep
-        state_ref[h] = state
-        send_ref[h] = state.astype(BF16)
     for copy in copies:
         copy.wait()
 
@@ -145,15 +153,22 @@
 PARTS = 4
 
 
-def finish_lin_body(intra_ref, qh_ref, lift_ref, before_ref, arrived_ref, out_ref, wide, narrow, sem):
+def finish_lin_body(intra_ref, qh_ref, lift_ref, *rest):
+    befores, arriveds = (rest[:HALVES], rest[HALVES : 2 * HALVES])
+    out_ref, wide, narrow, sem = rest[2 * HALVES :]
     heads, tok, dim = qh_ref.shape
+    states = [
+        before[i] + arrived[i]
+        for before, arrived in zip(befores, arriveds)
+        for i in range(heads // HALVES)
+    ]
     ones = jnp.full((dim, dim), 1.0, BF16)
     size = tok // PARTS
     copies = []
     for part in range(PARTS):
         rows = pl.ds(part * size, size)
         for h in range(heads):
-            inter = dot(qh_ref[h, rows], before_ref[h] + arrived_ref[h])
+            inter = dot(qh_ref[h, rows], states[h])
             total = intra_ref[h, rows] + lift_ref[h, rows] * inter
             mean = dot((total * total).astype(BF16), ones) * (1.0 / dim)
             wide[pl.ds(part * size * heads + h, size, stride=heads), :] = total * lax.rsqrt(
@@ -200,44 +215,65 @@
 
 
 def next_tile_body(
-    kv_heads, step, last, flags_ref, qh_ref, k_ref, v_ref, top_ref, acc_ref, *rest
+    kv_heads, step, last, me_ref, flags_ref, qh_ref, k_ref, v_ref, top_ref, acc_ref, *rest
 ):
     heads, tok, dim = qh_ref.shape
     kw, vw = rest[-2:]
     power = LOG2E / math.sqrt(dim)
-    bias = flags_ref[step : step + 1, :]
     parts = PARTS if last else 2
     size = tok // parts
-    ones = jnp.ones((tok, 128), BF16)
-    sides = []
-    for g in range(kv_heads):
-        value = jnp.concatenate([keys_of(v_ref, vw, kv_heads, g), ones], axis=1)
-        sides.append((keys_of(k_ref, kw, kv_heads, g), value))
-    copies = []
-    for part in range(parts):
-        rows = pl.ds(part * size, size)
-        for h in range(heads):
-            key, value = sides[h * kv_heads // heads]
-            scores = dot_t(qh_ref[h, rows], key)
-            old = top_ref[h, rows]
-            top = jnp.max(scores, axis=-1, keepdims=True) + bias
-            new = jnp.maximum(old, top)
-            shift = jnp.tile(new - bias, (1, tok // 128))
-            weights = jnp.exp2((scores - shift) * power).astype(BF16)
-            shrink = jnp.exp2((old - new) * power)
-            both = dot(weights, value)
-            acc = acc_ref[h, rows, :dim] * shrink + both[:, :dim]
-            summed = acc_ref[h, rows, dim:] * shrink + both[:, dim:]
+
+    def put(part, h, acc, summed):
+        rest[1][pl.ds(part * size * heads + h, size, stride=heads), :] = acc / summed
+
+    @pl.when(me_ref[0] >= step)
+    def _():
+        bias = flags_ref[step : step + 1, :]
+        ones = jnp.ones((tok, 128), BF16)
+        sides = []
+        for g in range(kv_heads):
+            value = jnp.concatenate([keys_of(v_ref, vw, kv_heads, g), ones], axis=1)
+            sides.append((keys_of(k_ref, kw, kv_heads, g), value))
+        copies = []
+        for part in range(parts):
+            rows = pl.ds(part * size, size)
+            for h in range(heads):
+                key, value = sides[h * kv_heads // heads]
+                scores = dot_t(qh_ref[h, rows], key)
+                old = top_ref[h, rows]
+                top = jnp.max(scores, axis=-1, keepdims=True) + bias
+                new = jnp.maximum(old, top)
+                shift = jnp.tile(new - bias, (1, tok // 128))
+                weights = jnp.exp2((scores - shift) * power).astype(BF16)
+                shrink = jnp.exp2((old - new) * power)
+                both = dot(weights, value)
+                acc = acc_ref[h, rows, :dim] * shrink + both[:, :dim]
+                summed = acc_ref[h, rows, dim:] * shrink + both[:, dim:]
+                if last:
+                    put(part, h, acc, summed)
+                else:
+                    rest[0][h, rows] = new
+                    rest[1][h, rows, :dim] = acc
+                    rest[1][h, rows, dim:] = summed
             if last:
-                rest[1][pl.ds(part * size * heads + h, size, stride=heads), :] = acc / summed
-            else:
-                rest[0][h, rows] = new
-                rest[1][h, rows, :dim] = acc
-                rest[1][h, rows, dim:] = summed
+                copies.append(put_out(rest[1], rest[2], rest[0], rest[3], part, parts))
+        for copy in copies:
+            copy.wait()
+
+    @pl.when(me_ref[0] < step)
+    def _():
         if last:
-            copies.append(put_out(rest[1], rest[2], rest[0], rest[3], part, parts))
-    for copy in copies:
-        copy.wait()
+            copies = []
+            for part in range(parts):
+                rows = pl.ds(part * size, size)
+                for h in range(heads):
+                    put(part, h, acc_ref[h, rows, :dim], acc_ref[h, rows, dim:])
+                copies.append(put_out(rest[1], rest[2], rest[0], rest[3], part, parts))
+            for copy in copies:
+                copy.wait()
+        else:
+            rest[0][...] = top_ref[...]
+            rest[1][...] = acc_ref[...]
 
 
 def on_device(q_lin, k_lin, v_lin, decay_log, q_soft, k_soft, v_soft, doc_starts):
@@ -275,15 +311,22 @@
             DMA((4,)),
         ),
     )
+    part = heads // HALVES
+    outs = call(
+        state_body,
+        (shaped((part, dim, dim), F32),) * HALVES
+        + (shaped((part, dim, dim), BF16),) * HALVES
+        + (shaped((part, 128), F32),) * HALVES,
+        ((flags, VMEM), (rise, VMEM), (k_heads, VMEM), (v_heads, VMEM)),
+        flops=2 * heads * tok * dim * dim,
+    )
+    states, sends, factors = (outs[:HALVES], list(outs[HALVES : 2 * HALVES]), outs[2 * HALVES :])
     fetched = (q_lin, q_soft, k_soft, v_soft)
-    state, send, factor, q_lin_here, q_here, k_here, v_here = call(
-        state_body,
-        (shaped((heads, dim, dim), F32), shaped((heads, dim, dim), BF16), shaped((heads, 128), F32))
-        + tuple(shaped(x.shape, x.dtype) for x in fetched),
-        ((flags, VMEM), (rise, VMEM), (k_heads, VMEM), (v_heads, VMEM))
-        + tuple((x, HBM) for x in fetched),
-        (DMA((4,)),),
-        flops=2 * heads * tok * dim * dim,
+    q_lin_here, q_here, k_here, v_here = call(
+        fetch_body,
+        tuple(shaped(x.shape, x.dtype) for x in fetched),
+        tuple((x, HBM) for x in fetched),
+        (DMA((len(fetched),)),),
     )
 
     tile_flops = 6 * soft_heads * tok * tok * dim
@@ -304,7 +347,7 @@
         stats = call(
             functools.partial(next_tile_body, kv_heads, step, last),
             (shaped(q_soft.shape, BF16),) if last else stat_shapes,
-            ((flags, VMEM), (soft_query, VMEM), (keys, VMEM), (values, VMEM))
+            ((me, SMEM), (flags, VMEM), (soft_query, VMEM), (keys, VMEM), (values, VMEM))
             + tuple((x, VMEM) for x in stats),
             ((wide_q, pltpu.VMEM(q_soft.shape, BF16), DMA((PARTS,))) if last else ())
             + (wide_k, wide_k),
@@ -313,13 +356,15 @@
         )
     soft_out = stats[0].reshape(tok, soft_heads, dim)
 
-    before = jnp.zeros((heads, dim, dim), BF16)
-    arrived = None
+    befores = [jnp.zeros((part, dim, dim), BF16) for _ in range(HALVES)]
+    arrived = [None] * HALVES
     for step in range(1, ranks - 1):
-        if arrived is not None:
-            before = before + arrived
-            send = (factor[:, None, :] * arrived.astype(F32) + state).astype(BF16)
-        arrived = lax.ppermute(send, "ctx", [(step - 1, step)])
+        for half in range(HALVES):
+            if step > 1:
+                befores[half] = befores[half] + arrived[half]
+                moved = factors[half][:, None, :] * arrived[half].astype(F32)
+                sends[half] = (moved + states[half]).astype(BF16)
+            arrived[half] = lax.ppermute(sends[half], "ctx", [(step - 1, step)])
 
     intra, lin_query, lift = call(
         intra_body,
@@ -331,7 +376,7 @@
     (lin_out,) = call(
         finish_lin_body,
         (shaped(q_lin.shape, BF16),),
-        ((intra, VMEM), (lin_query, VMEM), (lift, VMEM), (before, VMEM), (arrived, VMEM)),
+        ((intra, VMEM), (lin_query, VMEM), (lift, VMEM)) + tuple((x, VMEM) for x in befores + arrived),
         (wide_lin, flat_lin, DMA((PARTS,))),
         flops=2 * heads * tok * dim * dim,
         out_spec=HBM,

time: 31 us -> 27.6 us (0.89)
  waiting for transfers between devices: 11.4 us -> 5.77 us
  starting transfers between devices: 7.11 us -> 9.07 us
    ppermute x2, waiting for transfers between devices: 9.33 us -> 2.3 us  [on_device(): keys = lax.ppermute(keys, 'ctx', pairs)]
    ppermute x2 -> x4, starting transfers between devices: 1.97 us -> 3.92 us  [on_device(): arrived[half] = lax.ppermute(sends[half], 'ctx', [(step - 1, step)])]
    ppermute x2, waiting for transfers between devices: 2.06 us -> 3.46 us  [on_device(): values = lax.ppermute(values, 'ctx', pairs)]
    pallas_call x7 -> x8, Pallas kernels: 11.3 us -> 11.6 us  [call(): pl.pallas_call(body, out_shape=tuple(outs), in_specs=[spec for _, spec in...]
  transfers between devices with their start and end apart: 6 -> 8, of which waited for: 4 -> 4; matrix products, arithmetic and copies ran while one was open for 0% -> 0% of each run, Pallas kernels for 22% -> 29%
where the time goes in v4:
time: 27.6 us; the launch traced here: 27.3 us
  Pallas kernels  11.6 us (42%)
  starting transfers between devices  9.07 us (33%)
  waiting for transfers between devices  5.77 us (21%)
  between operations  0.82 us (3%)
    pallas_call x8, Pallas kernels, call(): pl.pallas_call(body, out_shape=tuple(outs), in_specs=[spec for _, spec in...  11.6 us
    ppermute x4, starting transfers between devices, on_device(): arrived[half] = lax.ppermute(sends[half], 'ctx', [(step - 1, step)])  3.92 us
    ppermute x2, waiting for transfers between devices, on_device(): values = lax.ppermute(values, 'ctx', pairs)  3.46 us
    ppermute x2, starting transfers between devices, on_device(): values = lax.ppermute(values, 'ctx', pairs)  2.57 us
    ppermute x2, starting transfers between devices, on_device(): keys = lax.ppermute(keys, 'ctx', pairs)  2.57 us
    ppermute x2, waiting for transfers between devices, on_device(): keys = lax.ppermute(keys, 'ctx', pairs)  2.3 us
  transfers between devices with their start and end apart: 8, of which 4 were waited for; matrix products, arithmetic and copies ran while one was open for 0% of the time, Pallas kernels for 29%

profile of v4, /device:TPU:16, one launch (start us, length us, event | category | flops | bytes accessed | tf_op | source)
XLA Modules:
  0.0 27.3 jit_solution(12680823447138398261)
XLA Ops:
  0.6 0.0 copy-start
  0.6 0.0 copy-start.1
  0.7 1.6 %shard_map.96 = (bf16[8,256,128]{2,1,0:T(8,128)(2,1)S(1)}, bf16[8,256,128]{2,1,0:T(8,128)(2,1)S(1)}, f32[8,256]{1,0:T(8,128)S(1)}, f32[4,128]{1,0:T(4,128)S(1)}) custom-call(s32[1]{0:T(128)} %bitcast.4.me_ref, s32[6]{0:T(128)} %docs_hbm.1, bf16[2048,128]{1,0:T(8,128)(2,1)} %bitcast.12, bf16[2048,128]{1,0:T(8,128)(2,1)} %bitcast.13, f32[8,256]{1,0:T(8,128)} %bitcast.20), custom_call_target="tpu_custom_call" | custom-call | bytes 2115612 | tf_op jit(solution)/shard_map/pallas_call | solution.py:29
  2.3 0.4 %shard_map.98 = (f32[4,128,128]{2,1,0:T(8,128)S(1)}, f32[4,128,128]{2,1,0:T(8,128)S(1)}, bf16[4,128,128]{2,1,0:T(8,128)(2,1)S(1)}, bf16[4,128,128]{2,1,0:T(8,128...) custom-call(f32[4,128]{1,0:T(4,128)S(1)} %get-tuple-element.31.flags_ref, ...), custom_call_target="tpu_custom_call" | custom-call | flops 67108864 | bytes 1849344 | tf_op jit(solution)/shard_map/pallas_call | solution.py:29
  2.6 0.7 %collective-permute-start = (bf16[4,128,128]{2,1,0:T(8,128)(2,1)S(1)}, bf16[4,128,128]{2,1,0:T(8,128)(2,1)S(1)}, u32[]{:S(2)}, u32[]{:S(2)}) collective-permute-start(bf16[4,128,128]{2,1,0:T(8,128)(2,1)S(1)} %get-tuple-element.32), channel_id=1, source_target_pairs={{0,4},{1,5},{2,6},{3,7},{16,20},{17,21},{18,22},{19,23}} | collective-permute-start | bytes 393224 | tf_op jit(solution)/shard_map/ppermute | solution.py:367
  3.3 0.0 copy-done
  3.3 1.3 %collective-permute-start.4 = (bf16[512,128]{1,0:T(8,128)(2,1)S(1)}, bf16[512,128]{1,0:T(8,128)(2,1)S(1)}, u32[]{:S(2)}, u32[]{:S(2)}) collective-permute-start(bf16[512,128]{1,0:T(8,128)(2,1)S(1)} %bitcast.17), channel_id=1, source_target_pairs={{0,4},{4,8},{1,5},{5,9},{2,6},{6,10},{3,7},{7,11},{16,20},{20,24},... | collective-permute-start | bytes 393224 | tf_op jit(solution)/shard_map/ppermute | solution.py:344
  4.6 0.0 copy-done.1
  4.6 1.3 %collective-permute-start.6 = (bf16[512,128]{1,0:T(8,128)(2,1)S(1)}, bf16[512,128]{1,0:T(8,128)(2,1)S(1)}, u32[]{:S(2)}, u32[]{:S(2)}) collective-permute-start(bf16[512,128]{1,0:T(8,128)(2,1)S(1)} %bitcast.19), channel_id=1, source_target_pairs={{0,4},{4,8},{1,5},{5,9},{2,6},{6,10},{3,7},{7,11},{16,20},{20,24},... | collective-permute-start | bytes 393224 | tf_op jit(solution)/shard_map/ppermute | solution.py:345
  5.9 0.7 %collective-permute-start.1 = (bf16[4,128,128]{2,1,0:T(8,128)(2,1)S(1)}, bf16[4,128,128]{2,1,0:T(8,128)(2,1)S(1)}, u32[]{:S(2)}, u32[]{:S(2)}) collective-permute-start(bf16[4,128,128]{2,1,0:T(8,128)(2,1)S(1)} %get-tuple-element.33), channel_id=1, source_target_pairs={{0,4},{1,5},{2,6},{3,7},{16,20},{17,21},{18,22},{19,23}} | collective-permute-start | bytes 393224 | tf_op jit(solution)/shard_map/ppermute | solution.py:367
  6.6 1.3 %shard_map.95 = (bf16[2048,128]{1,0:T(8,128)(2,1)S(1)}, bf16[2048,128]{1,0:T(8,128)(2,1)S(1)}, bf16[512,128]{1,0:T(8,128)(2,1)S(1)}, bf16[512,128]{1,0:T(8,128)(2,1)S(1)}) custom-call(bf16[2048,128]{1,0:T(8,128)(2,1)} %bitcast.14, bf16[2048,128]{1,0:T(8,128)(2,1)} %bitcast.15, bf16[512,128]{1,0:T(8,128)(2,1)} %bitcast.16, bf16[512,128]{1,0:T(8,128)(2,1)} %bitcast.18), custom_call_target="tpu_custom_call" | custom-call | bytes 2621440 | tf_op jit(solution)/shard_map/pallas_call | solution.py:29
  7.9 0.0 collective-permute-done.rest_0_
  8.0 1.3 %collective-permute-start.2 = (bf16[4,128,128]{2,1,0:T(8,128)(2,1)S(1)}, bf16[4,128,128]{2,1,0:T(8,128)(2,1)S(1)}, u32[]{:S(2)}, u32[]{:S(2)}) collective-permute-start(bf16[4,128,128]{2,1,0:T(8,128)(2,1)S(1)} %add_convert_fusion.1), channel_id=1, source_target_pairs={{4,8},{5,9},{6,10},{7,11},{20,24},{21,25},{22,26},{23,27}} | collective-permute-start | bytes 393224 | tf_op jit(solution)/shard_map/ppermute | solution.py:367
  9.3 2.0 %collective-permute-done.4.k_ref = bf16[512,128]{1,0:T(8,128)(2,1)S(1)} collective-permute-done((bf16[512,128]{1,0:T(8,128)(2,1)S(1)}, bf16[512,128]{1,0:T(8,128)(2,1)S(1)}, u32[]{:S(2)}, u32[]{:S(2)}) %collective-permute-start.4) | collective-permute-done | bytes 131104 | tf_op jit(solution)/shard_map/ppermute | solution.py:344
  11.3 1.3 %collective-permute-start.5 = (bf16[512,128]{1,0:T(8,128)(2,1)S(1)}, bf16[512,128]{1,0:T(8,128)(2,1)S(1)}, u32[]{:S(2)}, u32[]{:S(2)}) collective-permute-start(bf16[512,128]{1,0:T(8,128)(2,1)S(1)} %collective-permute-done.4.k_ref), channel_id=1, source_target_pairs={{4,8},{5,9},{6,10},{7,11},{20,24},{21,25},{22,26},{23,27}} | collective-permute-start | bytes 393224 | tf_op jit(solution)/shard_map/ppermute | solution.py:344
  12.6 0.7 %collective-permute-done.6.v_ref = bf16[512,128]{1,0:T(8,128)(2,1)S(1)} collective-permute-done((bf16[512,128]{1,0:T(8,128)(2,1)S(1)}, bf16[512,128]{1,0:T(8,128)(2,1)S(1)}, u32[]{:S(2)}, u32[]{:S(2)}) %collective-permute-start.6) | collective-permute-done | bytes 131104 | tf_op jit(solution)/shard_map/ppermute | solution.py:345
  13.3 1.3 %collective-permute-start.7 = (bf16[512,128]{1,0:T(8,128)(2,1)S(1)}, bf16[512,128]{1,0:T(8,128)(2,1)S(1)}, u32[]{:S(2)}, u32[]{:S(2)}) collective-permute-start(bf16[512,128]{1,0:T(8,128)(2,1)S(1)} %collective-permute-done.6.v_ref), channel_id=1, source_target_pairs={{4,8},{5,9},{6,10},{7,11},{20,24},{21,25},{22,26},{23,27}} | collective-permute-start | bytes 393224 | tf_op jit(solution)/shard_map/ppermute | solution.py:345
  14.6 0.0 collective-permute-done.1.rest_1_
  14.6 1.3 %collective-permute-start.3 = (bf16[4,128,128]{2,1,0:T(8,128)(2,1)S(1)}, bf16[4,128,128]{2,1,0:T(8,128)(2,1)S(1)}, u32[]{:S(2)}, u32[]{:S(2)}) collective-permute-start(bf16[4,128,128]{2,1,0:T(8,128)(2,1)S(1)} %add_convert_fusion), channel_id=1, source_target_pairs={{4,8},{5,9},{6,10},{7,11},{20,24},{21,25},{22,26},{23,27}} | collective-permute-start | bytes 393224 | tf_op jit(solution)/shard_map/ppermute | solution.py:367
  15.9 1.9 %shard_map.97 = (f32[8,256,128]{2,1,0:T(8,128)S(1)}, bf16[8,256,128]{2,1,0:T(8,128)(2,1)S(1)}, f32[8,256,128]{2,1,0:T(8,128)S(1)}) custom-call(bf16[2048,128]{1,0:T(8,128)(2,1)S(1)} %get-tuple-element.24.q_ref, bf16[8,256,128]{2,1,0:T(8,128)(2,1)S(1)} %get-tuple-element.25.kh_ref, bf16[8,256,128]{2,1,0:T(8,128)(2,1)S(1)} %get-tuple-element.26.vh_ref, ...), custom_call_target="tpu_custom_call" | custom-call | flops 268435456 | bytes 4202496 | tf_op jit(solution)/shard_map/pallas_call | solution.py:29
  17.8 1.2 %shard_map.100 = (bf16[8,256,128]{2,1,0:T(8,128)(2,1)S(1)}, f32[8,256,128]{2,1,0:T(8,128)S(1)}, f32[8,256,256]{2,1,0:T(8,128)S(1)}) custom-call(bf16[2048,128]{1,0:T(8,128)(2,1)S(1)} %get-tuple-element.38.q_ref, bf16[512,128]{1,0:T(8,128)(2,1)S(1)} %get-tuple-element.39.k_ref, bf16[512,128]{1,0:T(8,128)(2,1)S(1)} %get-tuple-element.40.v_ref), custom_call_target="tpu_custom_call" | custom-call | flops 402653184 | bytes 4456448 | tf_op jit(solution)/shard_map/pallas_call | solution.py:29
  19.0 1.1 %shard_map.101 = (f32[8,256,128]{2,1,0:T(8,128)S(1)}, f32[8,256,256]{2,1,0:T(8,128)S(1)}) custom-call(s32[1]{0:T(128)} %bitcast.4.me_ref, f32[4,128]{1,0:T(4,128)S(1)} %get-tuple-element.31.flags_ref, bf16[8,256,128]{2,1,0:T(8,128)(2,1)S(1)} %get-tuple-element.41.qh_ref, bf16[512,128]{1,0:T(8,128)(2,1)S(1)} %collective-permute-done.4.k_ref, ...), custom_call_target="tpu_custom_call" | custom-call | flops 402653184 | bytes 7079940 | tf_op jit(solution)/shard_map/pallas_call | solution.py:29
  20.1 0.3 collective-permute-done.5.k_ref
  20.3 2.8 %collective-permute-done.7.v_ref = bf16[512,128]{1,0:T(8,128)(2,1)S(1)} collective-permute-done((bf16[512,128]{1,0:T(8,128)(2,1)S(1)}, bf16[512,128]{1,0:T(8,128)(2,1)S(1)}, u32[]{:S(2)}, u32[]{:S(2)}) %collective-permute-start.7) | collective-permute-done | bytes 131104 | tf_op jit(solution)/shard_map/ppermute | solution.py:345
  23.1 2.6 %shard_map.102 = bf16[2048,128]{1,0:T(8,128)(2,1)} custom-call(s32[1]{0:T(128)} %bitcast.4.me_ref, f32[4,128]{1,0:T(4,128)S(1)} %get-tuple-element.31.flags_ref, bf16[8,256,128]{2,1,0:T(8,128)(2,1)S(1)} %get-tuple-element.41.qh_ref, bf16[512,128]{1,0:T(8,128)(2,1)S(1)} %collective-permute-done.5.k_ref, bf16[512,128]{1,0:T(8,128)(2,1)S(1)} %collective-permute-done.7.v_ref, ...), custom_call_target="tpu_custom_call" | custom-call | flops 402653184 | bytes 4458500 | tf_op jit(solution)/shard_map/pallas_call | solution.py:29
  25.7 0.0 collective-permute-done.2.rest_2_
  25.7 0.0 collective-permute-done.3.rest_3_
  25.7 1.6 %shard_map.99 = bf16[2048,128]{1,0:T(8,128)(2,1)} custom-call(f32[8,256,128]{2,1,0:T(8,128)S(1)} %get-tuple-element.28.intra_ref, bf16[8,256,128]{2,1,0:T(8,128)(2,1)S(1)} %get-tuple-element.29.qh_ref, f32[8,256,128]{2,1,0:T(8,128)S(1)} %get-tuple-element.30.lift_ref, bf16[4,128,128]{2,1,0:T(8,128)(2,1)S(1)} %collective-permute-done.rest_0_, ...), custom_call_target="tpu_custom_call" | custom-call | flops 67108864 | bytes 3670016 | tf_op jit(solution)/shard_map/pallas_call | solution.py:29
  (2 shorter events, 0.1 us)
Async XLA Ops:
  0.6 2.7 %copy-start = (bf16[256,2,128]{2,1,0:T(2,128)(2,1)S(1)}, bf16[256,2,128]{2,1,0:T(2,128)(2,1)}, u32[]{:S(2)}) copy-start(bf16[256,2,128]{2,1,0:T(2,128)(2,1)} %param.13) | copy-start | bytes 393220
  0.6 4.0 %copy-start.1 = (bf16[256,2,128]{2,1,0:T(2,128)(2,1)S(1)}, bf16[256,2,128]{2,1,0:T(2,128)(2,1)}, u32[]{:S(2)}) copy-start(bf16[256,2,128]{2,1,0:T(2,128)(2,1)} %param.14) | copy-start | bytes 393220
  2.6 5.3 %collective-permute-start = (bf16[4,128,128]{2,1,0:T(8,128)(2,1)S(1)}, bf16[4,128,128]{2,1,0:T(8,128)(2,1)S(1)}, u32[]{:S(2)}, u32[]{:S(2)}) collective-permute-start(bf16[4,128,128]{2,1,0:T(8,128)(2,1)S(1)} %get-tuple-element.32), channel_id=1, source_target_pairs={{0,4},{1,5},{2,6},{3,7},{16,20},{17,21},{18,22},{19,23}} | collective-permute-start | bytes 393224 | tf_op jit(solution)/shard_map/ppermute | solution.py:367
  3.3 8.0 %collective-permute-start.4 = (bf16[512,128]{1,0:T(8,128)(2,1)S(1)}, bf16[512,128]{1,0:T(8,128)(2,1)S(1)}, u32[]{:S(2)}, u32[]{:S(2)}) collective-permute-start(bf16[512,128]{1,0:T(8,128)(2,1)S(1)} %bitcast.17), channel_id=1, source_target_pairs={{0,4},{4,8},{1,5},{5,9},{2,6},{6,10},{3,7},{7,11},{16,20},{20,24},... | collective-permute-start | bytes 393224 | tf_op jit(solution)/shard_map/ppermute | solution.py:344
  4.6 8.6 %collective-permute-start.6 = (bf16[512,128]{1,0:T(8,128)(2,1)S(1)}, bf16[512,128]{1,0:T(8,128)(2,1)S(1)}, u32[]{:S(2)}, u32[]{:S(2)}) collective-permute-start(bf16[512,128]{1,0:T(8,128)(2,1)S(1)} %bitcast.19), channel_id=1, source_target_pairs={{0,4},{4,8},{1,5},{5,9},{2,6},{6,10},{3,7},{7,11},{16,20},{20,24},... | collective-permute-start | bytes 393224 | tf_op jit(solution)/shard_map/ppermute | solution.py:345
  5.9 8.6 %collective-permute-start.1 = (bf16[4,128,128]{2,1,0:T(8,128)(2,1)S(1)}, bf16[4,128,128]{2,1,0:T(8,128)(2,1)S(1)}, u32[]{:S(2)}, u32[]{:S(2)}) collective-permute-start(bf16[4,128,128]{2,1,0:T(8,128)(2,1)S(1)} %get-tuple-element.33), channel_id=1, source_target_pairs={{0,4},{1,5},{2,6},{3,7},{16,20},{17,21},{18,22},{19,23}} | collective-permute-start | bytes 393224 | tf_op jit(solution)/shard_map/ppermute | solution.py:367
  8.0 17.7 %collective-permute-start.2 = (bf16[4,128,128]{2,1,0:T(8,128)(2,1)S(1)}, bf16[4,128,128]{2,1,0:T(8,128)(2,1)S(1)}, u32[]{:S(2)}, u32[]{:S(2)}) collective-permute-start(bf16[4,128,128]{2,1,0:T(8,128)(2,1)S(1)} %add_convert_fusion.1), channel_id=1, source_target_pairs={{4,8},{5,9},{6,10},{7,11},{20,24},{21,25},{22,26},{23,27}} | collective-permute-start | bytes 393224 | tf_op jit(solution)/shard_map/ppermute | solution.py:367
  11.3 9.0 %collective-permute-start.5 = (bf16[512,128]{1,0:T(8,128)(2,1)S(1)}, bf16[512,128]{1,0:T(8,128)(2,1)S(1)}, u32[]{:S(2)}, u32[]{:S(2)}) collective-permute-start(bf16[512,128]{1,0:T(8,128)(2,1)S(1)} %collective-permute-done.4.k_ref), channel_id=1, source_target_pairs={{4,8},{5,9},{6,10},{7,11},{20,24},{21,25},{22,26},{23,27}} | collective-permute-start | bytes 393224 | tf_op jit(solution)/shard_map/ppermute | solution.py:344
  13.3 9.8 %collective-permute-start.7 = (bf16[512,128]{1,0:T(8,128)(2,1)S(1)}, bf16[512,128]{1,0:T(8,128)(2,1)S(1)}, u32[]{:S(2)}, u32[]{:S(2)}) collective-permute-start(bf16[512,128]{1,0:T(8,128)(2,1)S(1)} %collective-permute-done.6.v_ref), channel_id=1, source_target_pairs={{4,8},{5,9},{6,10},{7,11},{20,24},{21,25},{22,26},{23,27}} | collective-permute-start | bytes 393224 | tf_op jit(solution)/shard_map/ppermute | solution.py:345
  14.6 11.1 %collective-permute-start.3 = (bf16[4,128,128]{2,1,0:T(8,128)(2,1)S(1)}, bf16[4,128,128]{2,1,0:T(8,128)(2,1)S(1)}, u32[]{:S(2)}, u32[]{:S(2)}) collective-permute-start(bf16[4,128,128]{2,1,0:T(8,128)(2,1)S(1)} %add_convert_fusion), channel_id=1, source_target_pairs={{4,8},{5,9},{6,10},{7,11},{20,24},{21,25},{22,26},{23,27}} | collective-permute-start | bytes 393224 | tf_op jit(solution)/shard_map/ppermute | solution.py:367

commit v5 on v4

--- a/solution.py
+++ b/solution.py
@@ -17,6 +17,7 @@
 SMEM = pl.BlockSpec(memory_space=pltpu.SMEM)
 HBM = pl.BlockSpec(memory_space=pltpu.HBM)
 DMA = pltpu.SemaphoreType.DMA
+SHARE = 7
 HALVES = 2
 
 
@@ -24,14 +25,15 @@
     return jax.ShapeDtypeStruct(shape, dtype)
 
 
-def call(body, outs, ins, scratch=(), flops=0, out_spec=VMEM):
+def call(body, outs, ins, scratch=(), flops=0, out_spec=VMEM, aliases={}):
     moved = sum(math.prod(x.shape) * x.dtype.itemsize for x in list(outs) + [i for i, _ in ins])
     return pl.pallas_call(
         body,
         out_shape=tuple(outs),
         in_specs=[spec for _, spec in ins],
-        out_specs=tuple(out_spec for _ in outs),
+        out_specs=out_spec if isinstance(out_spec, tuple) else (out_spec,) * len(outs),
         scratch_shapes=list(scratch),
+        input_output_aliases=aliases,
         cost_estimate=pl.CostEstimate(flops=flops, bytes_accessed=moved, transcendentals=0),
         compiler_params=pltpu.CompilerParams(vmem_limit_bytes=16 << 20),
     )(*[pltpu.with_memory_space_constraint(x, pltpu.HBM) if spec is HBM else x for x, spec in ins])
@@ -60,14 +62,44 @@
     return jnp.dot(a, b, preferred_element_type=F32)
 
 
-def load_body(me_ref, docs_hbm, k_hbm, v_hbm, a_hbm, kh_ref, vh_ref, rise_ref, flags_ref, docs, kb, vb, ab, kw, vw, sems):
+def pack_body(ranks, me_ref, k_hbm, v_hbm, *rest):
+    parts, sems = (rest[:-1], rest[-1])
+
+    @pl.when(me_ref[0] < ranks - 2)
+    def _():
+        rows = k_hbm.shape[0]
+        copies = []
+        first = 0
+        for part in parts:
+            end = first + part.shape[0]
+            for i, x in enumerate((k_hbm, v_hbm)):
+                low, high = (max(first, i * rows), min(end, (i + 1) * rows))
+                if low < high:
+                    copies.append(
+                        pltpu.make_async_copy(
+                            x.at[pl.ds(low - i * rows, high - low)],
+                            part.at[pl.ds(low - first, high - low)],
+                            sems.at[len(copies)],
+                        )
+                    )
+            first = end
+        for copy in copies:
+            copy.start()
+        for copy in copies:
+            copy.wait()
+
+
+def load_body(me_ref, docs_hbm, a_hbm, k_hbm, v_hbm, *rest):
+    later = (len(rest) - 12) // 2
+    fetched, (kh_ref, vh_ref, rise_ref, flags_ref), placed = (
+        rest[:later],
+        rest[later : later + 4],
+        rest[later + 4 : 2 * later + 4],
+    )
+    docs, ab, kb, vb, kw, vw, sems, later_sems = rest[2 * later + 4 :]
     heads, tok, _ = kh_ref.shape
-    copies = [
-        pltpu.make_async_copy(src, dst, sems.at[i])
-        for i, (src, dst) in enumerate(((docs_hbm, docs), (a_hbm, ab), (k_hbm, kb), (v_hbm, vb)))
-    ]
-    for copy in copies:
-        copy.start()
+    copies = start_all((docs_hbm, a_hbm, k_hbm, v_hbm), (docs, ab, kb, vb), sems)
+    extra = start_all(fetched, placed, later_sems)
     copies[0].wait()
     here = me_ref[0]
     doc = doc_at(docs, here * tok)
@@ -83,6 +115,18 @@
         wide[...] = narrow[...].astype(F32)
         for h in range(heads):
             out[h] = wide[pl.ds(h, tok, stride=heads), :].astype(BF16)
+    for copy in extra:
+        copy.wait()
+
+
+def start_all(sources, targets, sems):
+    copies = [
+        pltpu.make_async_copy(src, dst, sems.at[i])
+        for i, (src, dst) in enumerate(zip(sources, targets))
+    ]
+    for copy in copies:
+        copy.start()
+    return copies
 
 
 def state_body(flags_ref, rise_ref, kh_ref, vh_ref, *outs):
@@ -104,18 +148,6 @@
             sends[half][i] = state.astype(BF16)
 
 
-def fetch_body(*refs):
-    count = len(refs) // 2
-    copies = [
-        pltpu.make_async_copy(src, dst, refs[-1].at[i])
-        for i, (src, dst) in enumerate(zip(refs[:count], refs[count:-1]))
-    ]
-    for copy in copies:
-        copy.start()
-    for copy in copies:
-        copy.wait()
-
-
 def intra_body(q_ref, kh_ref, vh_ref, rise_ref, intra_ref, qh_ref, lift_ref, qw):
     heads, tok, dim = kh_ref.shape
     rise_t = rise_ref[...] * LOG2E
@@ -153,42 +185,48 @@
 PARTS = 4
 
 
-def finish_lin_body(intra_ref, qh_ref, lift_ref, *rest):
-    befores, arriveds = (rest[:HALVES], rest[HALVES : 2 * HALVES])
-    out_ref, wide, narrow, sem = rest[2 * HALVES :]
+def finish_body(half, intra_ref, qh_ref, lift_ref, before_ref, arrived_ref, *rest):
     heads, tok, dim = qh_ref.shape
-    states = [
-        before[i] + arrived[i]
-        for before, arrived in zip(befores, arriveds)
-        for i in range(heads // HALVES)
-    ]
+    count = heads // HALVES
+    last = half == HALVES - 1
+    wide = rest[-3] if last else rest[-1]
     ones = jnp.full((dim, dim), 1.0, BF16)
     size = tok // PARTS
     copies = []
     for part in range(PARTS):
         rows = pl.ds(part * size, size)
-        for h in range(heads):
-            inter = dot(qh_ref[h, rows], states[h])
+        for i in range(count):
+            h = half * count + i
+            inter = dot(qh_ref[h, rows], before_ref[i] + arrived_ref[i])
             total = intra_ref[h, rows] + lift_ref[h, rows] * inter
             mean = dot((total * total).astype(BF16), ones) * (1.0 / dim)
             wide[pl.ds(part * size * heads + h, size, stride=heads), :] = total * lax.rsqrt(
                 mean + 1e-06
             )
-        copies.append(put_out(wide, narrow, out_ref, sem, part, PARTS))
+        if last:
+            copies.append(put_out(wide, rest[-2], rest[-4], rest[-1], part, PARTS))
     for copy in copies:
         copy.wait()
 
 
-def keys_of(ref, wide, count, g):
-    keys = ref.shape[0] // count
-    if count == 1:
-        return ref[...]
-    if g == 0:
-        wide[...] = ref[...].astype(F32)
-    return wide[pl.ds(g, keys, stride=count), :].astype(BF16)
-
-
-def first_tile_body(kv_heads, heads, q_ref, k_ref, v_ref, qh_ref, top_ref, acc_ref, qw, kw, vw):
+def sides_of(parts, wide, count):
+    first = 0
+    for part in parts:
+        wide[first : first + part.shape[0]] = part[...].astype(F32)
+        first += part.shape[0]
+    keys = first // (2 * count)
+    ones = jnp.ones((keys, 128), BF16)
+    sides = []
+    for g in range(count):
+        key, value = (
+            wide[pl.ds(side * (first // 2) + g, keys, stride=count), :].astype(BF16)
+            for side in range(2)
+        )
+        sides.append((key, jnp.concatenate([value, ones], axis=1)))
+    return sides
+
+
+def first_tile_body(kv_heads, heads, q_ref, k_ref, v_ref, qh_ref, top_ref, acc_ref, qw, kvw):
     tok = q_ref.shape[0] // heads
     power = LOG2E / math.sqrt(q_ref.shape[1])
     half = tok // 2
@@ -196,10 +234,7 @@
         jnp.int32, (half, half), 1
     )
     qw[...] = q_ref[...].astype(F32)
-    ones = jnp.ones((tok, 128), BF16)
-    for g in range(kv_heads):
-        key = keys_of(k_ref, kw, kv_heads, g)
-        value = jnp.concatenate([keys_of(v_ref, vw, kv_heads, g), ones], axis=1)
+    for g, (key, value) in enumerate(sides_of((k_ref, v_ref), kvw, kv_heads)):
         for h in range(g * heads // kv_heads, (g + 1) * heads // kv_heads):
             query = qw[pl.ds(h, tok, stride=heads), :].astype(BF16)
             qh_ref[h] = query
@@ -215,10 +250,9 @@
 
 
 def next_tile_body(
-    kv_heads, step, last, me_ref, flags_ref, qh_ref, k_ref, v_ref, top_ref, acc_ref, *rest
+    kv_heads, step, last, me_ref, flags_ref, qh_ref, a_ref, b_ref, top_ref, acc_ref, *rest
 ):
     heads, tok, dim = qh_ref.shape
-    kw, vw = rest[-2:]
     power = LOG2E / math.sqrt(dim)
     parts = PARTS if last else 2
     size = tok // parts
@@ -229,11 +263,7 @@
     @pl.when(me_ref[0] >= step)
     def _():
         bias = flags_ref[step : step + 1, :]
-        ones = jnp.ones((tok, 128), BF16)
-        sides = []
-        for g in range(kv_heads):
-            value = jnp.concatenate([keys_of(v_ref, vw, kv_heads, g), ones], axis=1)
-            sides.append((keys_of(k_ref, kw, kv_heads, g), value))
+        sides = sides_of((a_ref, b_ref), rest[-1], kv_heads)
         copies = []
         for part in range(parts):
             rows = pl.ds(part * size, size)
@@ -288,27 +318,39 @@
     decay_t = decay_log.T
     wide_lin = pltpu.VMEM(q_lin.shape, F32)
     wide_q = pltpu.VMEM(q_soft.shape, F32)
-    wide_k = pltpu.VMEM(k_soft.shape, F32)
+    wide_kv = pltpu.VMEM((2 * k_soft.shape[0], dim), F32)
     flat_lin = pltpu.VMEM(q_lin.shape, BF16)
     per_head = shaped((heads, tok, dim), BF16)
 
-    k_heads, v_heads, rise, flags = call(
+    fetched = (q_lin, q_soft, k_soft, v_soft)
+    total = 2 * k_soft.shape[0]
+    early = total * SHARE // 16
+    part_a, part_b = call(
+        functools.partial(pack_body, ranks),
+        (shaped((early, dim), BF16), shaped((total - early, dim), BF16)),
+        ((me, SMEM), (k_soft, HBM), (v_soft, HBM)),
+        (DMA((4,)),),
+    )
+    k_heads, v_heads, rise, flags, q_lin_here, q_here, k_here, v_here = call(
         load_body,
         (
             per_head,
             per_head,
             shaped((heads, tok), F32),
             shaped((ranks, 128), F32),
-        ),
-        ((me, SMEM), (doc_starts, HBM), (k_lin, HBM), (v_lin, HBM), (decay_t, HBM)),
+        )
+        + tuple(shaped(x.shape, x.dtype) for x in fetched),
+        ((me, SMEM),)
+        + tuple((x, HBM) for x in (doc_starts, decay_t, k_lin, v_lin) + fetched),
         (
             pltpu.SMEM(doc_starts.shape, jnp.int32),
+            pltpu.VMEM((heads, tok), F32),
             flat_lin,
             flat_lin,
-            pltpu.VMEM((heads, tok), F32),
             wide_lin,
             wide_lin,
             DMA((4,)),
+            DMA((len(fetched),)),
         ),
     )
     part = heads // HALVES
@@ -321,36 +363,27 @@
         flops=2 * heads * tok * dim * dim,
     )
     states, sends, factors = (outs[:HALVES], list(outs[HALVES : 2 * HALVES]), outs[2 * HALVES :])
-    fetched = (q_lin, q_soft, k_soft, v_soft)
-    q_lin_here, q_here, k_here, v_here = call(
-        fetch_body,
-        tuple(shaped(x.shape, x.dtype) for x in fetched),
-        tuple((x, HBM) for x in fetched),
-        (DMA((len(fetched),)),),
-    )
-
     tile_flops = 6 * soft_heads * tok * tok * dim
     stat_shapes = (shaped((soft_heads, tok, 128), F32), shaped((soft_heads, tok, 2 * dim), F32))
     soft_query, *stats = call(
         functools.partial(first_tile_body, kv_heads, soft_heads),
         (shaped((soft_heads, tok, dim), BF16),) + stat_shapes,
         ((q_here, VMEM), (k_here, VMEM), (v_here, VMEM)),
-        (wide_q, wide_k, wide_k),
+        (wide_q, wide_kv),
         flops=tile_flops,
     )
-    keys, values = k_soft, v_soft
     for step in range(1, ranks - 1):
         pairs = [(i, i + 1) for i in range(step - 1, ranks - 2)]
-        keys = lax.ppermute(keys, "ctx", pairs)
-        values = lax.ppermute(values, "ctx", pairs)
+        part_a = lax.ppermute(part_a, "ctx", pairs)
+        part_b = lax.ppermute(part_b, "ctx", pairs)
         last = step == ranks - 2
         stats = call(
             functools.partial(next_tile_body, kv_heads, step, last),
             (shaped(q_soft.shape, BF16),) if last else stat_shapes,
-            ((me, SMEM), (flags, VMEM), (soft_query, VMEM), (keys, VMEM), (values, VMEM))
+            ((me, SMEM), (flags, VMEM), (soft_query, VMEM), (part_a, VMEM), (part_b, VMEM))
             + tuple((x, VMEM) for x in stats),
             ((wide_q, pltpu.VMEM(q_soft.shape, BF16), DMA((PARTS,))) if last else ())
-            + (wide_k, wide_k),
+            + (wide_kv,),
             flops=tile_flops,
             out_spec=HBM if last else VMEM,
         )
@@ -373,14 +406,22 @@
         (wide_lin,),
         flops=4 * heads * tok * tok * dim,
     )
-    (lin_out,) = call(
-        finish_lin_body,
-        (shaped(q_lin.shape, BF16),),
-        ((intra, VMEM), (lin_query, VMEM), (lift, VMEM)) + tuple((x, VMEM) for x in befores + arrived),
-        (wide_lin, flat_lin, DMA((PARTS,))),
-        flops=2 * heads * tok * dim * dim,
-        out_spec=HBM,
-    )
+    result = ()
+    for half in range(HALVES):
+        last = half == HALVES - 1
+        result = call(
+            functools.partial(finish_body, half),
+            ((shaped(q_lin.shape, BF16),) if last else ()) + (shaped(q_lin.shape, F32),),
+            tuple(
+                (x, VMEM)
+                for x in (intra, lin_query, lift, befores[half], arrived[half]) + result
+            ),
+            (flat_lin, DMA((PARTS,))) if last else (),
+            flops=2 * part * tok * dim * dim,
+            out_spec=(HBM, VMEM) if last else VMEM,
+            aliases={5: int(last)} if half else {},
+        )
+    lin_out = result[0]
     return (lin_out.reshape(tok, heads, dim), soft_out)
 
 

time: 27.6 us -> 29.6 us (1.072)
  waiting for transfers between devices: 5.77 us -> 8.5 us
  Pallas kernels: 11.6 us -> 10.8 us
    ppermute x4, waiting for transfers between devices: 0.01 us -> 2.07 us  [on_device(): arrived[half] = lax.ppermute(sends[half], 'ctx', [(step - 1, step)])]
    pallas_call x8 -> x9, Pallas kernels: 11.6 us -> 10.8 us  [call(): pl.pallas_call(body, out_shape=tuple(outs), in_specs=[spec for _, spec in...]
    ppermute x4, waiting for transfers between devices: 5.76 us -> 6.43 us  [the longest x2 6.14 us: on_device(): part_b = lax.ppermute(part_b, 'ctx', pairs)]
  transfers between devices with their start and end apart: 8 -> 8, of which waited for: 4 -> 3; matrix products, arithmetic and copies ran while one was open for 0% -> 0% of each run, Pallas kernels for 29% -> 20%
where the time goes in v5:
time: 29.6 us; the launch traced here: 29.3 us
  Pallas kernels  10.8 us (36%)
  starting transfers between devices  9.08 us (31%)
  waiting for transfers between devices  8.5 us (29%)
  between operations  0.79 us (3%)
    pallas_call x9, Pallas kernels, call(): pl.pallas_call(body, out_shape=tuple(outs), in_specs=[spec for _, spec in...  10.8 us
    ppermute x2, waiting for transfers between devices, on_device(): part_b = lax.ppermute(part_b, 'ctx', pairs)  6.14 us
    ppermute x4, starting transfers between devices, on_device(): arrived[half] = lax.ppermute(sends[half], 'ctx', [(step - 1, step)])  3.92 us
    ppermute x2, starting transfers between devices, on_device(): part_a = lax.ppermute(part_a, 'ctx', pairs)  2.58 us
    ppermute x2, starting transfers between devices, on_device(): part_b = lax.ppermute(part_b, 'ctx', pairs)  2.57 us
    ppermute x4, waiting for transfers between devices, on_device(): arrived[half] = lax.ppermute(sends[half], 'ctx', [(step - 1, step)])  2.07 us
  transfers between devices with their start and end apart: 8, of which 3 were waited for; matrix products, arithmetic and copies ran while one was open for 0% of the time, Pallas kernels for 20%

profile of v5, /device:TPU:16, one launch (start us, length us, event | category | flops | bytes accessed | tf_op | source)
XLA Modules:
  0.0 29.3 jit_solution(7358519331396658319)
XLA Ops:
  0.6 1.9 %shard_map.95 = (bf16[8,256,128]{2,1,0:T(8,128)(2,1)S(1)}, bf16[8,256,128]{2,1,0:T(8,128)(2,1)S(1)}, f32[8,256]{1,0:T(8,128)S(1)}, f32[4,128]{1,0:T(4,128)S(1)},...) custom-call(s32[1]{0:T(128)} %bitcast.me_ref, ...), custom_call_target="tpu_custom_call" | custom-call | bytes 4737052 | tf_op jit(solution)/shard_map/pallas_call | solution.py:30
  2.6 0.4 %shard_map.97 = (f32[4,128,128]{2,1,0:T(8,128)S(1)}, f32[4,128,128]{2,1,0:T(8,128)S(1)}, bf16[4,128,128]{2,1,0:T(8,128)(2,1)S(1)}, bf16[4,128,128]{2,1,0:T(8,128...) custom-call(f32[4,128]{1,0:T(4,128)S(1)} %get-tuple-element.34.flags_ref, ...), custom_call_target="tpu_custom_call" | custom-call | flops 67108864 | bytes 1849344 | tf_op jit(solution)/shard_map/pallas_call | solution.py:30
  2.9 0.7 %collective-permute-start.2 = (bf16[4,128,128]{2,1,0:T(8,128)(2,1)S(1)}, bf16[4,128,128]{2,1,0:T(8,128)(2,1)S(1)}, u32[]{:S(2)}, u32[]{:S(2)}) collective-permute-start(bf16[4,128,128]{2,1,0:T(8,128)(2,1)S(1)} %get-tuple-element.38), channel_id=1, source_target_pairs={{0,4},{1,5},{2,6},{3,7},{16,20},{17,21},{18,22},{19,23}} | collective-permute-start | bytes 393224 | tf_op jit(solution)/shard_map/ppermute | solution.py:400
  3.7 1.3 %collective-permute-start.4 = (bf16[448,128]{1,0:T(8,128)(2,1)S(1)}, bf16[448,128]{1,0:T(8,128)(2,1)S(1)}, u32[]{:S(2)}, u32[]{:S(2)}) collective-permute-start(bf16[448,128]{1,0:T(8,128)(2,1)S(1)} %get-tuple-element.46), channel_id=1, source_target_pairs={{0,4},{4,8},{1,5},{5,9},{2,6},{6,10},{3,7},{7,11},{16,20},{20,24},... | collective-permute-start | bytes 344072 | tf_op jit(solution)/shard_map/ppermute | solution.py:377
  5.0 1.3 %collective-permute-start.6 = (bf16[576,128]{1,0:T(8,128)(2,1)S(1)}, bf16[576,128]{1,0:T(8,128)(2,1)S(1)}, u32[]{:S(2)}, u32[]{:S(2)}) collective-permute-start(bf16[576,128]{1,0:T(8,128)(2,1)S(1)} %get-tuple-element.47), channel_id=1, source_target_pairs={{0,4},{4,8},{1,5},{5,9},{2,6},{6,10},{3,7},{7,11},{16,20},{20,24},... | collective-permute-start | bytes 442376 | tf_op jit(solution)/shard_map/ppermute | solution.py:378
  6.3 0.7 %collective-permute-start = (bf16[4,128,128]{2,1,0:T(8,128)(2,1)S(1)}, bf16[4,128,128]{2,1,0:T(8,128)(2,1)S(1)}, u32[]{:S(2)}, u32[]{:S(2)}) collective-permute-start(bf16[4,128,128]{2,1,0:T(8,128)(2,1)S(1)} %get-tuple-element.35), channel_id=1, source_target_pairs={{0,4},{1,5},{2,6},{3,7},{16,20},{17,21},{18,22},{19,23}} | collective-permute-start | bytes 393224 | tf_op jit(solution)/shard_map/ppermute | solution.py:400
  6.9 0.0 collective-permute-done.2.before_ref
  7.0 1.3 %collective-permute-start.3 = (bf16[4,128,128]{2,1,0:T(8,128)(2,1)S(1)}, bf16[4,128,128]{2,1,0:T(8,128)(2,1)S(1)}, u32[]{:S(2)}, u32[]{:S(2)}) collective-permute-start(bf16[4,128,128]{2,1,0:T(8,128)(2,1)S(1)} %add_convert_fusion), channel_id=1, source_target_pairs={{4,8},{5,9},{6,10},{7,11},{20,24},{21,25},{22,26},{23,27}} | collective-permute-start | bytes 393224 | tf_op jit(solution)/shard_map/ppermute | solution.py:400
  8.3 6.1 %collective-permute-done.6.b_ref = bf16[576,128]{1,0:T(8,128)(2,1)S(1)} collective-permute-done((bf16[576,128]{1,0:T(8,128)(2,1)S(1)}, bf16[576,128]{1,0:T(8,128)(2,1)S(1)}, u32[]{:S(2)}, u32[]{:S(2)}) %collective-permute-start.6) | collective-permute-done | bytes 147488 | tf_op jit(solution)/shard_map/ppermute | solution.py:378
  14.4 1.3 %collective-permute-start.7 = (bf16[576,128]{1,0:T(8,128)(2,1)S(1)}, bf16[576,128]{1,0:T(8,128)(2,1)S(1)}, u32[]{:S(2)}, u32[]{:S(2)}) collective-permute-start(bf16[576,128]{1,0:T(8,128)(2,1)S(1)} %collective-permute-done.6.b_ref), channel_id=1, source_target_pairs={{4,8},{5,9},{6,10},{7,11},{20,24},{21,25},{22,26},{23,27}} | collective-permute-start | bytes 442376 | tf_op jit(solution)/shard_map/ppermute | solution.py:378
  15.7 0.0 collective-permute-done.before_ref
  15.8 1.3 %collective-permute-start.1 = (bf16[4,128,128]{2,1,0:T(8,128)(2,1)S(1)}, bf16[4,128,128]{2,1,0:T(8,128)(2,1)S(1)}, u32[]{:S(2)}, u32[]{:S(2)}) collective-permute-start(bf16[4,128,128]{2,1,0:T(8,128)(2,1)S(1)} %add_convert_fusion.1), channel_id=1, source_target_pairs={{4,8},{5,9},{6,10},{7,11},{20,24},{21,25},{22,26},{23,27}} | collective-permute-start | bytes 393224 | tf_op jit(solution)/shard_map/ppermute | solution.py:400
  17.1 0.0 collective-permute-done.4.a_ref
  17.1 1.3 %collective-permute-start.5 = (bf16[448,128]{1,0:T(8,128)(2,1)S(1)}, bf16[448,128]{1,0:T(8,128)(2,1)S(1)}, u32[]{:S(2)}, u32[]{:S(2)}) collective-permute-start(bf16[448,128]{1,0:T(8,128)(2,1)S(1)} %collective-permute-done.4.a_ref), channel_id=1, source_target_pairs={{4,8},{5,9},{6,10},{7,11},{20,24},{21,25},{22,26},{23,27}} | collective-permute-start | bytes 344072 | tf_op jit(solution)/shard_map/ppermute | solution.py:377
  18.4 1.9 %shard_map.96 = (f32[8,256,128]{2,1,0:T(8,128)S(1)}, bf16[8,256,128]{2,1,0:T(8,128)(2,1)S(1)}, f32[8,256,128]{2,1,0:T(8,128)S(1)}) custom-call(bf16[2048,128]{1,0:T(8,128)(2,1)S(1)} %get-tuple-element.27.q_ref, bf16[8,256,128]{2,1,0:T(8,128)(2,1)S(1)} %get-tuple-element.28.kh_ref, bf16[8,256,128]{2,1,0:T(8,128)(2,1)S(1)} %get-tuple-element.29.vh_ref, ...), custom_call_target="tpu_custom_call" | custom-call | flops 268435456 | bytes 4202496 | tf_op jit(solution)/shard_map/pallas_call | solution.py:30
  20.3 1.2 %shard_map.100 = (bf16[8,256,128]{2,1,0:T(8,128)(2,1)S(1)}, f32[8,256,128]{2,1,0:T(8,128)S(1)}, f32[8,256,256]{2,1,0:T(8,128)S(1)}) custom-call(bf16[2048,128]{1,0:T(8,128)(2,1)S(1)} %get-tuple-element.42.q_ref, bf16[512,128]{1,0:T(8,128)(2,1)S(1)} %get-tuple-element.43.k_ref, bf16[512,128]{1,0:T(8,128)(2,1)S(1)} %get-tuple-element.44.v_ref), custom_call_target="tpu_custom_call" | custom-call | flops 402653184 | bytes 4456448 | tf_op jit(solution)/shard_map/pallas_call | solution.py:30
  21.4 1.1 %shard_map.102 = (f32[8,256,128]{2,1,0:T(8,128)S(1)}, f32[8,256,256]{2,1,0:T(8,128)S(1)}) custom-call(s32[1]{0:T(128)} %bitcast.me_ref, f32[4,128]{1,0:T(4,128)S(1)} %get-tuple-element.34.flags_ref, bf16[8,256,128]{2,1,0:T(8,128)(2,1)S(1)} %get-tuple-element.45.qh_ref, bf16[448,128]{1,0:T(8,128)(2,1)S(1)} %collective-permute-done.4.a_ref, ...), custom_call_target="tpu_custom_call" | custom-call | flops 402653184 | bytes 7079940 | tf_op jit(solution)/shard_map/pallas_call | solution.py:30
  22.5 0.0 collective-permute-done.3.arrived_ref
  22.5 0.5 %shard_map.98.rest_0_ = f32[2048,128]{1,0:T(8,128)S(1)} custom-call(f32[8,256,128]{2,1,0:T(8,128)S(1)} %get-tuple-element.31.intra_ref, bf16[8,256,128]{2,1,0:T(8,128)(2,1)S(1)} %get-tuple-element.32.qh_ref, f32[8,256,128]{2,1,0:T(8,128)S(1)} %get-tuple-element.33.lift_ref, bf16[4,128,128]{2,1,0:T(8,128)(2,1)S(1)} %collective-permute-done.2.before_ref, ...), custom_call_target="tpu_custom_call" | custom-call | flops 33554432 | bytes 3932160 | tf_op jit(solution)/shard_map/pallas_call | solution.py:30
  23.1 2.1 %collective-permute-done.1.arrived_ref = bf16[4,128,128]{2,1,0:T(8,128)(2,1)S(1)} collective-permute-done((bf16[4,128,128]{2,1,0:T(8,128)(2,1)S(1)}, bf16[4,128,128]{2,1,0:T(8,128)(2,1)S(1)}, u32[]{:S(2)}, u32[]{:S(2)}) %collective-permute-start.1) | collective-permute-done | bytes 131104 | tf_op jit(solution)/shard_map/ppermute | solution.py:400
  25.2 1.3 %shard_map.99 = (bf16[2048,128]{1,0:T(8,128)(2,1)}, f32[2048,128]{1,0:T(8,128)S(1)}) custom-call(f32[8,256,128]{2,1,0:T(8,128)S(1)} %get-tuple-element.31.intra_ref, bf16[8,256,128]{2,1,0:T(8,128)(2,1)S(1)} %get-tuple-element.32.qh_ref, f32[8,256,128]{2,1,0:T(8,128)S(1)} %get-tuple-element.33.lift_ref, ...), custom_call_target="tpu_custom_call", output_to_operand_aliasing={{1}: (5, {})} | custom-call | flops 33554432 | bytes 5505024 | tf_op jit(solution)/shard_map/pallas_call | solution.py:30
  26.4 0.3 collective-permute-done.5.a_ref
  26.7 0.0 collective-permute-done.7.b_ref
  26.7 2.6 %shard_map.103 = bf16[2048,128]{1,0:T(8,128)(2,1)} custom-call(s32[1]{0:T(128)} %bitcast.me_ref, f32[4,128]{1,0:T(4,128)S(1)} %get-tuple-element.34.flags_ref, bf16[8,256,128]{2,1,0:T(8,128)(2,1)S(1)} %get-tuple-element.45.qh_ref, bf16[448,128]{1,0:T(8,128)(2,1)S(1)} %collective-permute-done.5.a_ref, bf16[576,128]{1,0:T(8,128)(2,1)S(1)} %collective-permute-done.7.b_ref, ...), custom_call_target="tpu_custom_call" | custom-call | flops 402653184 | bytes 4458500 | tf_op jit(solution)/shard_map/pallas_call | solution.py:30
  (3 shorter events, 0.1 us)
Async XLA Ops:
  2.9 4.0 %collective-permute-start.2 = (bf16[4,128,128]{2,1,0:T(8,128)(2,1)S(1)}, bf16[4,128,128]{2,1,0:T(8,128)(2,1)S(1)}, u32[]{:S(2)}, u32[]{:S(2)}) collective-permute-start(bf16[4,128,128]{2,1,0:T(8,128)(2,1)S(1)} %get-tuple-element.38), channel_id=1, source_target_pairs={{0,4},{1,5},{2,6},{3,7},{16,20},{17,21},{18,22},{19,23}} | collective-permute-start | bytes 393224 | tf_op jit(solution)/shard_map/ppermute | solution.py:400
  3.7 13.4 %collective-permute-start.4 = (bf16[448,128]{1,0:T(8,128)(2,1)S(1)}, bf16[448,128]{1,0:T(8,128)(2,1)S(1)}, u32[]{:S(2)}, u32[]{:S(2)}) collective-permute-start(bf16[448,128]{1,0:T(8,128)(2,1)S(1)} %get-tuple-element.46), channel_id=1, source_target_pairs={{0,4},{4,8},{1,5},{5,9},{2,6},{6,10},{3,7},{7,11},{16,20},{20,24},... | collective-permute-start | bytes 344072 | tf_op jit(solution)/shard_map/ppermute | solution.py:377
  5.0 9.5 %collective-permute-start.6 = (bf16[576,128]{1,0:T(8,128)(2,1)S(1)}, bf16[576,128]{1,0:T(8,128)(2,1)S(1)}, u32[]{:S(2)}, u32[]{:S(2)}) collective-permute-start(bf16[576,128]{1,0:T(8,128)(2,1)S(1)} %get-tuple-element.47), channel_id=1, source_target_pairs={{0,4},{4,8},{1,5},{5,9},{2,6},{6,10},{3,7},{7,11},{16,20},{20,24},... | collective-permute-start | bytes 442376 | tf_op jit(solution)/shard_map/ppermute | solution.py:378
  6.3 9.5 %collective-permute-start = (bf16[4,128,128]{2,1,0:T(8,128)(2,1)S(1)}, bf16[4,128,128]{2,1,0:T(8,128)(2,1)S(1)}, u32[]{:S(2)}, u32[]{:S(2)}) collective-permute-start(bf16[4,128,128]{2,1,0:T(8,128)(2,1)S(1)} %get-tuple-element.35), channel_id=1, source_target_pairs={{0,4},{1,5},{2,6},{3,7},{16,20},{17,21},{18,22},{19,23}} | collective-permute-start | bytes 393224 | tf_op jit(solution)/shard_map/ppermute | solution.py:400
  7.0 15.5 %collective-permute-start.3 = (bf16[4,128,128]{2,1,0:T(8,128)(2,1)S(1)}, bf16[4,128,128]{2,1,0:T(8,128)(2,1)S(1)}, u32[]{:S(2)}, u32[]{:S(2)}) collective-permute-start(bf16[4,128,128]{2,1,0:T(8,128)(2,1)S(1)} %add_convert_fusion), channel_id=1, source_target_pairs={{4,8},{5,9},{6,10},{7,11},{20,24},{21,25},{22,26},{23,27}} | collective-permute-start | bytes 393224 | tf_op jit(solution)/shard_map/ppermute | solution.py:400
  14.4 12.3 %collective-permute-start.7 = (bf16[576,128]{1,0:T(8,128)(2,1)S(1)}, bf16[576,128]{1,0:T(8,128)(2,1)S(1)}, u32[]{:S(2)}, u32[]{:S(2)}) collective-permute-start(bf16[576,128]{1,0:T(8,128)(2,1)S(1)} %collective-permute-done.6.b_ref), channel_id=1, source_target_pairs={{4,8},{5,9},{6,10},{7,11},{20,24},{21,25},{22,26},{23,27}} | collective-permute-start | bytes 442376 | tf_op jit(solution)/shard_map/ppermute | solution.py:378
  15.8 9.4 %collective-permute-start.1 = (bf16[4,128,128]{2,1,0:T(8,128)(2,1)S(1)}, bf16[4,128,128]{2,1,0:T(8,128)(2,1)S(1)}, u32[]{:S(2)}, u32[]{:S(2)}) collective-permute-start(bf16[4,128,128]{2,1,0:T(8,128)(2,1)S(1)} %add_convert_fusion.1), channel_id=1, source_target_pairs={{4,8},{5,9},{6,10},{7,11},{20,24},{21,25},{22,26},{23,27}} | collective-permute-start | bytes 393224 | tf_op jit(solution)/shard_map/ppermute | solution.py:400
  17.1 9.6 %collective-permute-start.5 = (bf16[448,128]{1,0:T(8,128)(2,1)S(1)}, bf16[448,128]{1,0:T(8,128)(2,1)S(1)}, u32[]{:S(2)}, u32[]{:S(2)}) collective-permute-start(bf16[448,128]{1,0:T(8,128)(2,1)S(1)} %collective-permute-done.4.a_ref), channel_id=1, source_target_pairs={{4,8},{5,9},{6,10},{7,11},{20,24},{21,25},{22,26},{23,27}} | collective-permute-start | bytes 344072 | tf_op jit(solution)/shard_map/ppermute | solution.py:377

commit v6 on v5

--- a/solution.py
+++ b/solution.py
@@ -18,7 +18,8 @@
 HBM = pl.BlockSpec(memory_space=pltpu.HBM)
 DMA = pltpu.SemaphoreType.DMA
 SHARE = 7
-HALVES = 2
+CUTS = (0, 4, 8)
+HALVES = len(CUTS) - 1
 
 
 def shaped(shape, dtype):
@@ -137,11 +138,11 @@
     last = rise[:, tok - 1 : tok]
     factor = jnp.broadcast_to(jnp.exp(last), (heads, 128)) * keep
     fade = jnp.exp(last - rise)
-    size = heads // HALVES
     for half in range(HALVES):
-        factors[half][...] = factor[half * size : (half + 1) * size]
+        first, size = group_of(half, heads)
+        factors[half][...] = factor[first : first + size]
         for i in range(size):
-            h = half * size + i
+            h = first + i
             tail_t = (jnp.transpose(kh_ref[h].astype(F32)) * fade[h : h + 1, :]).astype(BF16)
             state = dot(tail_t, vh_ref[h]) * keep
             states[half][i] = state
@@ -182,12 +183,17 @@
     return copy
 
 
-PARTS = 4
+PARTS = 2
+
+
+def group_of(half, heads):
+    low, high = (CUTS[half] * heads // 8, CUTS[half + 1] * heads // 8)
+    return low, high - low
 
 
 def finish_body(half, intra_ref, qh_ref, lift_ref, before_ref, arrived_ref, *rest):
     heads, tok, dim = qh_ref.shape
-    count = heads // HALVES
+    first, count = group_of(half, heads)
     last = half == HALVES - 1
     wide = rest[-3] if last else rest[-1]
     ones = jnp.full((dim, dim), 1.0, BF16)
@@ -196,7 +202,7 @@
     for part in range(PARTS):
         rows = pl.ds(part * size, size)
         for i in range(count):
-            h = half * count + i
+            h = first + i
             inter = dot(qh_ref[h, rows], before_ref[i] + arrived_ref[i])
             total = intra_ref[h, rows] + lift_ref[h, rows] * inter
             mean = dot((total * total).astype(BF16), ones) * (1.0 / dim)
@@ -353,12 +359,12 @@
             DMA((len(fetched),)),
         ),
     )
-    part = heads // HALVES
+    counts = [group_of(half, heads)[1] for half in range(HALVES)]
     outs = call(
         state_body,
-        (shaped((part, dim, dim), F32),) * HALVES
-        + (shaped((part, dim, dim), BF16),) * HALVES
-        + (shaped((part, 128), F32),) * HALVES,
+        tuple(shaped((count, dim, dim), F32) for count in counts)
+        + tuple(shaped((count, dim, dim), BF16) for count in counts)
+        + tuple(shaped((count, 128), F32) for count in counts),
         ((flags, VMEM), (rise, VMEM), (k_heads, VMEM), (v_heads, VMEM)),
         flops=2 * heads * tok * dim * dim,
     )
@@ -389,7 +395,7 @@
         )
     soft_out = stats[0].reshape(tok, soft_heads, dim)
 
-    befores = [jnp.zeros((part, dim, dim), BF16) for _ in range(HALVES)]
+    befores = [jnp.zeros((count, dim, dim), BF16) for count in counts]
     arrived = [None] * HALVES
     for step in range(1, ranks - 1):
         for half in range(HALVES):
@@ -417,7 +423,7 @@
                 for x in (intra, lin_query, lift, befores[half], arrived[half]) + result
             ),
             (flat_lin, DMA((PARTS,))) if last else (),
-            flops=2 * part * tok * dim * dim,
+            flops=2 * counts[half] * tok * dim * dim,
             out_spec=(HBM, VMEM) if last else VMEM,
             aliases={5: int(last)} if half else {},
         )

time: 29.6 us -> 29 us (0.980)
  the two profiles are of different devices: /device:TPU:16 before, /device:TPU:22 now
where the time goes in v6:
time: 29 us; the launch traced here: 28.7 us
  Pallas kernels  10 us (34%)
  starting transfers between devices  9.08 us (31%)
  waiting for transfers between devices  8.71 us (30%)
  between operations  0.79 us (3%)
    pallas_call x9, Pallas kernels, call(): pl.pallas_call(body, out_shape=tuple(outs), in_specs=[spec for _, spec in...  10 us
    ppermute x2, waiting for transfers between devices, on_device(): part_b = lax.ppermute(part_b, 'ctx', pairs)  6.14 us
    ppermute x4, starting transfers between devices, on_device(): arrived[half] = lax.ppermute(sends[half], 'ctx', [(step - 1, step)])  3.92 us
    ppermute x2, starting transfers between devices, on_device(): part_a = lax.ppermute(part_a, 'ctx', pairs)  2.58 us
    ppermute x2, starting transfers between devices, on_device(): part_b = lax.ppermute(part_b, 'ctx', pairs)  2.57 us
    ppermute x4, waiting for transfers between devices, on_device(): arrived[half] = lax.ppermute(sends[half], 'ctx', [(step - 1, step)])  2.2 us
  transfers between devices with their start and end apart: 8, of which 3 were waited for; matrix products, arithmetic and copies ran while one was open for 0% of the time, Pallas kernels for 20%

profile of v6, /device:TPU:22, one launch (start us, length us, event | category | flops | bytes accessed | tf_op | source)
XLA Modules:
  0.0 28.7 jit_solution(9632744971016451855)
XLA Ops:
  0.6 1.9 %shard_map.95 = (bf16[8,256,128]{2,1,0:T(8,128)(2,1)S(1)}, bf16[8,256,128]{2,1,0:T(8,128)(2,1)S(1)}, f32[8,256]{1,0:T(8,128)S(1)}, f32[4,128]{1,0:T(4,128)S(1)},...) custom-call(s32[1]{0:T(128)} %bitcast.me_ref, ...), custom_call_target="tpu_custom_call" | custom-call | bytes 4737052 | tf_op jit(solution)/shard_map/pallas_call | solution.py:31
  2.6 0.4 %shard_map.97 = (f32[4,128,128]{2,1,0:T(8,128)S(1)}, f32[4,128,128]{2,1,0:T(8,128)S(1)}, bf16[4,128,128]{2,1,0:T(8,128)(2,1)S(1)}, bf16[4,128,128]{2,1,0:T(8,128...) custom-call(f32[4,128]{1,0:T(4,128)S(1)} %get-tuple-element.34.flags_ref, ...), custom_call_target="tpu_custom_call" | custom-call | flops 67108864 | bytes 1849344 | tf_op jit(solution)/shard_map/pallas_call | solution.py:31
  2.9 0.7 %collective-permute-start.2 = (bf16[4,128,128]{2,1,0:T(8,128)(2,1)S(1)}, bf16[4,128,128]{2,1,0:T(8,128)(2,1)S(1)}, u32[]{:S(2)}, u32[]{:S(2)}) collective-permute-start(bf16[4,128,128]{2,1,0:T(8,128)(2,1)S(1)} %get-tuple-element.38), channel_id=1, source_target_pairs={{0,4},{1,5},{2,6},{3,7},{16,20},{17,21},{18,22},{19,23}} | collective-permute-start | bytes 393224 | tf_op jit(solution)/shard_map/ppermute | solution.py:406
  3.7 1.3 %collective-permute-start.4 = (bf16[448,128]{1,0:T(8,128)(2,1)S(1)}, bf16[448,128]{1,0:T(8,128)(2,1)S(1)}, u32[]{:S(2)}, u32[]{:S(2)}) collective-permute-start(bf16[448,128]{1,0:T(8,128)(2,1)S(1)} %get-tuple-element.46), channel_id=1, source_target_pairs={{0,4},{4,8},{1,5},{5,9},{2,6},{6,10},{3,7},{7,11},{16,20},{20,24},... | collective-permute-start | bytes 344072 | tf_op jit(solution)/shard_map/ppermute | solution.py:383
  5.0 1.3 %collective-permute-start.6 = (bf16[576,128]{1,0:T(8,128)(2,1)S(1)}, bf16[576,128]{1,0:T(8,128)(2,1)S(1)}, u32[]{:S(2)}, u32[]{:S(2)}) collective-permute-start(bf16[576,128]{1,0:T(8,128)(2,1)S(1)} %get-tuple-element.47), channel_id=1, source_target_pairs={{0,4},{4,8},{1,5},{5,9},{2,6},{6,10},{3,7},{7,11},{16,20},{20,24},... | collective-permute-start | bytes 442376 | tf_op jit(solution)/shard_map/ppermute | solution.py:384
  6.3 0.7 %collective-permute-start = (bf16[4,128,128]{2,1,0:T(8,128)(2,1)S(1)}, bf16[4,128,128]{2,1,0:T(8,128)(2,1)S(1)}, u32[]{:S(2)}, u32[]{:S(2)}) collective-permute-start(bf16[4,128,128]{2,1,0:T(8,128)(2,1)S(1)} %get-tuple-element.35), channel_id=1, source_target_pairs={{0,4},{1,5},{2,6},{3,7},{16,20},{17,21},{18,22},{19,23}} | collective-permute-start | bytes 393224 | tf_op jit(solution)/shard_map/ppermute | solution.py:406
  6.9 0.0 collective-permute-done.2.before_ref
  7.0 1.3 %collective-permute-start.3 = (bf16[4,128,128]{2,1,0:T(8,128)(2,1)S(1)}, bf16[4,128,128]{2,1,0:T(8,128)(2,1)S(1)}, u32[]{:S(2)}, u32[]{:S(2)}) collective-permute-start(bf16[4,128,128]{2,1,0:T(8,128)(2,1)S(1)} %add_convert_fusion), channel_id=1, source_target_pairs={{4,8},{5,9},{6,10},{7,11},{20,24},{21,25},{22,26},{23,27}} | collective-permute-start | bytes 393224 | tf_op jit(solution)/shard_map/ppermute | solution.py:406
  8.3 6.1 %collective-permute-done.6.b_ref = bf16[576,128]{1,0:T(8,128)(2,1)S(1)} collective-permute-done((bf16[576,128]{1,0:T(8,128)(2,1)S(1)}, bf16[576,128]{1,0:T(8,128)(2,1)S(1)}, u32[]{:S(2)}, u32[]{:S(2)}) %collective-permute-start.6) | collective-permute-done | bytes 147488 | tf_op jit(solution)/shard_map/ppermute | solution.py:384
  14.4 1.3 %collective-permute-start.7 = (bf16[576,128]{1,0:T(8,128)(2,1)S(1)}, bf16[576,128]{1,0:T(8,128)(2,1)S(1)}, u32[]{:S(2)}, u32[]{:S(2)}) collective-permute-start(bf16[576,128]{1,0:T(8,128)(2,1)S(1)} %collective-permute-done.6.b_ref), channel_id=1, source_target_pairs={{4,8},{5,9},{6,10},{7,11},{20,24},{21,25},{22,26},{23,27}} | collective-permute-start | bytes 442376 | tf_op jit(solution)/shard_map/ppermute | solution.py:384
  15.7 0.0 collective-permute-done.before_ref
  15.8 1.3 %collective-permute-start.1 = (bf16[4,128,128]{2,1,0:T(8,128)(2,1)S(1)}, bf16[4,128,128]{2,1,0:T(8,128)(2,1)S(1)}, u32[]{:S(2)}, u32[]{:S(2)}) collective-permute-start(bf16[4,128,128]{2,1,0:T(8,128)(2,1)S(1)} %add_convert_fusion.1), channel_id=1, source_target_pairs={{4,8},{5,9},{6,10},{7,11},{20,24},{21,25},{22,26},{23,27}} | collective-permute-start | bytes 393224 | tf_op jit(solution)/shard_map/ppermute | solution.py:406
  17.1 0.0 collective-permute-done.4.a_ref
  17.1 1.3 %collective-permute-start.5 = (bf16[448,128]{1,0:T(8,128)(2,1)S(1)}, bf16[448,128]{1,0:T(8,128)(2,1)S(1)}, u32[]{:S(2)}, u32[]{:S(2)}) collective-permute-start(bf16[448,128]{1,0:T(8,128)(2,1)S(1)} %collective-permute-done.4.a_ref), channel_id=1, source_target_pairs={{4,8},{5,9},{6,10},{7,11},{20,24},{21,25},{22,26},{23,27}} | collective-permute-start | bytes 344072 | tf_op jit(solution)/shard_map/ppermute | solution.py:383
  18.4 1.9 %shard_map.96 = (f32[8,256,128]{2,1,0:T(8,128)S(1)}, bf16[8,256,128]{2,1,0:T(8,128)(2,1)S(1)}, f32[8,256,128]{2,1,0:T(8,128)S(1)}) custom-call(bf16[2048,128]{1,0:T(8,128)(2,1)S(1)} %get-tuple-element.27.q_ref, bf16[8,256,128]{2,1,0:T(8,128)(2,1)S(1)} %get-tuple-element.28.kh_ref, bf16[8,256,128]{2,1,0:T(8,128)(2,1)S(1)} %get-tuple-element.29.vh_ref, ...), custom_call_target="tpu_custom_call" | custom-call | flops 268435456 | bytes 4202496 | tf_op jit(solution)/shard_map/pallas_call | solution.py:31
  20.3 1.2 %shard_map.100 = (bf16[8,256,128]{2,1,0:T(8,128)(2,1)S(1)}, f32[8,256,128]{2,1,0:T(8,128)S(1)}, f32[8,256,256]{2,1,0:T(8,128)S(1)}) custom-call(bf16[2048,128]{1,0:T(8,128)(2,1)S(1)} %get-tuple-element.42.q_ref, bf16[512,128]{1,0:T(8,128)(2,1)S(1)} %get-tuple-element.43.k_ref, bf16[512,128]{1,0:T(8,128)(2,1)S(1)} %get-tuple-element.44.v_ref), custom_call_target="tpu_custom_call" | custom-call | flops 402653184 | bytes 4456448 | tf_op jit(solution)/shard_map/pallas_call | solution.py:31
  21.4 1.1 %shard_map.102 = (f32[8,256,128]{2,1,0:T(8,128)S(1)}, f32[8,256,256]{2,1,0:T(8,128)S(1)}) custom-call(s32[1]{0:T(128)} %bitcast.me_ref, f32[4,128]{1,0:T(4,128)S(1)} %get-tuple-element.34.flags_ref, bf16[8,256,128]{2,1,0:T(8,128)(2,1)S(1)} %get-tuple-element.45.qh_ref, bf16[448,128]{1,0:T(8,128)(2,1)S(1)} %collective-permute-done.4.a_ref, ...), custom_call_target="tpu_custom_call" | custom-call | flops 402653184 | bytes 7079940 | tf_op jit(solution)/shard_map/pallas_call | solution.py:31
  22.5 0.0 collective-permute-done.3.arrived_ref
  22.5 0.4 %shard_map.98.rest_0_ = f32[2048,128]{1,0:T(8,128)S(1)} custom-call(f32[8,256,128]{2,1,0:T(8,128)S(1)} %get-tuple-element.31.intra_ref, bf16[8,256,128]{2,1,0:T(8,128)(2,1)S(1)} %get-tuple-element.32.qh_ref, f32[8,256,128]{2,1,0:T(8,128)S(1)} %get-tuple-element.33.lift_ref, bf16[4,128,128]{2,1,0:T(8,128)(2,1)S(1)} %collective-permute-done.2.before_ref, ...), custom_call_target="tpu_custom_call" | custom-call | flops 33554432 | bytes 3932160 | tf_op jit(solution)/shard_map/pallas_call | solution.py:31
  23.0 2.2 %collective-permute-done.1.arrived_ref = bf16[4,128,128]{2,1,0:T(8,128)(2,1)S(1)} collective-permute-done((bf16[4,128,128]{2,1,0:T(8,128)(2,1)S(1)}, bf16[4,128,128]{2,1,0:T(8,128)(2,1)S(1)}, u32[]{:S(2)}, u32[]{:S(2)}) %collective-permute-start.1) | collective-permute-done | bytes 131104 | tf_op jit(solution)/shard_map/ppermute | solution.py:406
  25.2 1.2 %shard_map.99 = (bf16[2048,128]{1,0:T(8,128)(2,1)}, f32[2048,128]{1,0:T(8,128)S(1)}) custom-call(f32[8,256,128]{2,1,0:T(8,128)S(1)} %get-tuple-element.31.intra_ref, bf16[8,256,128]{2,1,0:T(8,128)(2,1)S(1)} %get-tuple-element.32.qh_ref, f32[8,256,128]{2,1,0:T(8,128)S(1)} %get-tuple-element.33.lift_ref, ...), custom_call_target="tpu_custom_call", output_to_operand_aliasing={{1}: (5, {})} | custom-call | flops 33554432 | bytes 5505024 | tf_op jit(solution)/shard_map/pallas_call | solution.py:31
  26.4 0.4 %collective-permute-done.5.a_ref = bf16[448,128]{1,0:T(8,128)(2,1)S(1)} collective-permute-done((bf16[448,128]{1,0:T(8,128)(2,1)S(1)}, bf16[448,128]{1,0:T(8,128)(2,1)S(1)}, u32[]{:S(2)}, u32[]{:S(2)}) %collective-permute-start.5) | collective-permute-done | bytes 114720 | tf_op jit(solution)/shard_map/ppermute | solution.py:383
  26.7 0.0 collective-permute-done.7.b_ref
  26.7 2.0 %shard_map.103 = bf16[2048,128]{1,0:T(8,128)(2,1)} custom-call(s32[1]{0:T(128)} %bitcast.me_ref, f32[4,128]{1,0:T(4,128)S(1)} %get-tuple-element.34.flags_ref, bf16[8,256,128]{2,1,0:T(8,128)(2,1)S(1)} %get-tuple-element.45.qh_ref, bf16[448,128]{1,0:T(8,128)(2,1)S(1)} %collective-permute-done.5.a_ref, bf16[576,128]{1,0:T(8,128)(2,1)S(1)} %collective-permute-done.7.b_ref, ...), custom_call_target="tpu_custom_call" | custom-call | flops 402653184 | bytes 4458500 | tf_op jit(solution)/shard_map/pallas_call | solution.py:31
  (3 shorter events, 0.1 us)
Async XLA Ops:
  2.9 4.0 %collective-permute-start.2 = (bf16[4,128,128]{2,1,0:T(8,128)(2,1)S(1)}, bf16[4,128,128]{2,1,0:T(8,128)(2,1)S(1)}, u32[]{:S(2)}, u32[]{:S(2)}) collective-permute-start(bf16[4,128,128]{2,1,0:T(8,128)(2,1)S(1)} %get-tuple-element.38), channel_id=1, source_target_pairs={{0,4},{1,5},{2,6},{3,7},{16,20},{17,21},{18,22},{19,23}} | collective-permute-start | bytes 393224 | tf_op jit(solution)/shard_map/ppermute | solution.py:406
  3.7 13.4 %collective-permute-start.4 = (bf16[448,128]{1,0:T(8,128)(2,1)S(1)}, bf16[448,128]{1,0:T(8,128)(2,1)S(1)}, u32[]{:S(2)}, u32[]{:S(2)}) collective-permute-start(bf16[448,128]{1,0:T(8,128)(2,1)S(1)} %get-tuple-element.46), channel_id=1, source_target_pairs={{0,4},{4,8},{1,5},{5,9},{2,6},{6,10},{3,7},{7,11},{16,20},{20,24},... | collective-permute-start | bytes 344072 | tf_op jit(solution)/shard_map/ppermute | solution.py:383
  5.0 9.5 %collective-permute-start.6 = (bf16[576,128]{1,0:T(8,128)(2,1)S(1)}, bf16[576,128]{1,0:T(8,128)(2,1)S(1)}, u32[]{:S(2)}, u32[]{:S(2)}) collective-permute-start(bf16[576,128]{1,0:T(8,128)(2,1)S(1)} %get-tuple-element.47), channel_id=1, source_target_pairs={{0,4},{4,8},{1,5},{5,9},{2,6},{6,10},{3,7},{7,11},{16,20},{20,24},... | collective-permute-start | bytes 442376 | tf_op jit(solution)/shard_map/ppermute | solution.py:384
  6.3 9.5 %collective-permute-start = (bf16[4,128,128]{2,1,0:T(8,128)(2,1)S(1)}, bf16[4,128,128]{2,1,0:T(8,128)(2,1)S(1)}, u32[]{:S(2)}, u32[]{:S(2)}) collective-permute-start(bf16[4,128,128]{2,1,0:T(8,128)(2,1)S(1)} %get-tuple-element.35), channel_id=1, source_target_pairs={{0,4},{1,5},{2,6},{3,7},{16,20},{17,21},{18,22},{19,23}} | collective-permute-start | bytes 393224 | tf_op jit(solution)/shard_map/ppermute | solution.py:406
  7.0 15.5 %collective-permute-start.3 = (bf16[4,128,128]{2,1,0:T(8,128)(2,1)S(1)}, bf16[4,128,128]{2,1,0:T(8,128)(2,1)S(1)}, u32[]{:S(2)}, u32[]{:S(2)}) collective-permute-start(bf16[4,128,128]{2,1,0:T(8,128)(2,1)S(1)} %add_convert_fusion), channel_id=1, source_target_pairs={{4,8},{5,9},{6,10},{7,11},{20,24},{21,25},{22,26},{23,27}} | collective-permute-start | bytes 393224 | tf_op jit(solution)/shard_map/ppermute | solution.py:406
  14.4 12.3 %collective-permute-start.7 = (bf16[576,128]{1,0:T(8,128)(2,1)S(1)}, bf16[576,128]{1,0:T(8,128)(2,1)S(1)}, u32[]{:S(2)}, u32[]{:S(2)}) collective-permute-start(bf16[576,128]{1,0:T(8,128)(2,1)S(1)} %collective-permute-done.6.b_ref), channel_id=1, source_target_pairs={{4,8},{5,9},{6,10},{7,11},{20,24},{21,25},{22,26},{23,27}} | collective-permute-start | bytes 442376 | tf_op jit(solution)/shard_map/ppermute | solution.py:384
  15.8 9.4 %collective-permute-start.1 = (bf16[4,128,128]{2,1,0:T(8,128)(2,1)S(1)}, bf16[4,128,128]{2,1,0:T(8,128)(2,1)S(1)}, u32[]{:S(2)}, u32[]{:S(2)}) collective-permute-start(bf16[4,128,128]{2,1,0:T(8,128)(2,1)S(1)} %add_convert_fusion.1), channel_id=1, source_target_pairs={{4,8},{5,9},{6,10},{7,11},{20,24},{21,25},{22,26},{23,27}} | collective-permute-start | bytes 393224 | tf_op jit(solution)/shard_map/ppermute | solution.py:406
  17.1 9.6 %collective-permute-start.5 = (bf16[448,128]{1,0:T(8,128)(2,1)S(1)}, bf16[448,128]{1,0:T(8,128)(2,1)S(1)}, u32[]{:S(2)}, u32[]{:S(2)}) collective-permute-start(bf16[448,128]{1,0:T(8,128)(2,1)S(1)} %collective-permute-done.4.a_ref), channel_id=1, source_target_pairs={{4,8},{5,9},{6,10},{7,11},{20,24},{21,25},{22,26},{23,27}} | collective-permute-start | bytes 344072 | tf_op jit(solution)/shard_map/ppermute | solution.py:383

commit v7 on v6

--- a/solution.py
+++ b/solution.py
@@ -17,7 +17,7 @@
 SMEM = pl.BlockSpec(memory_space=pltpu.SMEM)
 HBM = pl.BlockSpec(memory_space=pltpu.HBM)
 DMA = pltpu.SemaphoreType.DMA
-SHARE = 7
+SHARE = 13
 CUTS = (0, 4, 8)
 HALVES = len(CUTS) - 1
 
@@ -174,10 +174,10 @@
             intra_ref[h, low:high] = dot((scores * fade).astype(BF16), value[:high])
 
 
-def put_out(wide, narrow, out_hbm, sem, part, parts):
+def put_out(wide, narrow, out_hbm, sem, part, parts, pick=lambda x, here: x):
     rows = wide.shape[0] // parts
     here = pl.ds(part * rows, rows)
-    narrow[here] = wide[here].astype(BF16)
+    narrow[here] = pick(wide[here], here).astype(BF16)
     copy = pltpu.make_async_copy(narrow.at[here], out_hbm.at[here], sem.at[part])
     copy.start()
     return copy
@@ -196,6 +196,13 @@
     first, count = group_of(half, heads)
     last = half == HALVES - 1
     wide = rest[-3] if last else rest[-1]
+
+    def pick(rows, here):
+        if not half:
+            return rows
+        head = lax.broadcasted_iota(jnp.int32, rows.shape, 0) % heads
+        return jnp.where(head < first, rest[0][here], rows)
+
     ones = jnp.full((dim, dim), 1.0, BF16)
     size = tok // PARTS
     copies = []
@@ -210,7 +217,9 @@
                 mean + 1e-06
             )
         if last:
-            copies.append(put_out(wide, rest[-2], rest[-4], rest[-1], part, PARTS))
+            copies.append(put_out(wide, rest[-2], rest[-4], rest[-1], part, PARTS, pick))
+    if not last and half:
+        wide[...] = pick(wide[...], slice(None))
     for copy in copies:
         copy.wait()
 
@@ -330,7 +339,7 @@
 
     fetched = (q_lin, q_soft, k_soft, v_soft)
     total = 2 * k_soft.shape[0]
-    early = total * SHARE // 16
+    early = total * SHARE // 32
     part_a, part_b = call(
         functools.partial(pack_body, ranks),
         (shaped((early, dim), BF16), shaped((total - early, dim), BF16)),
@@ -417,15 +426,14 @@
         last = half == HALVES - 1
         result = call(
             functools.partial(finish_body, half),
-            ((shaped(q_lin.shape, BF16),) if last else ()) + (shaped(q_lin.shape, F32),),
+            (shaped(q_lin.shape, BF16 if last else F32),),
             tuple(
                 (x, VMEM)
                 for x in (intra, lin_query, lift, befores[half], arrived[half]) + result
             ),
-            (flat_lin, DMA((PARTS,))) if last else (),
+            (wide_lin, flat_lin, DMA((PARTS,))) if last else (),
             flops=2 * counts[half] * tok * dim * dim,
-            out_spec=(HBM, VMEM) if last else VMEM,
-            aliases={5: int(last)} if half else {},
+            out_spec=HBM if last else VMEM,
         )
     lin_out = result[0]
     return (lin_out.reshape(tok, heads, dim), soft_out)

time: 29 us -> 28.9 us (level)
  the two profiles are of different devices: /device:TPU:22 before, /device:TPU:16 now
where the time goes in v7:
time: 28.9 us; the launch traced here: 28.6 us
  Pallas kernels  10.1 us (35%)
  starting transfers between devices  9.08 us (31%)
  waiting for transfers between devices  8.49 us (29%)
  between operations  0.79 us (3%)
    pallas_call x9, Pallas kernels, call(): pl.pallas_call(body, out_shape=tuple(outs), in_specs=[spec for _, spec in...  10.1 us
    ppermute x2, waiting for transfers between devices, on_device(): part_b = lax.ppermute(part_b, 'ctx', pairs)  6.11 us
    ppermute x4, starting transfers between devices, on_device(): arrived[half] = lax.ppermute(sends[half], 'ctx', [(step - 1, step)])  3.92 us
    ppermute x2, starting transfers between devices, on_device(): part_a = lax.ppermute(part_a, 'ctx', pairs)  2.58 us
    ppermute x2, starting transfers between devices, on_device(): part_b = lax.ppermute(part_b, 'ctx', pairs)  2.57 us
    ppermute x4, waiting for transfers between devices, on_device(): arrived[half] = lax.ppermute(sends[half], 'ctx', [(step - 1, step)])  2.34 us
  transfers between devices with their start and end apart: 8, of which 2 were waited for; matrix products, arithmetic and copies ran while one was open for 0% of the time, Pallas kernels for 21%

profile of v7, /device:TPU:16, one launch (start us, length us, event | category | flops | bytes accessed | tf_op | source)
XLA Modules:
  0.0 28.6 jit_solution(18376119631514631086)
XLA Ops:
  0.6 1.9 %shard_map.95 = (bf16[8,256,128]{2,1,0:T(8,128)(2,1)S(1)}, bf16[8,256,128]{2,1,0:T(8,128)(2,1)S(1)}, f32[8,256]{1,0:T(8,128)S(1)}, f32[4,128]{1,0:T(4,128)S(1)},...) custom-call(s32[1]{0:T(128)} %bitcast.me_ref, ...), custom_call_target="tpu_custom_call" | custom-call | bytes 4737052 | tf_op jit(solution)/shard_map/pallas_call | solution.py:31
  2.6 0.4 %shard_map.97 = (f32[4,128,128]{2,1,0:T(8,128)S(1)}, f32[4,128,128]{2,1,0:T(8,128)S(1)}, bf16[4,128,128]{2,1,0:T(8,128)(2,1)S(1)}, bf16[4,128,128]{2,1,0:T(8,128...) custom-call(f32[4,128]{1,0:T(4,128)S(1)} %get-tuple-element.33.flags_ref, ...), custom_call_target="tpu_custom_call" | custom-call | flops 67108864 | bytes 1849344 | tf_op jit(solution)/shard_map/pallas_call | solution.py:31
  2.9 0.7 %collective-permute-start.2 = (bf16[4,128,128]{2,1,0:T(8,128)(2,1)S(1)}, bf16[4,128,128]{2,1,0:T(8,128)(2,1)S(1)}, u32[]{:S(2)}, u32[]{:S(2)}) collective-permute-start(bf16[4,128,128]{2,1,0:T(8,128)(2,1)S(1)} %get-tuple-element.37), channel_id=1, source_target_pairs={{0,4},{1,5},{2,6},{3,7},{16,20},{17,21},{18,22},{19,23}} | collective-permute-start | bytes 393224 | tf_op jit(solution)/shard_map/ppermute | solution.py:415
  3.7 1.3 %collective-permute-start.4 = (bf16[416,128]{1,0:T(8,128)(2,1)S(1)}, bf16[416,128]{1,0:T(8,128)(2,1)S(1)}, u32[]{:S(2)}, u32[]{:S(2)}) collective-permute-start(bf16[416,128]{1,0:T(8,128)(2,1)S(1)} %get-tuple-element.44), channel_id=1, source_target_pairs={{0,4},{4,8},{1,5},{5,9},{2,6},{6,10},{3,7},{7,11},{16,20},{20,24},... | collective-permute-start | bytes 319496 | tf_op jit(solution)/shard_map/ppermute | solution.py:392
  5.0 1.3 %collective-permute-start.6 = (bf16[608,128]{1,0:T(8,128)(2,1)S(1)}, bf16[608,128]{1,0:T(8,128)(2,1)S(1)}, u32[]{:S(2)}, u32[]{:S(2)}) collective-permute-start(bf16[608,128]{1,0:T(8,128)(2,1)S(1)} %get-tuple-element.45), channel_id=1, source_target_pairs={{0,4},{4,8},{1,5},{5,9},{2,6},{6,10},{3,7},{7,11},{16,20},{20,24},... | collective-permute-start | bytes 466952 | tf_op jit(solution)/shard_map/ppermute | solution.py:393
  6.3 0.7 %collective-permute-start = (bf16[4,128,128]{2,1,0:T(8,128)(2,1)S(1)}, bf16[4,128,128]{2,1,0:T(8,128)(2,1)S(1)}, u32[]{:S(2)}, u32[]{:S(2)}) collective-permute-start(bf16[4,128,128]{2,1,0:T(8,128)(2,1)S(1)} %get-tuple-element.34), channel_id=1, source_target_pairs={{0,4},{1,5},{2,6},{3,7},{16,20},{17,21},{18,22},{19,23}} | collective-permute-start | bytes 393224 | tf_op jit(solution)/shard_map/ppermute | solution.py:415
  6.9 0.0 collective-permute-done.2.before_ref
  7.0 1.3 %collective-permute-start.3 = (bf16[4,128,128]{2,1,0:T(8,128)(2,1)S(1)}, bf16[4,128,128]{2,1,0:T(8,128)(2,1)S(1)}, u32[]{:S(2)}, u32[]{:S(2)}) collective-permute-start(bf16[4,128,128]{2,1,0:T(8,128)(2,1)S(1)} %add_convert_fusion), channel_id=1, source_target_pairs={{4,8},{5,9},{6,10},{7,11},{20,24},{21,25},{22,26},{23,27}} | collective-permute-start | bytes 393224 | tf_op jit(solution)/shard_map/ppermute | solution.py:415
  8.3 6.1 %collective-permute-done.6.b_ref = bf16[608,128]{1,0:T(8,128)(2,1)S(1)} collective-permute-done((bf16[608,128]{1,0:T(8,128)(2,1)S(1)}, bf16[608,128]{1,0:T(8,128)(2,1)S(1)}, u32[]{:S(2)}, u32[]{:S(2)}) %collective-permute-start.6) | collective-permute-done | bytes 155680 | tf_op jit(solution)/shard_map/ppermute | solution.py:393
  14.4 1.3 %collective-permute-start.7 = (bf16[608,128]{1,0:T(8,128)(2,1)S(1)}, bf16[608,128]{1,0:T(8,128)(2,1)S(1)}, u32[]{:S(2)}, u32[]{:S(2)}) collective-permute-start(bf16[608,128]{1,0:T(8,128)(2,1)S(1)} %collective-permute-done.6.b_ref), channel_id=1, source_target_pairs={{4,8},{5,9},{6,10},{7,11},{20,24},{21,25},{22,26},{23,27}} | collective-permute-start | bytes 466952 | tf_op jit(solution)/shard_map/ppermute | solution.py:393
  15.7 0.0 collective-permute-done.before_ref
  15.8 1.3 %collective-permute-start.1 = (bf16[4,128,128]{2,1,0:T(8,128)(2,1)S(1)}, bf16[4,128,128]{2,1,0:T(8,128)(2,1)S(1)}, u32[]{:S(2)}, u32[]{:S(2)}) collective-permute-start(bf16[4,128,128]{2,1,0:T(8,128)(2,1)S(1)} %add_convert_fusion.1), channel_id=1, source_target_pairs={{4,8},{5,9},{6,10},{7,11},{20,24},{21,25},{22,26},{23,27}} | collective-permute-start | bytes 393224 | tf_op jit(solution)/shard_map/ppermute | solution.py:415
  17.1 0.0 collective-permute-done.4.a_ref
  17.1 1.3 %collective-permute-start.5 = (bf16[416,128]{1,0:T(8,128)(2,1)S(1)}, bf16[416,128]{1,0:T(8,128)(2,1)S(1)}, u32[]{:S(2)}, u32[]{:S(2)}) collective-permute-start(bf16[416,128]{1,0:T(8,128)(2,1)S(1)} %collective-permute-done.4.a_ref), channel_id=1, source_target_pairs={{4,8},{5,9},{6,10},{7,11},{20,24},{21,25},{22,26},{23,27}} | collective-permute-start | bytes 319496 | tf_op jit(solution)/shard_map/ppermute | solution.py:392
  18.4 1.9 %shard_map.96 = (f32[8,256,128]{2,1,0:T(8,128)S(1)}, bf16[8,256,128]{2,1,0:T(8,128)(2,1)S(1)}, f32[8,256,128]{2,1,0:T(8,128)S(1)}) custom-call(bf16[2048,128]{1,0:T(8,128)(2,1)S(1)} %get-tuple-element.26.q_ref, bf16[8,256,128]{2,1,0:T(8,128)(2,1)S(1)} %get-tuple-element.27.kh_ref, bf16[8,256,128]{2,1,0:T(8,128)(2,1)S(1)} %get-tuple-element.28.vh_ref, ...), custom_call_target="tpu_custom_call" | custom-call | flops 268435456 | bytes 4202496 | tf_op jit(solution)/shard_map/pallas_call | solution.py:31
  20.2 1.2 %shard_map.100 = (bf16[8,256,128]{2,1,0:T(8,128)(2,1)S(1)}, f32[8,256,128]{2,1,0:T(8,128)S(1)}, f32[8,256,256]{2,1,0:T(8,128)S(1)}) custom-call(bf16[2048,128]{1,0:T(8,128)(2,1)S(1)} %get-tuple-element.40.q_ref, bf16[512,128]{1,0:T(8,128)(2,1)S(1)} %get-tuple-element.41.k_ref, bf16[512,128]{1,0:T(8,128)(2,1)S(1)} %get-tuple-element.42.v_ref), custom_call_target="tpu_custom_call" | custom-call | flops 402653184 | bytes 4456448 | tf_op jit(solution)/shard_map/pallas_call | solution.py:31
  21.4 1.1 %shard_map.102 = (f32[8,256,128]{2,1,0:T(8,128)S(1)}, f32[8,256,256]{2,1,0:T(8,128)S(1)}) custom-call(s32[1]{0:T(128)} %bitcast.me_ref, f32[4,128]{1,0:T(4,128)S(1)} %get-tuple-element.33.flags_ref, bf16[8,256,128]{2,1,0:T(8,128)(2,1)S(1)} %get-tuple-element.43.qh_ref, bf16[416,128]{1,0:T(8,128)(2,1)S(1)} %collective-permute-done.4.a_ref, ...), custom_call_target="tpu_custom_call" | custom-call | flops 402653184 | bytes 7079940 | tf_op jit(solution)/shard_map/pallas_call | solution.py:31
  22.5 0.0 collective-permute-done.3.arrived_ref
  22.5 0.4 %shard_map.98.rest_0_ = f32[2048,128]{1,0:T(8,128)S(1)} custom-call(f32[8,256,128]{2,1,0:T(8,128)S(1)} %get-tuple-element.30.intra_ref, bf16[8,256,128]{2,1,0:T(8,128)(2,1)S(1)} %get-tuple-element.31.qh_ref, f32[8,256,128]{2,1,0:T(8,128)S(1)} %get-tuple-element.32.lift_ref, bf16[4,128,128]{2,1,0:T(8,128)(2,1)S(1)} %collective-permute-done.2.before_ref, ...), custom_call_target="tpu_custom_call" | custom-call | flops 33554432 | bytes 3932160 | tf_op jit(solution)/shard_map/pallas_call | solution.py:31
  22.9 2.3 %collective-permute-done.1.arrived_ref = bf16[4,128,128]{2,1,0:T(8,128)(2,1)S(1)} collective-permute-done((bf16[4,128,128]{2,1,0:T(8,128)(2,1)S(1)}, bf16[4,128,128]{2,1,0:T(8,128)(2,1)S(1)}, u32[]{:S(2)}, u32[]{:S(2)}) %collective-permute-start.1) | collective-permute-done | bytes 131104 | tf_op jit(solution)/shard_map/ppermute | solution.py:415
  25.3 1.3 %shard_map.99 = bf16[2048,128]{1,0:T(8,128)(2,1)} custom-call(f32[8,256,128]{2,1,0:T(8,128)S(1)} %get-tuple-element.30.intra_ref, bf16[8,256,128]{2,1,0:T(8,128)(2,1)S(1)} %get-tuple-element.31.qh_ref, f32[8,256,128]{2,1,0:T(8,128)S(1)} %get-tuple-element.32.lift_ref, bf16[4,128,128]{2,1,0:T(8,128)(2,1)S(1)} %collective-permute-done.before_ref, ...), custom_call_target="tpu_custom_call" | custom-call | flops 33554432 | bytes 4456448 | tf_op jit(solution)/shard_map/pallas_call | solution.py:31
  26.6 0.0 collective-permute-done.5.a_ref
  26.6 0.0 collective-permute-done.7.b_ref
  26.6 2.0 %shard_map.103 = bf16[2048,128]{1,0:T(8,128)(2,1)} custom-call(s32[1]{0:T(128)} %bitcast.me_ref, f32[4,128]{1,0:T(4,128)S(1)} %get-tuple-element.33.flags_ref, bf16[8,256,128]{2,1,0:T(8,128)(2,1)S(1)} %get-tuple-element.43.qh_ref, bf16[416,128]{1,0:T(8,128)(2,1)S(1)} %collective-permute-done.5.a_ref, bf16[608,128]{1,0:T(8,128)(2,1)S(1)} %collective-permute-done.7.b_ref, ...), custom_call_target="tpu_custom_call" | custom-call | flops 402653184 | bytes 4458500 | tf_op jit(solution)/shard_map/pallas_call | solution.py:31
  (3 shorter events, 0.1 us)
Async XLA Ops:
  2.9 4.0 %collective-permute-start.2 = (bf16[4,128,128]{2,1,0:T(8,128)(2,1)S(1)}, bf16[4,128,128]{2,1,0:T(8,128)(2,1)S(1)}, u32[]{:S(2)}, u32[]{:S(2)}) collective-permute-start(bf16[4,128,128]{2,1,0:T(8,128)(2,1)S(1)} %get-tuple-element.37), channel_id=1, source_target_pairs={{0,4},{1,5},{2,6},{3,7},{16,20},{17,21},{18,22},{19,23}} | collective-permute-start | bytes 393224 | tf_op jit(solution)/shard_map/ppermute | solution.py:415
  3.7 13.4 %collective-permute-start.4 = (bf16[416,128]{1,0:T(8,128)(2,1)S(1)}, bf16[416,128]{1,0:T(8,128)(2,1)S(1)}, u32[]{:S(2)}, u32[]{:S(2)}) collective-permute-start(bf16[416,128]{1,0:T(8,128)(2,1)S(1)} %get-tuple-element.44), channel_id=1, source_target_pairs={{0,4},{4,8},{1,5},{5,9},{2,6},{6,10},{3,7},{7,11},{16,20},{20,24},... | collective-permute-start | bytes 319496 | tf_op jit(solution)/shard_map/ppermute | solution.py:392
  5.0 9.4 %collective-permute-start.6 = (bf16[608,128]{1,0:T(8,128)(2,1)S(1)}, bf16[608,128]{1,0:T(8,128)(2,1)S(1)}, u32[]{:S(2)}, u32[]{:S(2)}) collective-permute-start(bf16[608,128]{1,0:T(8,128)(2,1)S(1)} %get-tuple-element.45), channel_id=1, source_target_pairs={{0,4},{4,8},{1,5},{5,9},{2,6},{6,10},{3,7},{7,11},{16,20},{20,24},... | collective-permute-start | bytes 466952 | tf_op jit(solution)/shard_map/ppermute | solution.py:393
  6.3 9.4 %collective-permute-start = (bf16[4,128,128]{2,1,0:T(8,128)(2,1)S(1)}, bf16[4,128,128]{2,1,0:T(8,128)(2,1)S(1)}, u32[]{:S(2)}, u32[]{:S(2)}) collective-permute-start(bf16[4,128,128]{2,1,0:T(8,128)(2,1)S(1)} %get-tuple-element.34), channel_id=1, source_target_pairs={{0,4},{1,5},{2,6},{3,7},{16,20},{17,21},{18,22},{19,23}} | collective-permute-start | bytes 393224 | tf_op jit(solution)/shard_map/ppermute | solution.py:415
  7.0 15.5 %collective-permute-start.3 = (bf16[4,128,128]{2,1,0:T(8,128)(2,1)S(1)}, bf16[4,128,128]{2,1,0:T(8,128)(2,1)S(1)}, u32[]{:S(2)}, u32[]{:S(2)}) collective-permute-start(bf16[4,128,128]{2,1,0:T(8,128)(2,1)S(1)} %add_convert_fusion), channel_id=1, source_target_pairs={{4,8},{5,9},{6,10},{7,11},{20,24},{21,25},{22,26},{23,27}} | collective-permute-start | bytes 393224 | tf_op jit(solution)/shard_map/ppermute | solution.py:415
  14.4 12.2 %collective-permute-start.7 = (bf16[608,128]{1,0:T(8,128)(2,1)S(1)}, bf16[608,128]{1,0:T(8,128)(2,1)S(1)}, u32[]{:S(2)}, u32[]{:S(2)}) collective-permute-start(bf16[608,128]{1,0:T(8,128)(2,1)S(1)} %collective-permute-done.6.b_ref), channel_id=1, source_target_pairs={{4,8},{5,9},{6,10},{7,11},{20,24},{21,25},{22,26},{23,27}} | collective-permute-start | bytes 466952 | tf_op jit(solution)/shard_map/ppermute | solution.py:393
  15.8 9.5 %collective-permute-start.1 = (bf16[4,128,128]{2,1,0:T(8,128)(2,1)S(1)}, bf16[4,128,128]{2,1,0:T(8,128)(2,1)S(1)}, u32[]{:S(2)}, u32[]{:S(2)}) collective-permute-start(bf16[4,128,128]{2,1,0:T(8,128)(2,1)S(1)} %add_convert_fusion.1), channel_id=1, source_target_pairs={{4,8},{5,9},{6,10},{7,11},{20,24},{21,25},{22,26},{23,27}} | collective-permute-start | bytes 393224 | tf_op jit(solution)/shard_map/ppermute | solution.py:415
  17.1 9.5 %collective-permute-start.5 = (bf16[416,128]{1,0:T(8,128)(2,1)S(1)}, bf16[416,128]{1,0:T(8,128)(2,1)S(1)}, u32[]{:S(2)}, u32[]{:S(2)}) collective-permute-start(bf16[416,128]{1,0:T(8,128)(2,1)S(1)} %collective-permute-done.4.a_ref), channel_id=1, source_target_pairs={{4,8},{5,9},{6,10},{7,11},{20,24},{21,25},{22,26},{23,27}} | collective-permute-start | bytes 319496 | tf_op jit(solution)/shard_map/ppermute | solution.py:392

commit v8 on v7

--- a/solution.py
+++ b/solution.py
@@ -204,19 +204,15 @@
         return jnp.where(head < first, rest[0][here], rows)
 
     ones = jnp.full((dim, dim), 1.0, BF16)
-    size = tok // PARTS
+    for i in range(count):
+        h = first + i
+        inter = dot(qh_ref[h], before_ref[i] + arrived_ref[i])
+        total = intra_ref[h] + lift_ref[h] * inter
+        mean = dot((total * total).astype(BF16), ones) * (1.0 / dim)
+        wide[pl.ds(h, tok, stride=heads), :] = total * lax.rsqrt(mean + 1e-06)
     copies = []
-    for part in range(PARTS):
-        rows = pl.ds(part * size, size)
-        for i in range(count):
-            h = first + i
-            inter = dot(qh_ref[h, rows], before_ref[i] + arrived_ref[i])
-            total = intra_ref[h, rows] + lift_ref[h, rows] * inter
-            mean = dot((total * total).astype(BF16), ones) * (1.0 / dim)
-            wide[pl.ds(part * size * heads + h, size, stride=heads), :] = total * lax.rsqrt(
-                mean + 1e-06
-            )
-        if last:
+    if last:
+        for part in range(PARTS):
             copies.append(put_out(wide, rest[-2], rest[-4], rest[-1], part, PARTS, pick))
     if not last and half:
         wide[...] = pick(wide[...], slice(None))

time: 28.9 us -> 28.9 us (level)
  the two profiles are of different devices: /device:TPU:16 before, /device:TPU:22 now
where the time goes in v8:
time: 28.9 us; the launch traced here: 28.6 us
  Pallas kernels  10.2 us (35%)
  starting transfers between devices  9.08 us (31%)
  waiting for transfers between devices  8.47 us (29%)
  between operations  0.8 us (3%)
    pallas_call x9, Pallas kernels, call(): pl.pallas_call(body, out_shape=tuple(outs), in_specs=[spec for _, spec in...  10.2 us
    ppermute x2, waiting for transfers between devices, on_device(): part_b = lax.ppermute(part_b, 'ctx', pairs)  6.11 us
    ppermute x4, starting transfers between devices, on_device(): arrived[half] = lax.ppermute(sends[half], 'ctx', [(step - 1, step)])  3.92 us
    ppermute x2, starting transfers between devices, on_device(): part_a = lax.ppermute(part_a, 'ctx', pairs)  2.58 us
    ppermute x2, starting transfers between devices, on_device(): part_b = lax.ppermute(part_b, 'ctx', pairs)  2.57 us
    ppermute x4, waiting for transfers between devices, on_device(): arrived[half] = lax.ppermute(sends[half], 'ctx', [(step - 1, step)])  2.34 us
  transfers between devices with their start and end apart: 8, of which 2 were waited for; matrix products, arithmetic and copies ran while one was open for 0% of the time, Pallas kernels for 21%

profile of v8, /device:TPU:22, one launch (start us, length us, event | category | flops | bytes accessed | tf_op | source)
XLA Modules:
  0.0 28.6 jit_solution(17301149987079723994)
XLA Ops:
  0.6 1.9 %shard_map.95 = (bf16[8,256,128]{2,1,0:T(8,128)(2,1)S(1)}, bf16[8,256,128]{2,1,0:T(8,128)(2,1)S(1)}, f32[8,256]{1,0:T(8,128)S(1)}, f32[4,128]{1,0:T(4,128)S(1)},...) custom-call(s32[1]{0:T(128)} %bitcast.me_ref, ...), custom_call_target="tpu_custom_call" | custom-call | bytes 4737052 | tf_op jit(solution)/shard_map/pallas_call | solution.py:31
  2.6 0.4 %shard_map.97 = (f32[4,128,128]{2,1,0:T(8,128)S(1)}, f32[4,128,128]{2,1,0:T(8,128)S(1)}, bf16[4,128,128]{2,1,0:T(8,128)(2,1)S(1)}, bf16[4,128,128]{2,1,0:T(8,128...) custom-call(f32[4,128]{1,0:T(4,128)S(1)} %get-tuple-element.33.flags_ref, ...), custom_call_target="tpu_custom_call" | custom-call | flops 67108864 | bytes 1849344 | tf_op jit(solution)/shard_map/pallas_call | solution.py:31
  2.9 0.7 %collective-permute-start.2 = (bf16[4,128,128]{2,1,0:T(8,128)(2,1)S(1)}, bf16[4,128,128]{2,1,0:T(8,128)(2,1)S(1)}, u32[]{:S(2)}, u32[]{:S(2)}) collective-permute-start(bf16[4,128,128]{2,1,0:T(8,128)(2,1)S(1)} %get-tuple-element.37), channel_id=1, source_target_pairs={{0,4},{1,5},{2,6},{3,7},{16,20},{17,21},{18,22},{19,23}} | collective-permute-start | bytes 393224 | tf_op jit(solution)/shard_map/ppermute | solution.py:411
  3.7 1.3 %collective-permute-start.4 = (bf16[416,128]{1,0:T(8,128)(2,1)S(1)}, bf16[416,128]{1,0:T(8,128)(2,1)S(1)}, u32[]{:S(2)}, u32[]{:S(2)}) collective-permute-start(bf16[416,128]{1,0:T(8,128)(2,1)S(1)} %get-tuple-element.44), channel_id=1, source_target_pairs={{0,4},{4,8},{1,5},{5,9},{2,6},{6,10},{3,7},{7,11},{16,20},{20,24},... | collective-permute-start | bytes 319496 | tf_op jit(solution)/shard_map/ppermute | solution.py:388
  5.0 1.3 %collective-permute-start.6 = (bf16[608,128]{1,0:T(8,128)(2,1)S(1)}, bf16[608,128]{1,0:T(8,128)(2,1)S(1)}, u32[]{:S(2)}, u32[]{:S(2)}) collective-permute-start(bf16[608,128]{1,0:T(8,128)(2,1)S(1)} %get-tuple-element.45), channel_id=1, source_target_pairs={{0,4},{4,8},{1,5},{5,9},{2,6},{6,10},{3,7},{7,11},{16,20},{20,24},... | collective-permute-start | bytes 466952 | tf_op jit(solution)/shard_map/ppermute | solution.py:389
  6.3 0.7 %collective-permute-start = (bf16[4,128,128]{2,1,0:T(8,128)(2,1)S(1)}, bf16[4,128,128]{2,1,0:T(8,128)(2,1)S(1)}, u32[]{:S(2)}, u32[]{:S(2)}) collective-permute-start(bf16[4,128,128]{2,1,0:T(8,128)(2,1)S(1)} %get-tuple-element.34), channel_id=1, source_target_pairs={{0,4},{1,5},{2,6},{3,7},{16,20},{17,21},{18,22},{19,23}} | collective-permute-start | bytes 393224 | tf_op jit(solution)/shard_map/ppermute | solution.py:411
  6.9 0.0 collective-permute-done.2.before_ref
  7.0 1.3 %collective-permute-start.3 = (bf16[4,128,128]{2,1,0:T(8,128)(2,1)S(1)}, bf16[4,128,128]{2,1,0:T(8,128)(2,1)S(1)}, u32[]{:S(2)}, u32[]{:S(2)}) collective-permute-start(bf16[4,128,128]{2,1,0:T(8,128)(2,1)S(1)} %add_convert_fusion), channel_id=1, source_target_pairs={{4,8},{5,9},{6,10},{7,11},{20,24},{21,25},{22,26},{23,27}} | collective-permute-start | bytes 393224 | tf_op jit(solution)/shard_map/ppermute | solution.py:411
  8.3 6.1 %collective-permute-done.6.b_ref = bf16[608,128]{1,0:T(8,128)(2,1)S(1)} collective-permute-done((bf16[608,128]{1,0:T(8,128)(2,1)S(1)}, bf16[608,128]{1,0:T(8,128)(2,1)S(1)}, u32[]{:S(2)}, u32[]{:S(2)}) %collective-permute-start.6) | collective-permute-done | bytes 155680 | tf_op jit(solution)/shard_map/ppermute | solution.py:389
  14.4 1.3 %collective-permute-start.7 = (bf16[608,128]{1,0:T(8,128)(2,1)S(1)}, bf16[608,128]{1,0:T(8,128)(2,1)S(1)}, u32[]{:S(2)}, u32[]{:S(2)}) collective-permute-start(bf16[608,128]{1,0:T(8,128)(2,1)S(1)} %collective-permute-done.6.b_ref), channel_id=1, source_target_pairs={{4,8},{5,9},{6,10},{7,11},{20,24},{21,25},{22,26},{23,27}} | collective-permute-start | bytes 466952 | tf_op jit(solution)/shard_map/ppermute | solution.py:389
  15.7 0.0 collective-permute-done.before_ref
  15.8 1.3 %collective-permute-start.1 = (bf16[4,128,128]{2,1,0:T(8,128)(2,1)S(1)}, bf16[4,128,128]{2,1,0:T(8,128)(2,1)S(1)}, u32[]{:S(2)}, u32[]{:S(2)}) collective-permute-start(bf16[4,128,128]{2,1,0:T(8,128)(2,1)S(1)} %add_convert_fusion.1), channel_id=1, source_target_pairs={{4,8},{5,9},{6,10},{7,11},{20,24},{21,25},{22,26},{23,27}} | collective-permute-start | bytes 393224 | tf_op jit(solution)/shard_map/ppermute | solution.py:411
  17.1 0.0 collective-permute-done.4.a_ref
  17.1 1.3 %collective-permute-start.5 = (bf16[416,128]{1,0:T(8,128)(2,1)S(1)}, bf16[416,128]{1,0:T(8,128)(2,1)S(1)}, u32[]{:S(2)}, u32[]{:S(2)}) collective-permute-start(bf16[416,128]{1,0:T(8,128)(2,1)S(1)} %collective-permute-done.4.a_ref), channel_id=1, source_target_pairs={{4,8},{5,9},{6,10},{7,11},{20,24},{21,25},{22,26},{23,27}} | collective-permute-start | bytes 319496 | tf_op jit(solution)/shard_map/ppermute | solution.py:388
  18.4 1.9 %shard_map.96 = (f32[8,256,128]{2,1,0:T(8,128)S(1)}, bf16[8,256,128]{2,1,0:T(8,128)(2,1)S(1)}, f32[8,256,128]{2,1,0:T(8,128)S(1)}) custom-call(bf16[2048,128]{1,0:T(8,128)(2,1)S(1)} %get-tuple-element.26.q_ref, bf16[8,256,128]{2,1,0:T(8,128)(2,1)S(1)} %get-tuple-element.27.kh_ref, bf16[8,256,128]{2,1,0:T(8,128)(2,1)S(1)} %get-tuple-element.28.vh_ref, ...), custom_call_target="tpu_custom_call" | custom-call | flops 268435456 | bytes 4202496 | tf_op jit(solution)/shard_map/pallas_call | solution.py:31
  20.2 1.2 %shard_map.100 = (bf16[8,256,128]{2,1,0:T(8,128)(2,1)S(1)}, f32[8,256,128]{2,1,0:T(8,128)S(1)}, f32[8,256,256]{2,1,0:T(8,128)S(1)}) custom-call(bf16[2048,128]{1,0:T(8,128)(2,1)S(1)} %get-tuple-element.40.q_ref, bf16[512,128]{1,0:T(8,128)(2,1)S(1)} %get-tuple-element.41.k_ref, bf16[512,128]{1,0:T(8,128)(2,1)S(1)} %get-tuple-element.42.v_ref), custom_call_target="tpu_custom_call" | custom-call | flops 402653184 | bytes 4456448 | tf_op jit(solution)/shard_map/pallas_call | solution.py:31
  21.4 1.1 %shard_map.102 = (f32[8,256,128]{2,1,0:T(8,128)S(1)}, f32[8,256,256]{2,1,0:T(8,128)S(1)}) custom-call(s32[1]{0:T(128)} %bitcast.me_ref, f32[4,128]{1,0:T(4,128)S(1)} %get-tuple-element.33.flags_ref, bf16[8,256,128]{2,1,0:T(8,128)(2,1)S(1)} %get-tuple-element.43.qh_ref, bf16[416,128]{1,0:T(8,128)(2,1)S(1)} %collective-permute-done.4.a_ref, ...), custom_call_target="tpu_custom_call" | custom-call | flops 402653184 | bytes 7079940 | tf_op jit(solution)/shard_map/pallas_call | solution.py:31
  22.5 0.0 collective-permute-done.3.arrived_ref
  22.5 0.4 %shard_map.98.rest_0_ = f32[2048,128]{1,0:T(8,128)S(1)} custom-call(f32[8,256,128]{2,1,0:T(8,128)S(1)} %get-tuple-element.30.intra_ref, bf16[8,256,128]{2,1,0:T(8,128)(2,1)S(1)} %get-tuple-element.31.qh_ref, f32[8,256,128]{2,1,0:T(8,128)S(1)} %get-tuple-element.32.lift_ref, bf16[4,128,128]{2,1,0:T(8,128)(2,1)S(1)} %collective-permute-done.2.before_ref, ...), custom_call_target="tpu_custom_call" | custom-call | flops 33554432 | bytes 3932160 | tf_op jit(solution)/shard_map/pallas_call | solution.py:31
  22.9 2.3 %collective-permute-done.1.arrived_ref = bf16[4,128,128]{2,1,0:T(8,128)(2,1)S(1)} collective-permute-done((bf16[4,128,128]{2,1,0:T(8,128)(2,1)S(1)}, bf16[4,128,128]{2,1,0:T(8,128)(2,1)S(1)}, u32[]{:S(2)}, u32[]{:S(2)}) %collective-permute-start.1) | collective-permute-done | bytes 131104 | tf_op jit(solution)/shard_map/ppermute | solution.py:411
  25.3 1.3 %shard_map.99 = bf16[2048,128]{1,0:T(8,128)(2,1)} custom-call(f32[8,256,128]{2,1,0:T(8,128)S(1)} %get-tuple-element.30.intra_ref, bf16[8,256,128]{2,1,0:T(8,128)(2,1)S(1)} %get-tuple-element.31.qh_ref, f32[8,256,128]{2,1,0:T(8,128)S(1)} %get-tuple-element.32.lift_ref, bf16[4,128,128]{2,1,0:T(8,128)(2,1)S(1)} %collective-permute-done.before_ref, ...), custom_call_target="tpu_custom_call" | custom-call | flops 33554432 | bytes 4456448 | tf_op jit(solution)/shard_map/pallas_call | solution.py:31
  26.6 0.0 collective-permute-done.5.a_ref
  26.6 0.0 collective-permute-done.7.b_ref
  26.6 2.0 %shard_map.103 = bf16[2048,128]{1,0:T(8,128)(2,1)} custom-call(s32[1]{0:T(128)} %bitcast.me_ref, f32[4,128]{1,0:T(4,128)S(1)} %get-tuple-element.33.flags_ref, bf16[8,256,128]{2,1,0:T(8,128)(2,1)S(1)} %get-tuple-element.43.qh_ref, bf16[416,128]{1,0:T(8,128)(2,1)S(1)} %collective-permute-done.5.a_ref, bf16[608,128]{1,0:T(8,128)(2,1)S(1)} %collective-permute-done.7.b_ref, ...), custom_call_target="tpu_custom_call" | custom-call | flops 402653184 | bytes 4458500 | tf_op jit(solution)/shard_map/pallas_call | solution.py:31
  (3 shorter events, 0.1 us)
Async XLA Ops:
  2.9 4.0 %collective-permute-start.2 = (bf16[4,128,128]{2,1,0:T(8,128)(2,1)S(1)}, bf16[4,128,128]{2,1,0:T(8,128)(2,1)S(1)}, u32[]{:S(2)}, u32[]{:S(2)}) collective-permute-start(bf16[4,128,128]{2,1,0:T(8,128)(2,1)S(1)} %get-tuple-element.37), channel_id=1, source_target_pairs={{0,4},{1,5},{2,6},{3,7},{16,20},{17,21},{18,22},{19,23}} | collective-permute-start | bytes 393224 | tf_op jit(solution)/shard_map/ppermute | solution.py:411
  3.7 13.4 %collective-permute-start.4 = (bf16[416,128]{1,0:T(8,128)(2,1)S(1)}, bf16[416,128]{1,0:T(8,128)(2,1)S(1)}, u32[]{:S(2)}, u32[]{:S(2)}) collective-permute-start(bf16[416,128]{1,0:T(8,128)(2,1)S(1)} %get-tuple-element.44), channel_id=1, source_target_pairs={{0,4},{4,8},{1,5},{5,9},{2,6},{6,10},{3,7},{7,11},{16,20},{20,24},... | collective-permute-start | bytes 319496 | tf_op jit(solution)/shard_map/ppermute | solution.py:388
  5.0 9.4 %collective-permute-start.6 = (bf16[608,128]{1,0:T(8,128)(2,1)S(1)}, bf16[608,128]{1,0:T(8,128)(2,1)S(1)}, u32[]{:S(2)}, u32[]{:S(2)}) collective-permute-start(bf16[608,128]{1,0:T(8,128)(2,1)S(1)} %get-tuple-element.45), channel_id=1, source_target_pairs={{0,4},{4,8},{1,5},{5,9},{2,6},{6,10},{3,7},{7,11},{16,20},{20,24},... | collective-permute-start | bytes 466952 | tf_op jit(solution)/shard_map/ppermute | solution.py:389
  6.3 9.4 %collective-permute-start = (bf16[4,128,128]{2,1,0:T(8,128)(2,1)S(1)}, bf16[4,128,128]{2,1,0:T(8,128)(2,1)S(1)}, u32[]{:S(2)}, u32[]{:S(2)}) collective-permute-start(bf16[4,128,128]{2,1,0:T(8,128)(2,1)S(1)} %get-tuple-element.34), channel_id=1, source_target_pairs={{0,4},{1,5},{2,6},{3,7},{16,20},{17,21},{18,22},{19,23}} | collective-permute-start | bytes 393224 | tf_op jit(solution)/shard_map/ppermute | solution.py:411
  7.0 15.5 %collective-permute-start.3 = (bf16[4,128,128]{2,1,0:T(8,128)(2,1)S(1)}, bf16[4,128,128]{2,1,0:T(8,128)(2,1)S(1)}, u32[]{:S(2)}, u32[]{:S(2)}) collective-permute-start(bf16[4,128,128]{2,1,0:T(8,128)(2,1)S(1)} %add_convert_fusion), channel_id=1, source_target_pairs={{4,8},{5,9},{6,10},{7,11},{20,24},{21,25},{22,26},{23,27}} | collective-permute-start | bytes 393224 | tf_op jit(solution)/shard_map/ppermute | solution.py:411
  14.4 12.2 %collective-permute-start.7 = (bf16[608,128]{1,0:T(8,128)(2,1)S(1)}, bf16[608,128]{1,0:T(8,128)(2,1)S(1)}, u32[]{:S(2)}, u32[]{:S(2)}) collective-permute-start(bf16[608,128]{1,0:T(8,128)(2,1)S(1)} %collective-permute-done.6.b_ref), channel_id=1, source_target_pairs={{4,8},{5,9},{6,10},{7,11},{20,24},{21,25},{22,26},{23,27}} | collective-permute-start | bytes 466952 | tf_op jit(solution)/shard_map/ppermute | solution.py:389
  15.8 9.5 %collective-permute-start.1 = (bf16[4,128,128]{2,1,0:T(8,128)(2,1)S(1)}, bf16[4,128,128]{2,1,0:T(8,128)(2,1)S(1)}, u32[]{:S(2)}, u32[]{:S(2)}) collective-permute-start(bf16[4,128,128]{2,1,0:T(8,128)(2,1)S(1)} %add_convert_fusion.1), channel_id=1, source_target_pairs={{4,8},{5,9},{6,10},{7,11},{20,24},{21,25},{22,26},{23,27}} | collective-permute-start | bytes 393224 | tf_op jit(solution)/shard_map/ppermute | solution.py:411
  17.1 9.5 %collective-permute-start.5 = (bf16[416,128]{1,0:T(8,128)(2,1)S(1)}, bf16[416,128]{1,0:T(8,128)(2,1)S(1)}, u32[]{:S(2)}, u32[]{:S(2)}) collective-permute-start(bf16[416,128]{1,0:T(8,128)(2,1)S(1)} %collective-permute-done.4.a_ref), channel_id=1, source_target_pairs={{4,8},{5,9},{6,10},{7,11},{20,24},{21,25},{22,26},{23,27}} | collective-permute-start | bytes 319496 | tf_op jit(solution)/shard_map/ppermute | solution.py:388
